TPU v7x, 128 devices: a whole 4x4x4 slice. The times are simulated.
128 devices in a mesh: ga: 8 (over y_hi, z), ka: 16 (over y_lo, x, core).
Axes of the slice: x: 4, y: 4 (y_hi: 2, y_lo: 2; y = y_hi * 2 + y_lo), z: 4, core: 2. Of those that a mesh axis runs over, the one named last changes fastest.
Arguments:
- amplitudes: float32 [14400, 2048], P(None, ('ka', 'ga')), may hold values from -6 to 6
- integrals: float32 [2048, 15360], P('ga', 'ka'), may hold values from -0.125 to 0.125
Outputs:
- residual: float32 [14400, 15360], P('ga', 'ka')
All inputs are finite; a program needn't handle non-finite values.
Results may differ from a plain program's by a relative error of at most 0.00007.
Values sent between devices are 32-bit elements; how exact they have to be, the bound alone decides.
A program may use at most 128 MiB of HBM per device.

v0:
```python
import jax
import jax.numpy as jnp
from jax import lax
from jax.sharding import PartitionSpec as P


def per_device(amplitudes, integrals):
    regrouped = lax.all_to_all(amplitudes, "ga", split_axis=0, concat_axis=1, tiled=True)
    full_rows = lax.all_gather(regrouped, "ka", axis=1, tiled=True)
    ladder = jnp.dot(
        full_rows,
        lax.all_gather(integrals, "ga", axis=0, tiled=True),
        precision=lax.Precision.HIGHEST,
        preferred_element_type=jnp.float32,
    )
    return 0.5 * ladder


def solution(mesh):
    placed = (P(None, ("ka", "ga")), P("ga", "ka"))
    return jax.shard_map(
        per_device, mesh=mesh, in_specs=placed, out_specs=P("ga", "ka"), check_vma=False
    )
```

profile of v0, /device:TPU:1, one launch (start us, length us, event | category | flops | bytes accessed | tf_op | source)
XLA Modules:
  0.0 324.6 jit_solution(7381460113975320111)
XLA Ops:
  6.5 0.0 all-gather.5.cloned.1.call-start
  6.5 0.7 all-gather.5.cloned.1.call-update
  7.3 0.0 all-gather.3.cloned.1.call-start
  7.3 1.8 all_to_all.14
  9.1 0.2 copy.3
  9.3 26.1 %all_to_all.19 = f32[8,1800,16]{1,2,0:T(8,128)} all-to-all(f32[8,1800,16]{1,2,0:T(8,128)S(1)} %copy.3), channel_id=1, replica_groups=mesh['ga'=8,'ka'=16] {'ga'}, dimensions={0} | all-to-all | bytes 1843200 | tf_op jit(solution)/shard_map/all_to_all | solution.py:8
  35.4 0.0 all-gather.3.cloned.1.call-update
  35.4 90.2 %all-gather.5.cloned.1.call-done = f32[2048,960]{0,1:T(8,128)} async-done(((f32[256,960]{0,1:T(8,128)}), f32[2048,960]{0,1:T(8,128)}) %all-gather.5.cloned.1.call-update) | async-done | bytes 7864336 | tf_op jit(solution)/shard_map/all_gather | solution.py:12
  125.6 87.0 %all-gather.3.cloned.1.call-done = f32[1800,2048]{0,1:T(8,128)} async-done(((f32[1800,128]{0,1:T(8,128)}), f32[1800,2048]{0,1:T(8,128)}) %all-gather.3.cloned.1.call-update) | async-done | bytes 14745616 | tf_op jit(solution)/shard_map/all_gather | solution.py:9
  212.6 105.2 %convolution_multiply_fusion = f32[1800,960]{1,0:T(8,128)} fusion(f32[1800,2048]{0,1:T(8,128)} %all-gather.3.cloned.1.call-done, f32[2048,960]{0,1:T(8,128)} %all-gather.5.cloned.1.call-done), kind=kOutput, calls=%fused_computation | convolution fusion | flops 42469056512 | bytes 29521920 | tf_op jit(solution)/shard_map/dot_general | solution.py:10
Async XLA Ops:
  6.5 119.1 %all-gather.5.cloned.1.call-start = ((), (), s32[]{:S(2)}) async-start(), calls=%async_computation.2 | async-start | bytes 8847360 | tf_op jit(solution)/shard_map/all_gather | solution.py:12
  7.3 205.3 %all-gather.3.cloned.1.call-start = ((), (), s32[]{:S(2)}) async-start(), calls=%async_computation.1 | async-start | bytes 16711680 | tf_op jit(solution)/shard_map/all_gather | solution.py:9
Sparse Core Ops, SparseCore 0:
  9.5 116.0 all-gather.4
  127.3 85.2 all-gather.2
where the time goes:
time: 325 us
  waiting for transfers between devices  178 us (55%)
  matrix products  105 us (32%)
  blocking collectives  26.1 us (8%)
  between operations  13.4 us (4%)
    dot_general x1, matrix products, per_device(): jnp.dot(full_rows, lax.all_gather(integrals, 'ga', axis=0, tiled=True), p...  105 us
    all_gather x1, waiting for transfers between devices, per_device(): lax.all_gather(integrals, 'ga', axis=0, tiled=True)  90.2 us
    all_gather x1, waiting for transfers between devices, per_device(): full_rows = lax.all_gather(regrouped, 'ka', axis=1, tiled=True)  87 us
    all_to_all x1, blocking collectives, per_device(): lax.all_to_all(amplitudes, 'ga', split_axis=0, concat_axis=1, tiled=True)  26.1 us
  transfers between devices with their start and end apart: 2, of which 2 were waited for; matrix products, arithmetic and copies ran while one was open for 0% of the time, Pallas kernels for 0%

commit v1 on v0

--- a/solution.py
+++ b/solution.py
@@ -10,7 +10,7 @@
     ladder = jnp.dot(
         full_rows,
         lax.all_gather(integrals, "ga", axis=0, tiled=True),
-        precision=lax.Precision.HIGHEST,
+        precision=lax.Precision.HIGH,
         preferred_element_type=jnp.float32,
     )
     return 0.5 * ladder

time: 325 us -> 276 us (0.85)
  matrix products: 105 us -> 56.3 us
    dot_general x1, matrix products: 105 us -> 56.3 us  [per_device(): jnp.dot(full_rows, lax.all_gather(integrals, 'ga', axis=0, tiled=True), p...]
where the time goes in v1:
time: 276 us
  waiting for transfers between devices  178 us (64%)
  matrix products  56.3 us (20%)
  blocking collectives  26.1 us (9%)
  between operations  13.4 us (5%)
    all_gather x1, waiting for transfers between devices, per_device(): lax.all_gather(integrals, 'ga', axis=0, tiled=True)  90.2 us
    all_gather x1, waiting for transfers between devices, per_device(): full_rows = lax.all_gather(regrouped, 'ka', axis=1, tiled=True)  87 us
    dot_general x1, matrix products, per_device(): jnp.dot(full_rows, lax.all_gather(integrals, 'ga', axis=0, tiled=True), p...  56.3 us
    all_to_all x1, blocking collectives, per_device(): lax.all_to_all(amplitudes, 'ga', split_axis=0, concat_axis=1, tiled=True)  26.1 us
  transfers between devices with their start and end apart: 2, of which 2 were waited for; matrix products, arithmetic and copies ran while one was open for 0% of the time, Pallas kernels for 0%

profile of v1, /device:TPU:1, one launch (start us, length us, event | category | flops | bytes accessed | tf_op | source)
XLA Modules:
  0.0 275.7 jit_solution(6729287836098242063)
XLA Ops:
  6.5 0.0 all-gather.5.cloned.1.call-start
  6.5 0.7 all-gather.5.cloned.1.call-update
  7.3 0.0 all-gather.3.cloned.1.call-start
  7.3 1.8 all_to_all.14
  9.1 0.2 copy.3
  9.3 26.1 %all_to_all.19 = f32[8,1800,16]{1,2,0:T(8,128)} all-to-all(f32[8,1800,16]{1,2,0:T(8,128)S(1)} %copy.3), channel_id=1, replica_groups=mesh['ga'=8,'ka'=16] {'ga'}, dimensions={0} | all-to-all | bytes 1843200 | tf_op jit(solution)/shard_map/all_to_all | solution.py:8
  35.4 0.0 all-gather.3.cloned.1.call-update
  35.4 90.2 %all-gather.5.cloned.1.call-done = f32[2048,960]{0,1:T(8,128)} async-done(((f32[256,960]{0,1:T(8,128)}), f32[2048,960]{0,1:T(8,128)}) %all-gather.5.cloned.1.call-update) | async-done | bytes 7864336 | tf_op jit(solution)/shard_map/all_gather | solution.py:12
  125.6 87.0 %all-gather.3.cloned.1.call-done = f32[1800,2048]{0,1:T(8,128)} async-done(((f32[1800,128]{0,1:T(8,128)}), f32[1800,2048]{0,1:T(8,128)}) %all-gather.3.cloned.1.call-update) | async-done | bytes 14745616 | tf_op jit(solution)/shard_map/all_gather | solution.py:9
  212.6 56.3 %convolution_multiply_fusion = f32[1800,960]{1,0:T(8,128)} fusion(f32[1800,2048]{0,1:T(8,128)} %all-gather.3.cloned.1.call-done, f32[2048,960]{0,1:T(8,128)} %all-gather.5.cloned.1.call-done), kind=kOutput, calls=%fused_computation | convolution fusion | flops 21235392512 | bytes 29521920 | tf_op jit(solution)/shard_map/dot_general | solution.py:10
Async XLA Ops:
  6.5 119.1 %all-gather.5.cloned.1.call-start = ((), (), s32[]{:S(2)}) async-start(), calls=%async_computation.2 | async-start | bytes 8847360 | tf_op jit(solution)/shard_map/all_gather | solution.py:12
  7.3 205.3 %all-gather.3.cloned.1.call-start = ((), (), s32[]{:S(2)}) async-start(), calls=%async_computation.1 | async-start | bytes 16711680 | tf_op jit(solution)/shard_map/all_gather | solution.py:9
Sparse Core Ops, SparseCore 0:
  9.5 116.0 all-gather.4
  127.3 85.2 all-gather.2

commit v2 on v1

v2 whole, which is shorter than its diff:
```python
import functools

import jax
import jax.numpy as jnp
from jax import lax
from jax.experimental import pallas as pl
from jax.experimental.pallas import tpu as pltpu
from jax.sharding import PartitionSpec as P

MESH = pl.DeviceIdType.MESH


def _tile(n, cands):
    for c in cands:
        if n % c == 0:
            return c
    return n


def _split(x):
    hi = x.astype(jnp.bfloat16)
    lo = (x - hi.astype(jnp.float32)).astype(jnp.bfloat16)
    return hi, lo


def ladder_kernel(ng, nk, at_ref, bt_ref, ct_ref, a_full, b_full, ah, al, bh, bl,
                  sem_at, sem_a, sem_b, snd_at, snd_a, snd_b):
    g = lax.axis_index("ga")
    k = lax.axis_index("ka")
    cw = at_ref.shape[1]
    nb, bk = bt_ref.shape
    kb = ng * cw
    q = bk // kb
    rp = ct_ref.shape[1]

    barrier = pltpu.get_barrier_semaphore()
    for s in range(1, ng):
        pl.semaphore_signal(barrier, inc=1, device_id=(lax.rem(g + s, ng), k), device_id_type=MESH)
    for s in range(1, nk):
        pl.semaphore_signal(barrier, inc=1, device_id=(g, lax.rem(k + s, nk)), device_id_type=MESH)
    pl.semaphore_wait(barrier, ng - 1 + nk - 1)

    def a_rows(kk, gg):
        return a_full.at[pl.ds(pl.multiple_of(kk * kb + gg * cw, 8), cw), :]

    def a_block(kk):
        return a_full.at[pl.ds(pl.multiple_of(kk * kb, 8), kb), :]

    def b_cols(gg):
        return b_full.at[:, pl.ds(pl.multiple_of(gg * bk, 128), bk)]

    at_copies = []
    for s in range(1, ng):
        g2 = lax.rem(g + s, ng)
        c = pltpu.make_async_remote_copy(
            src_ref=at_ref.at[g2], dst_ref=a_rows(k, g), send_sem=snd_at.at[s],
            recv_sem=sem_at.at[g], device_id=(g2, k), device_id_type=MESH)
        c.start()
        at_copies.append(c)
    pltpu.make_async_copy(at_ref.at[g], a_rows(k, g), sem_at.at[g]).start()
    b_copies = []
    for s in range(1, ng):
        g2 = lax.rem(g + s, ng)
        c = pltpu.make_async_remote_copy(
            src_ref=bt_ref, dst_ref=b_cols(g), send_sem=snd_b.at[s],
            recv_sem=sem_b.at[g], device_id=(g2, k), device_id_type=MESH)
        c.start()
        b_copies.append(c)
    pltpu.make_async_copy(bt_ref, b_cols(g), sem_b.at[g]).start()

    ct_ref[...] = jnp.zeros_like(ct_ref)

    for s in range(ng):
        g2 = lax.rem(g + s, ng)
        pltpu.make_async_copy(at_ref.at[0], a_rows(k, g2), sem_at.at[g2]).wait()

    a_copies = []
    for s in range(1, nk):
        k2 = lax.rem(k + s, nk)
        c = pltpu.make_async_remote_copy(
            src_ref=a_block(k), dst_ref=a_block(k), send_sem=snd_a.at[s],
            recv_sem=sem_a.at[k], device_id=(g, k2), device_id_type=MESH)
        c.start()
        a_copies.append(c)

    tm = _tile(nb, (192, 240, 160, 128, 120, 96, 64, 48, 32, 16))
    tn = _tile(rp, (384, 640, 256, 128))
    nmt, nnt = nb // tm, rp // tn
    ra = _tile(bk, (32, 16, 8))
    rb = _tile(nb, (120, 96, 64, 48, 32, 16, 8))

    def chunk(i, carry):
        j = lax.rem(k // q + i, ng)
        pltpu.make_async_copy(bt_ref, b_cols(j), sem_b.at[j]).wait()
        for t in range(q):
            kk = j * q + t

            @pl.when(kk != k)
            def _():
                pltpu.make_async_copy(a_block(0), a_block(kk), sem_a.at[kk]).wait()

        k0 = pl.multiple_of(j * bk, 128)

        def split_a(r, c):
            r0 = pl.multiple_of(r * ra, 8)
            hi, lo = _split(a_full[pl.ds(k0 + r0, ra), :])
            ah[pl.ds(r0, ra), :] = hi
            al[pl.ds(r0, ra), :] = lo
            return c

        lax.fori_loop(0, bk // ra, split_a, 0)

        def split_b(r, c):
            r0 = pl.multiple_of(r * rb, 8)
            hi, lo = _split(b_full[pl.ds(r0, rb), pl.ds(k0, bk)])
            bh[pl.ds(r0, rb), :] = hi
            bl[pl.ds(r0, rb), :] = lo
            return c

        lax.fori_loop(0, nb // rb, split_b, 0)

        def mm(t, c):
            m0 = pl.multiple_of((t // nnt) * tm, 8)
            n0 = pl.multiple_of((t % nnt) * tn, 128)
            bh_t = bh[pl.ds(m0, tm), :]
            bl_t = bl[pl.ds(m0, tm), :]
            ah_t = ah[:, pl.ds(n0, tn)]
            al_t = al[:, pl.ds(n0, tn)]
            d = jnp.dot(bh_t, ah_t, preferred_element_type=jnp.float32)
            d = d + jnp.dot(bh_t, al_t, preferred_element_type=jnp.float32)
            d = d + jnp.dot(bl_t, ah_t, preferred_element_type=jnp.float32)
            ct_ref[pl.ds(m0, tm), pl.ds(n0, tn)] += d
            return c

        lax.fori_loop(0, nmt * nnt, mm, 0)
        return carry

    lax.fori_loop(0, ng, chunk, 0)

    for c in at_copies + b_copies + a_copies:
        c.wait_send()


def solution(mesh):
    ng = mesh.shape["ga"]
    nk = mesh.shape["ka"]

    def per_device(amplitudes, integrals):
        ij, cw = amplitudes.shape
        bk, nb = integrals.shape
        r = ij // ng
        rp = -(-r // 128) * 128
        cd = bk * ng
        at = amplitudes.reshape(ng, r, cw).transpose(0, 2, 1)
        at = jnp.pad(at, ((0, 0), (0, 0), (0, rp - r)))
        bt = integrals.T
        vmem = pltpu.VMEM
        ct = pl.pallas_call(
            functools.partial(ladder_kernel, ng, nk),
            out_shape=jax.ShapeDtypeStruct((nb, rp), jnp.float32),
            in_specs=[pl.BlockSpec(memory_space=vmem)] * 2,
            out_specs=pl.BlockSpec(memory_space=vmem),
            scratch_shapes=[
                vmem((cd, rp), jnp.float32),
                vmem((nb, cd), jnp.float32),
                vmem((bk, rp), jnp.bfloat16),
                vmem((bk, rp), jnp.bfloat16),
                vmem((nb, bk), jnp.bfloat16),
                vmem((nb, bk), jnp.bfloat16),
                pltpu.SemaphoreType.DMA((ng,)),
                pltpu.SemaphoreType.DMA((nk,)),
                pltpu.SemaphoreType.DMA((ng,)),
                pltpu.SemaphoreType.DMA((ng,)),
                pltpu.SemaphoreType.DMA((nk,)),
                pltpu.SemaphoreType.DMA((ng,)),
            ],
            compiler_params=pltpu.CompilerParams(
                collective_id=0, has_side_effects=True, vmem_limit_bytes=60 * 1024 * 1024
            ),
            cost_estimate=pl.CostEstimate(
                flops=6 * nb * rp * cd, bytes_accessed=4 * (cd * rp + nb * cd + nb * rp),
                transcendentals=0),
        )(at, bt)
        return (0.5 * ct[:, :r]).T

    placed = (P(None, ("ka", "ga")), P("ga", "ka"))
    return jax.shard_map(
        per_device, mesh=mesh, in_specs=placed, out_specs=P("ga", "ka"), check_vma=False
    )
```

time: 276 us -> 363 us (1.32)
  Pallas kernels: 0 us -> 343 us
  waiting for transfers between devices: 178 us -> 0 us
  matrix products: 56.3 us -> 0 us
  blocking collectives: 26.1 us -> 0 us
  between operations: 13.4 us -> 0.03 us
  local copies, waits for them, and re-layouts: 1.97 us -> 11.7 us
  other arithmetic: 0 us -> 6.58 us
    pallas_call x0 -> x1, Pallas kernels: none -> 343 us  [per_device(): pl.pallas_call(functools.partial(ladder_kernel, ng, nk), out_shape=jax.Sh...]
    all_gather x2 -> x0, waiting for transfers between devices: 177 us -> none  [the longest x1 90.2 us: per_device(): lax.all_gather(integrals, 'ga', axis=0, tiled=True)]
    dot_general x1 -> x0, matrix products: 56.3 us -> none  [per_device(): jnp.dot(full_rows, lax.all_gather(integrals, 'ga', axis=0, tiled=True), p...]
    all_to_all x1 -> x0, blocking collectives: 26.1 us -> none  [per_device(): lax.all_to_all(amplitudes, 'ga', split_axis=0, concat_axis=1, tiled=True)]
    transpose x0 -> x1, local copies, waits for them, and re-layouts: none -> 8.71 us  [per_device(): return (0.5 * ct[:, :r]).T]
    transpose x0 -> x1, other arithmetic: none -> 6.58 us  [per_device(): return (0.5 * ct[:, :r]).T]
  transfers between devices with their start and end apart: 2 -> 0, of which waited for: 2 -> 0; matrix products, arithmetic and copies ran while one was open for 0% -> 0% of each run, Pallas kernels for 0% -> 0%
where the time goes in v2:
time: 363 us; the launch traced here: 361 us
  Pallas kernels  343 us (94%)
  local copies, waits for them, and re-layouts  11.7 us (3%)
  other arithmetic  6.58 us (2%)
    pallas_call x1, Pallas kernels, per_device(): pl.pallas_call(functools.partial(ladder_kernel, ng, nk), out_shape=jax.Sh...  343 us
    transpose x1, local copies, waits for them, and re-layouts, per_device(): return (0.5 * ct[:, :r]).T  8.71 us

profile of v2, /device:TPU:1, one launch (start us, length us, event | category | flops | bytes accessed | tf_op | source)
XLA Modules:
  0.0 361.4 jit_solution(13103201976787737326)
XLA Ops:
  0.0 1.8 reshape.3
  1.8 0.2 copy.7
  2.0 1.0 pad.4.at_ref
  3.0 343.1 %shard_map.28 = f32[960,1920]{1,0:T(8,128)} custom-call(f32[8,16,1920]{2,1,0:T(8,128)} %pad.4.at_ref, f32[960,256]{1,0:T(8,128)} %bitcast.9), custom_call_target="tpu_custom_call" | custom-call | flops 22649241600 | bytes 30965760 | tf_op jit(solution)/shard_map/pallas_call | solution.py:158
  346.1 6.6 %multiply_bitcast_fusion = f32[1800,960]{0,1:T(8,128)} fusion(f32[960,1920]{1,0:T(8,128)} %shard_map.28), kind=kLoop, calls=%fused_computation | loop fusion | flops 1728000 | bytes 13824000 | tf_op jit(solution)/shard_map/transpose | solution.py:184
  352.7 8.7 %copy.5 = f32[1800,960]{1,0:T(8,128)} copy(f32[1800,960]{0,1:T(8,128)} %multiply_bitcast_fusion) | data formatting | bytes 13824000 | tf_op jit(solution)/shard_map/transpose | solution.py:184

commit v3 on v1

v3 whole, which is shorter than its diff:
```python
import jax
import jax.numpy as jnp
from jax import lax
from jax.sharding import PartitionSpec as P


def per_device(ng, amplitudes, integrals):
    g = lax.axis_index("ga")
    received = [integrals]
    for s in range(1, ng):
        received.append(lax.ppermute(integrals, "ga", [(i, (i + s) % ng) for i in range(ng)]))
    by_shift = jnp.stack(received)
    full_b = jnp.take(by_shift, lax.rem(g - jnp.arange(ng) + ng, ng), axis=0)
    full_b = full_b.reshape(-1, integrals.shape[1])
    regrouped = lax.all_to_all(amplitudes, "ga", split_axis=0, concat_axis=1, tiled=True)
    full_rows = lax.all_gather(regrouped, "ka", axis=1, tiled=True)
    ladder = jnp.dot(
        full_rows,
        full_b,
        precision=lax.Precision.HIGH,
        preferred_element_type=jnp.float32,
    )
    return 0.5 * ladder


def solution(mesh):
    placed = (P(None, ("ka", "ga")), P("ga", "ka"))
    ng = mesh.shape["ga"]
    return jax.shard_map(
        lambda a, b: per_device(ng, a, b), mesh=mesh, in_specs=placed, out_specs=P("ga", "ka"),
        check_vma=False
    )
```

time: 276 us -> 266 us (0.964); the launches traced: 276 us -> 262 us
  waiting for transfers between devices: 178 us -> 112 us
  starting transfers between devices: 0.04 us -> 43.7 us
  local copies, waits for them, and re-layouts: 1.97 us -> 38.9 us
  matrix products: 56.3 us -> 31.1 us
    ppermute x0 -> x7, waiting for transfers between devices: none -> 112 us  [per_device(): lax.ppermute(integrals, 'ga', [(i, (i + s) % ng) for i in range(ng)])]
    all_gather x1 -> x0, waiting for transfers between devices: 90.2 us -> none  [per_device(): lax.all_gather(integrals, 'ga', axis=0, tiled=True)]
    all_gather x1, waiting for transfers between devices: 87 us -> 0.01 us  [per_device(): full_rows = lax.all_gather(regrouped, 'ka', axis=1, tiled=True)]
    ppermute x0 -> x7, starting transfers between devices: none -> 43.7 us  [per_device(): lax.ppermute(integrals, 'ga', [(i, (i + s) % ng) for i in range(ng)])]
    dot_general x1, matrix products: 56.3 us -> 31.1 us  [per_device(): jnp.dot(full_rows, full_b, precision=lax.Precision.HIGH, preferred_elemen...]
    gather x0 -> x2, local copies, waits for them, and re-layouts: none -> 15 us  [per_device(): full_b = jnp.take(by_shift, lax.rem(g - jnp.arange(ng) + ng, ng), axis=0)]
    unnamed x0 -> x9, local copies, waits for them, and re-layouts: none -> 12 us
    mul x0 -> x1, local copies, waits for them, and re-layouts: none -> 8.71 us  [per_device(): return 0.5 * ladder]
  transfers between devices with their start and end apart: 2 -> 8, of which waited for: 2 -> 4; matrix products, arithmetic and copies ran while one was open for 0% -> 11% of each run, Pallas kernels for 0% -> 0%
where the time goes in v3:
time: 266 us; the launch traced here: 262 us
  waiting for transfers between devices  112 us (42%)
  starting transfers between devices  43.7 us (16%)
  local copies, waits for them, and re-layouts  38.9 us (15%)
  matrix products  31.1 us (12%)
  blocking collectives  23.5 us (9%)
  between operations  13.4 us (5%)
    ppermute x7, waiting for transfers between devices, per_device(): lax.ppermute(integrals, 'ga', [(i, (i + s) % ng) for i in range(ng)])  112 us
    ppermute x7, starting transfers between devices, per_device(): lax.ppermute(integrals, 'ga', [(i, (i + s) % ng) for i in range(ng)])  43.7 us
    dot_general x1, matrix products, per_device(): jnp.dot(full_rows, full_b, precision=lax.Precision.HIGH, preferred_elemen...  31.1 us
    all_to_all x1, blocking collectives, per_device(): lax.all_to_all(amplitudes, 'ga', split_axis=0, concat_axis=1, tiled=True)  23.5 us
    gather x2, local copies, waits for them, and re-layouts, per_device(): full_b = jnp.take(by_shift, lax.rem(g - jnp.arange(ng) + ng, ng), axis=0)  15 us
    unnamed x9, local copies, waits for them, and re-layouts  12 us
    mul x1, local copies, waits for them, and re-layouts, per_device(): return 0.5 * ladder  8.71 us
  transfers between devices with their start and end apart: 8, of which 4 were waited for; matrix products, arithmetic and copies ran while one was open for 11% of the time, Pallas kernels for 0%

profile of v3, /device:TPU:1, one launch (start us, length us, event | category | flops | bytes accessed | tf_op | source)
XLA Modules:
  0.0 262.4 jit_solution(82143842702994081)
XLA Ops:
  6.5 0.0 all-gather.2.cloned.1.call-start
  6.5 1.9 all_to_all.14
  8.4 0.2 copy.5
  8.6 23.5 %all_to_all.19 = f32[8,1800,16]{1,2,0:T(8,128)} all-to-all(f32[8,1800,16]{1,2,0:T(8,128)S(1)} %copy.5), channel_id=1, replica_groups=mesh['ga'=8,'ka'=16] {'ga'}, dimensions={0} | all-to-all | bytes 1843200 | tf_op jit(solution)/shard_map/all_to_all | solution.py:15
  32.1 0.0 all-gather.2.cloned.1.call-update
  32.1 0.1 collective-permute-start
  32.2 1.9 collective-permute-start.1
  34.2 1.8 collective-permute-start.2
  35.9 2.1 collective-permute-start.3
  38.0 1.4 collective-permute-start.4
  39.4 2.2 bitcast_dynamic-update-slice_fusion.7
  41.7 0.1 broadcast_in_dim.14
  41.8 32.2 %collective-permute-done = f32[256,960]{0,1:T(8,128)} collective-permute-done((f32[256,960]{0,1:T(8,128)}, f32[256,960]{0,1:T(8,128)}, u32[]{:S(2)}, u32[]{:S(2)}) %collective-permute-start) | collective-permute-done | bytes 983072 | tf_op jit(solution)/shard_map/ppermute | solution.py:11
  74.0 0.0 collective-permute-start.5
  74.0 2.2 bitcast_dynamic-update-slice_fusion.6
  76.2 0.0 collective-permute-done.1
  76.2 36.4 %collective-permute-start.6 = (f32[256,960]{0,1:T(8,128)S(1)}, f32[256,960]{0,1:T(8,128)S(1)}, u32[]{:S(2)}, u32[]{:S(2)}) collective-permute-start(f32[256,960]{0,1:T(8,128)S(1)} %copy-done), channel_id=1, source_target_pairs={{0,112},{16,0},{32,16},{48,32},{64,48},{80,64},{96,80},{112,96},{1... | collective-permute-start | bytes 2949128 | tf_op jit(solution)/shard_map/ppermute | solution.py:11
  112.6 2.3 bitcast_dynamic-update-slice_fusion.5
  114.9 0.0 collective-permute-done.2
  114.9 2.2 bitcast_dynamic-update-slice_fusion.4
  117.2 0.0 collective-permute-done.3
  117.2 1.0 bitcast_dynamic-update-slice_fusion.3
  118.2 4.7 %collective-permute-done.4 = f32[256,960]{0,1:T(8,128)S(1)} collective-permute-done((f32[256,960]{0,1:T(8,128)}, f32[256,960]{0,1:T(8,128)S(1)}, u32[]{:S(2)}, u32[]{:S(2)}) %collective-permute-start.4) | collective-permute-done | bytes 983072 | tf_op jit(solution)/shard_map/ppermute | solution.py:11
  122.9 1.0 bitcast_dynamic-update-slice_fusion.2
  123.9 35.9 %collective-permute-done.5 = f32[256,960]{0,1:T(8,128)S(1)} collective-permute-done((f32[256,960]{0,1:T(8,128)S(1)}, f32[256,960]{0,1:T(8,128)S(1)}, u32[]{:S(2)}, u32[]{:S(2)}) %collective-permute-start.5) | collective-permute-done | bytes 983072 | tf_op jit(solution)/shard_map/ppermute | solution.py:11
  159.8 1.0 bitcast_dynamic-update-slice_fusion.1
  160.8 38.9 %collective-permute-done.6 = f32[256,960]{0,1:T(8,128)S(1)} collective-permute-done((f32[256,960]{0,1:T(8,128)S(1)}, f32[256,960]{0,1:T(8,128)S(1)}, u32[]{:S(2)}, u32[]{:S(2)}) %collective-permute-start.6) | collective-permute-done | bytes 983072 | tf_op jit(solution)/shard_map/ppermute | solution.py:11
  199.7 1.0 bitcast_dynamic-update-slice_fusion
  200.7 7.4 %gather_fusion = f32[8,256,960]{1,2,0:T(8,128)} fusion(f32[8,256,960]{1,2,0:T(8,128)} %bitcast_dynamic-update-slice_fusion, s32[1024]{0:T(1024)S(1)} %pad_clamp_fusion), kind=kCustom, calls=%fused_computation | custom fusion | bytes 15728672 | tf_op jit(solution)/shard_map/jit(_take)/gather | solution.py:13
  208.2 7.6 %copy.7 = f32[8,120,8,256]{3,2,0,1:T(8,128)} copy(f32[8,120,8,256]{3,2,1,0:T(8,128)} %bitcast.28) | data formatting | bytes 15728640 | tf_op jit(solution)/shard_map/jit(_take)/gather | solution.py:13
  215.7 31.1 %multiply_bitcast_fusion = f32[1800,960]{0,1:T(8,128)} fusion(f32[1800,2048]{0,1:T(8,128)} %all-gather.2.cloned.1.call-done, f32[2048,960]{0,1:T(8,128)} %bitcast.29, pred[2048]{0:T(1024)(128)(4,1)S(1)} %broadcast_in_dim.15), kind=kOutput, calls=%fused_computation.3 | convolution fusion | flops 21237358592 | bytes 29523968 | tf_op jit(solution)/shard_map/dot_general | solution.py:17
  246.8 8.7 %copy.6 = f32[1800,960]{1,0:T(8,128)} copy(f32[1800,960]{0,1:T(8,128)} %multiply_bitcast_fusion) | data formatting | bytes 13824000 | tf_op jit(solution)/shard_map/mul | solution.py:23
  (7 shorter events, 0.0 us)
Async XLA Ops:
  6.5 67.4 %copy-start = (f32[256,960]{0,1:T(8,128)S(1)}, f32[256,960]{0,1:T(8,128)}, u32[]{:S(2)}) copy-start(f32[256,960]{0,1:T(8,128)} %param.3) | copy-start | bytes 2949124
  6.5 209.2 %all-gather.2.cloned.1.call-start = ((), (), s32[]{:S(2)}) async-start(), calls=%async_computation.1 | async-start | bytes 16711680 | tf_op jit(solution)/shard_map/all_gather | solution.py:16
  32.1 41.9 %collective-permute-start = (f32[256,960]{0,1:T(8,128)}, f32[256,960]{0,1:T(8,128)}, u32[]{:S(2)}, u32[]{:S(2)}) collective-permute-start(f32[256,960]{0,1:T(8,128)} %param.3), channel_id=1, source_target_pairs={{0,16},{16,32},{32,48},{48,64},{64,80},{80,96},{96,112},{112,0},{1... | collective-permute-start | bytes 2949128 | tf_op jit(solution)/shard_map/ppermute | solution.py:11
  32.2 44.0 %collective-permute-start.1 = (f32[256,960]{0,1:T(8,128)}, f32[256,960]{0,1:T(8,128)}, u32[]{:S(2)}, u32[]{:S(2)}) collective-permute-start(f32[256,960]{0,1:T(8,128)} %param.3), channel_id=1, source_target_pairs={{0,32},{16,48},{32,64},{48,80},{64,96},{80,112},{96,0},{112,16},{1... | collective-permute-start | bytes 2949128 | tf_op jit(solution)/shard_map/ppermute | solution.py:11
  34.2 80.8 %collective-permute-start.2 = (f32[256,960]{0,1:T(8,128)}, f32[256,960]{0,1:T(8,128)}, u32[]{:S(2)}, u32[]{:S(2)}) collective-permute-start(f32[256,960]{0,1:T(8,128)} %param.3), channel_id=1, source_target_pairs={{0,48},{16,64},{32,80},{48,96},{64,112},{80,0},{96,16},{112,32},{1... | collective-permute-start | bytes 2949128 | tf_op jit(solution)/shard_map/ppermute | solution.py:11
  35.9 81.2 %collective-permute-start.3 = (f32[256,960]{0,1:T(8,128)}, f32[256,960]{0,1:T(8,128)S(1)}, u32[]{:S(2)}, u32[]{:S(2)}) collective-permute-start(f32[256,960]{0,1:T(8,128)} %param.3), channel_id=1, source_target_pairs={{0,64},{16,80},{32,96},{48,112},{64,0},{80,16},{96,32},{112,48},{1... | collective-permute-start | bytes 2949128 | tf_op jit(solution)/shard_map/ppermute | solution.py:11
  38.0 84.8 %collective-permute-start.4 = (f32[256,960]{0,1:T(8,128)}, f32[256,960]{0,1:T(8,128)S(1)}, u32[]{:S(2)}, u32[]{:S(2)}) collective-permute-start(f32[256,960]{0,1:T(8,128)} %param.3), channel_id=1, source_target_pairs={{0,80},{16,96},{32,112},{48,0},{64,16},{80,32},{96,48},{112,64},{1... | collective-permute-start | bytes 2949128 | tf_op jit(solution)/shard_map/ppermute | solution.py:11
  74.0 85.8 %collective-permute-start.5 = (f32[256,960]{0,1:T(8,128)S(1)}, f32[256,960]{0,1:T(8,128)S(1)}, u32[]{:S(2)}, u32[]{:S(2)}) collective-permute-start(f32[256,960]{0,1:T(8,128)S(1)} %copy-done), channel_id=1, source_target_pairs={{0,96},{16,112},{32,0},{48,16},{64,32},{80,48},{96,64},{112,80},{1... | collective-permute-start | bytes 2949128 | tf_op jit(solution)/shard_map/ppermute | solution.py:11
  76.2 123.5 %collective-permute-start.6 = (f32[256,960]{0,1:T(8,128)S(1)}, f32[256,960]{0,1:T(8,128)S(1)}, u32[]{:S(2)}, u32[]{:S(2)}) collective-permute-start(f32[256,960]{0,1:T(8,128)S(1)} %copy-done), channel_id=1, source_target_pairs={{0,112},{16,0},{32,16},{48,32},{64,48},{80,64},{96,80},{112,96},{1... | collective-permute-start | bytes 2949128 | tf_op jit(solution)/shard_map/ppermute | solution.py:11
Sparse Core Ops, SparseCore 0:
  32.2 159.7 all-gather.1

commit v4 on v3

v4 whole, which is shorter than its diff:
```python
import jax
import jax.numpy as jnp
from jax import lax
from jax.sharding import PartitionSpec as P


def per_device(ng, amplitudes, integrals):
    g = lax.axis_index("ga")
    bk, nb = integrals.shape
    bt = integrals.T
    full_bt = jnp.zeros((nb, bk * ng), jnp.float32)
    for s in range(ng):
        got = bt if s == 0 else lax.ppermute(bt, "ga", [(i, (i + s) % ng) for i in range(ng)])
        full_bt = lax.dynamic_update_slice(full_bt, got, (0, lax.rem(g - s + ng, ng) * bk))
    regrouped = lax.all_to_all(amplitudes, "ga", split_axis=0, concat_axis=1, tiled=True)
    full_rows = lax.all_gather(regrouped, "ka", axis=1, tiled=True)
    ladder = lax.dot_general(
        full_rows,
        full_bt,
        (((1,), (1,)), ((), ())),
        precision=lax.Precision.HIGH,
        preferred_element_type=jnp.float32,
    )
    return 0.5 * ladder


def solution(mesh):
    placed = (P(None, ("ka", "ga")), P("ga", "ka"))
    ng = mesh.shape["ga"]
    return jax.shard_map(
        lambda a, b: per_device(ng, a, b), mesh=mesh, in_specs=placed, out_specs=P("ga", "ka"),
        check_vma=False
    )
```

time: 266 us -> 251 us (0.944)
  local copies, waits for them, and re-layouts: 38.9 us -> 28.6 us
  waiting for transfers between devices: 112 us -> 106 us
    gather x2 -> x0, local copies, waits for them, and re-layouts: 15 us -> none  [per_device(): full_b = jnp.take(by_shift, lax.rem(g - jnp.arange(ng) + ng, ng), axis=0)]
    dynamic_update_slice x0 -> x8, local copies, waits for them, and re-layouts: none -> 13.7 us  [per_device(): lax.dynamic_update_slice(full_bt, got, (0, lax.rem(g - s + ng, ng) * bk))]
    unnamed x9 -> x2, local copies, waits for them, and re-layouts: 12 us -> 0.01 us
    ppermute x7, waiting for transfers between devices: 112 us -> 106 us  [per_device(): lax.ppermute(bt, 'ga', [(i, (i + s) % ng) for i in range(ng)])]
    broadcast_in_dim x2 -> x1, local copies, waits for them, and re-layouts: 0.09 us -> 4.1 us  [per_device(): full_bt = jnp.zeros((nb, bk * ng), jnp.float32)]
  transfers between devices with their start and end apart: 8 -> 8, of which waited for: 4 -> 4; matrix products, arithmetic and copies ran while one was open for 11% -> 7% of each run, Pallas kernels for 0% -> 0%
where the time goes in v4:
time: 251 us; the launch traced here: 247 us
  waiting for transfers between devices  106 us (42%)
  starting transfers between devices  44.8 us (18%)
  matrix products  30.9 us (12%)
  local copies, waits for them, and re-layouts  28.6 us (11%)
  blocking collectives  23.5 us (9%)
  between operations  13.4 us (5%)
    ppermute x7, waiting for transfers between devices, per_device(): lax.ppermute(bt, 'ga', [(i, (i + s) % ng) for i in range(ng)])  106 us
    ppermute x7, starting transfers between devices, per_device(): lax.ppermute(bt, 'ga', [(i, (i + s) % ng) for i in range(ng)])  44.8 us
    dot_general x1, matrix products, per_device(): lax.dot_general(full_rows, full_bt, (((1,), (1,)), ((), ())), precision=l...  30.9 us
    all_to_all x1, blocking collectives, per_device(): lax.all_to_all(amplitudes, 'ga', split_axis=0, concat_axis=1, tiled=True)  23.5 us
    dynamic_update_slice x8, local copies, waits for them, and re-layouts, per_device(): lax.dynamic_update_slice(full_bt, got, (0, lax.rem(g - s + ng, ng) * bk))  13.7 us
    mul x1, local copies, waits for them, and re-layouts, per_device(): return 0.5 * ladder  8.71 us
  transfers between devices with their start and end apart: 8, of which 4 were waited for; matrix products, arithmetic and copies ran while one was open for 7% of the time, Pallas kernels for 0%

profile of v4, /device:TPU:1, one launch (start us, length us, event | category | flops | bytes accessed | tf_op | source)
XLA Modules:
  0.0 247.5 jit_solution(5019920644292792922)
XLA Ops:
  6.5 0.0 all-gather.2.cloned.1.call-start
  6.5 1.9 all_to_all.14
  8.4 0.2 copy.4
  8.6 23.5 %all_to_all.19 = f32[8,1800,16]{1,2,0:T(8,128)} all-to-all(f32[8,1800,16]{1,2,0:T(8,128)S(1)} %copy.4), channel_id=1, replica_groups=mesh['ga'=8,'ka'=16] {'ga'}, dimensions={0} | all-to-all | bytes 1843200 | tf_op jit(solution)/shard_map/all_to_all | solution.py:15
  32.1 0.0 all-gather.2.cloned.1.call-update
  32.1 0.1 collective-permute-start
  32.2 1.9 collective-permute-start.1
  34.2 1.8 collective-permute-start.2
  35.9 2.1 collective-permute-start.3
  38.0 1.4 collective-permute-start.4
  39.4 34.6 %collective-permute-done = f32[960,256]{1,0:T(8,128)} collective-permute-done((f32[960,256]{1,0:T(8,128)}, f32[960,256]{1,0:T(8,128)}, u32[]{:S(2)}, u32[]{:S(2)}) %collective-permute-start) | collective-permute-done | bytes 983072 | tf_op jit(solution)/shard_map/ppermute | solution.py:13
  74.0 0.0 collective-permute-start.5
  74.0 1.1 collective-permute-done.1
  75.1 37.5 %collective-permute-start.6 = (f32[960,256]{1,0:T(8,128)}, f32[960,256]{1,0:T(8,128)S(1)}, u32[]{:S(2)}, u32[]{:S(2)}) collective-permute-start(f32[960,256]{1,0:T(8,128)} %bitcast.18), channel_id=1, source_target_pairs={{0,112},{16,0},{32,16},{48,32},{64,48},{80,64},{96,80},{112,96},{1... | collective-permute-start | bytes 2949128 | tf_op jit(solution)/shard_map/ppermute | solution.py:13
  112.6 4.1 %broadcast_in_dim.3 = f32[960,2048]{1,0:T(8,128)} broadcast(f32[]{:T(128)} %constant.47.clone.1), dimensions={} | broadcast | bytes 7864324 | tf_op jit(solution)/shard_map/broadcast_in_dim | solution.py:11
  116.7 0.0 copy-done
  116.7 1.1 constant_dynamic-update-slice_fusion.7
  117.8 2.3 constant_dynamic-update-slice_fusion.6
  120.1 2.3 constant_dynamic-update-slice_fusion.5
  122.4 0.0 collective-permute-done.2
  122.4 2.4 constant_dynamic-update-slice_fusion.4
  124.8 0.0 collective-permute-done.3
  124.8 2.4 constant_dynamic-update-slice_fusion.3
  127.1 0.0 collective-permute-done.4
  127.1 1.1 constant_dynamic-update-slice_fusion.2
  128.2 31.6 %collective-permute-done.5 = f32[960,256]{1,0:T(8,128)S(1)} collective-permute-done((f32[960,256]{1,0:T(8,128)}, f32[960,256]{1,0:T(8,128)S(1)}, u32[]{:S(2)}, u32[]{:S(2)}) %collective-permute-start.5) | collective-permute-done | bytes 983072 | tf_op jit(solution)/shard_map/ppermute | solution.py:13
  159.9 1.1 constant_dynamic-update-slice_fusion.1
  161.0 38.9 %collective-permute-done.6 = f32[960,256]{1,0:T(8,128)S(1)} collective-permute-done((f32[960,256]{1,0:T(8,128)}, f32[960,256]{1,0:T(8,128)S(1)}, u32[]{:S(2)}, u32[]{:S(2)}) %collective-permute-start.6) | collective-permute-done | bytes 983072 | tf_op jit(solution)/shard_map/ppermute | solution.py:13
  199.8 1.2 constant_dynamic-update-slice_fusion
  201.0 0.0 all-gather.2.cloned.1.call-done
  201.0 30.9 %multiply_bitcast_fusion = f32[1800,960]{0,1:T(8,128)} fusion(f32[960,2048]{1,0:T(8,128)} %constant_dynamic-update-slice_fusion, f32[1800,2048]{0,1:T(8,128)} %all-gather.2.cloned.1.call-done), kind=kOutput, calls=%fused_computation | convolution fusion | flops 21235392512 | bytes 29521920 | tf_op jit(solution)/shard_map/dot_general | solution.py:17
  231.9 8.7 %copy.5 = f32[1800,960]{1,0:T(8,128)} copy(f32[1800,960]{0,1:T(8,128)} %multiply_bitcast_fusion) | data formatting | bytes 13824000 | tf_op jit(solution)/shard_map/mul | solution.py:24
  (1 shorter events, 0.0 us)
Async XLA Ops:
  6.5 110.2 %copy-start = (f32[256,960]{0,1:T(8,128)S(1)}, f32[256,960]{0,1:T(8,128)}, u32[]{:S(2)}) copy-start(f32[256,960]{0,1:T(8,128)} %param.3) | copy-start | bytes 2949124
  6.5 194.5 %all-gather.2.cloned.1.call-start = ((), (), s32[]{:S(2)}) async-start(), calls=%async_computation.1 | async-start | bytes 16711680 | tf_op jit(solution)/shard_map/all_gather | solution.py:16
  32.1 41.9 %collective-permute-start = (f32[960,256]{1,0:T(8,128)}, f32[960,256]{1,0:T(8,128)}, u32[]{:S(2)}, u32[]{:S(2)}) collective-permute-start(f32[960,256]{1,0:T(8,128)} %bitcast.12), channel_id=1, source_target_pairs={{0,16},{16,32},{32,48},{48,64},{64,80},{80,96},{96,112},{112,0},{1... | collective-permute-start | bytes 2949128 | tf_op jit(solution)/shard_map/ppermute | solution.py:13
  32.2 42.9 %collective-permute-start.1 = (f32[960,256]{1,0:T(8,128)}, f32[960,256]{1,0:T(8,128)}, u32[]{:S(2)}, u32[]{:S(2)}) collective-permute-start(f32[960,256]{1,0:T(8,128)} %bitcast.13), channel_id=1, source_target_pairs={{0,32},{16,48},{32,64},{48,80},{64,96},{80,112},{96,0},{112,16},{1... | collective-permute-start | bytes 2949128 | tf_op jit(solution)/shard_map/ppermute | solution.py:13
  34.2 88.3 %collective-permute-start.2 = (f32[960,256]{1,0:T(8,128)}, f32[960,256]{1,0:T(8,128)}, u32[]{:S(2)}, u32[]{:S(2)}) collective-permute-start(f32[960,256]{1,0:T(8,128)} %bitcast.14), channel_id=1, source_target_pairs={{0,48},{16,64},{32,80},{48,96},{64,112},{80,0},{96,16},{112,32},{1... | collective-permute-start | bytes 2949128 | tf_op jit(solution)/shard_map/ppermute | solution.py:13
  35.9 88.8 %collective-permute-start.3 = (f32[960,256]{1,0:T(8,128)}, f32[960,256]{1,0:T(8,128)}, u32[]{:S(2)}, u32[]{:S(2)}) collective-permute-start(f32[960,256]{1,0:T(8,128)} %bitcast.15), channel_id=1, source_target_pairs={{0,64},{16,80},{32,96},{48,112},{64,0},{80,16},{96,32},{112,48},{1... | collective-permute-start | bytes 2949128 | tf_op jit(solution)/shard_map/ppermute | solution.py:13
  38.0 89.1 %collective-permute-start.4 = (f32[960,256]{1,0:T(8,128)}, f32[960,256]{1,0:T(8,128)S(1)}, u32[]{:S(2)}, u32[]{:S(2)}) collective-permute-start(f32[960,256]{1,0:T(8,128)} %bitcast.16), channel_id=1, source_target_pairs={{0,80},{16,96},{32,112},{48,0},{64,16},{80,32},{96,48},{112,64},{1... | collective-permute-start | bytes 2949128 | tf_op jit(solution)/shard_map/ppermute | solution.py:13
  74.0 85.9 %collective-permute-start.5 = (f32[960,256]{1,0:T(8,128)}, f32[960,256]{1,0:T(8,128)S(1)}, u32[]{:S(2)}, u32[]{:S(2)}) collective-permute-start(f32[960,256]{1,0:T(8,128)} %bitcast.17), channel_id=1, source_target_pairs={{0,96},{16,112},{32,0},{48,16},{64,32},{80,48},{96,64},{112,80},{1... | collective-permute-start | bytes 2949128 | tf_op jit(solution)/shard_map/ppermute | solution.py:13
  75.1 124.7 %collective-permute-start.6 = (f32[960,256]{1,0:T(8,128)}, f32[960,256]{1,0:T(8,128)S(1)}, u32[]{:S(2)}, u32[]{:S(2)}) collective-permute-start(f32[960,256]{1,0:T(8,128)} %bitcast.18), channel_id=1, source_target_pairs={{0,112},{16,0},{32,16},{48,32},{64,48},{80,64},{96,80},{112,96},{1... | collective-permute-start | bytes 2949128 | tf_op jit(solution)/shard_map/ppermute | solution.py:13
Sparse Core Ops, SparseCore 0:
  32.2 159.7 all-gather.1

commit v5 on v4

--- a/solution.py
+++ b/solution.py
@@ -7,11 +7,17 @@
 def per_device(ng, amplitudes, integrals):
     g = lax.axis_index("ga")
     bk, nb = integrals.shape
+    nz = ng // 2
+    yh, z = g // nz, lax.rem(g, nz)
     bt = integrals.T
-    full_bt = jnp.zeros((nb, bk * ng), jnp.float32)
-    for s in range(ng):
-        got = bt if s == 0 else lax.ppermute(bt, "ga", [(i, (i + s) % ng) for i in range(ng)])
-        full_bt = lax.dynamic_update_slice(full_bt, got, (0, lax.rem(g - s + ng, ng) * bk))
+    full_bt = lax.dynamic_update_slice(jnp.zeros((nb, bk * ng), jnp.float32), bt, (0, g * bk))
+    offsets = [(1, dz) for dz in range(nz)] + [(0, dz) for dz in range(nz // 2, 0, -1)]
+    offsets += [(0, dz) for dz in range(nz // 2 + 1, nz)]
+    for dy, dz in offsets:
+        pairs = [(i, ((i // nz + dy) % 2) * nz + (i % nz + dz) % nz) for i in range(ng)]
+        got = lax.ppermute(bt, "ga", pairs)
+        src = lax.rem(yh + dy, 2) * nz + lax.rem(z - dz + nz, nz)
+        full_bt = lax.dynamic_update_slice(full_bt, got, (0, src * bk))
     regrouped = lax.all_to_all(amplitudes, "ga", split_axis=0, concat_axis=1, tiled=True)
     full_rows = lax.all_gather(regrouped, "ka", axis=1, tiled=True)
     ladder = lax.dot_general(

time: 251 us -> 246 us (0.980)
  starting transfers between devices: 44.8 us -> 10.9 us
  waiting for transfers between devices: 106 us -> 135 us
    ppermute x7, starting transfers between devices: 44.8 us -> 10.9 us  [per_device(): got = lax.ppermute(bt, 'ga', pairs)]
    ppermute x7, waiting for transfers between devices: 106 us -> 135 us  [per_device(): got = lax.ppermute(bt, 'ga', pairs)]
where the time goes in v5:
time: 246 us; the launch traced here: 243 us
  waiting for transfers between devices  135 us (55%)
  matrix products  30.9 us (13%)
  local copies, waits for them, and re-layouts  28.7 us (12%)
  blocking collectives  23.5 us (10%)
  between operations  13.4 us (5%)
  starting transfers between devices  10.9 us (4%)
    ppermute x7, waiting for transfers between devices, per_device(): got = lax.ppermute(bt, 'ga', pairs)  135 us
    dot_general x1, matrix products, per_device(): lax.dot_general(full_rows, full_bt, (((1,), (1,)), ((), ())), precision=l...  30.9 us
    all_to_all x1, blocking collectives, per_device(): lax.all_to_all(amplitudes, 'ga', split_axis=0, concat_axis=1, tiled=True)  23.5 us
    dynamic_update_slice x7, local copies, waits for them, and re-layouts, per_device(): full_bt = lax.dynamic_update_slice(full_bt, got, (0, src * bk))  12.7 us
    ppermute x7, starting transfers between devices, per_device(): got = lax.ppermute(bt, 'ga', pairs)  10.9 us
    mul x1, local copies, waits for them, and re-layouts, per_device(): return 0.5 * ladder  8.71 us
  transfers between devices with their start and end apart: 8, of which 4 were waited for; matrix products, arithmetic and copies ran while one was open for 7% of the time, Pallas kernels for 0%

profile of v5, /device:TPU:1, one launch (start us, length us, event | category | flops | bytes accessed | tf_op | source)
XLA Modules:
  0.0 242.7 jit_solution(2678853566754020403)
XLA Ops:
  6.5 0.0 all-gather.2.cloned.1.call-start
  6.5 1.9 all_to_all.14
  8.4 0.2 copy.4
  8.6 23.5 %all_to_all.19 = f32[8,1800,16]{1,2,0:T(8,128)} all-to-all(f32[8,1800,16]{1,2,0:T(8,128)S(1)} %copy.4), channel_id=1, replica_groups=mesh['ga'=8,'ka'=16] {'ga'}, dimensions={0} | all-to-all | bytes 1843200 | tf_op jit(solution)/shard_map/all_to_all | solution.py:21
  32.1 0.0 all-gather.2.cloned.1.call-update
  32.1 1.1 collective-permute-start
  33.2 1.7 collective-permute-start.1
  34.9 3.0 %collective-permute-start.2 = (f32[960,256]{1,0:T(8,128)}, f32[960,256]{1,0:T(8,128)}, u32[]{:S(2)}, u32[]{:S(2)}) collective-permute-start(f32[960,256]{1,0:T(8,128)} %bitcast.14), channel_id=1, source_target_pairs={{0,96},{16,112},{32,64},{48,80},{64,32},{80,48},{96,0},{112,16},{1... | collective-permute-start | bytes 2949128 | tf_op jit(solution)/shard_map/ppermute | solution.py:18
  37.9 2.5 %collective-permute-start.3 = (f32[960,256]{1,0:T(8,128)}, f32[960,256]{1,0:T(8,128)}, u32[]{:S(2)}, u32[]{:S(2)}) collective-permute-start(f32[960,256]{1,0:T(8,128)} %bitcast.15), channel_id=1, source_target_pairs={{0,112},{16,64},{32,80},{48,96},{64,48},{80,0},{96,16},{112,32},{1... | collective-permute-start | bytes 2949128 | tf_op jit(solution)/shard_map/ppermute | solution.py:18
  40.4 1.9 collective-permute-start.4
  42.3 23.2 %collective-permute-done = f32[960,256]{1,0:T(8,128)} collective-permute-done((f32[960,256]{1,0:T(8,128)}, f32[960,256]{1,0:T(8,128)}, u32[]{:S(2)}, u32[]{:S(2)}) %collective-permute-start) | collective-permute-done | bytes 983072 | tf_op jit(solution)/shard_map/ppermute | solution.py:18
  65.5 0.0 collective-permute-start.5
  65.5 41.8 %collective-permute-done.1 = f32[960,256]{1,0:T(8,128)} collective-permute-done((f32[960,256]{1,0:T(8,128)}, f32[960,256]{1,0:T(8,128)}, u32[]{:S(2)}, u32[]{:S(2)}) %collective-permute-start.1) | collective-permute-done | bytes 983072 | tf_op jit(solution)/shard_map/ppermute | solution.py:18
  107.3 0.7 collective-permute-start.6
  108.0 4.1 %broadcast_in_dim.3 = f32[960,2048]{1,0:T(8,128)} broadcast(f32[]{:T(128)} %constant.41.clone.1), dimensions={} | broadcast | bytes 7864324 | tf_op jit(solution)/shard_map/broadcast_in_dim | solution.py:13
  112.1 0.0 copy-done
  112.1 1.1 constant_dynamic-update-slice_fusion.7
  113.2 2.4 constant_dynamic-update-slice_fusion.6
  115.5 2.3 constant_dynamic-update-slice_fusion.5
  117.8 32.0 %collective-permute-done.2 = f32[960,256]{1,0:T(8,128)} collective-permute-done((f32[960,256]{1,0:T(8,128)}, f32[960,256]{1,0:T(8,128)}, u32[]{:S(2)}, u32[]{:S(2)}) %collective-permute-start.2) | collective-permute-done | bytes 983072 | tf_op jit(solution)/shard_map/ppermute | solution.py:18
  149.8 2.3 constant_dynamic-update-slice_fusion.4
  152.1 38.3 %collective-permute-done.3 = f32[960,256]{1,0:T(8,128)} collective-permute-done((f32[960,256]{1,0:T(8,128)}, f32[960,256]{1,0:T(8,128)}, u32[]{:S(2)}, u32[]{:S(2)}) %collective-permute-start.3) | collective-permute-done | bytes 983072 | tf_op jit(solution)/shard_map/ppermute | solution.py:18
  190.4 2.4 constant_dynamic-update-slice_fusion.3
  192.8 0.0 collective-permute-done.4
  192.8 1.1 constant_dynamic-update-slice_fusion.2
  193.9 0.0 collective-permute-done.5
  193.9 1.1 constant_dynamic-update-slice_fusion.1
  195.0 0.0 collective-permute-done.6
  195.0 1.2 constant_dynamic-update-slice_fusion
  196.2 0.0 all-gather.2.cloned.1.call-done
  196.2 30.9 %multiply_bitcast_fusion = f32[1800,960]{0,1:T(8,128)} fusion(f32[960,2048]{1,0:T(8,128)} %constant_dynamic-update-slice_fusion, f32[1800,2048]{0,1:T(8,128)} %all-gather.2.cloned.1.call-done), kind=kOutput, calls=%fused_computation | convolution fusion | flops 21235392512 | bytes 29521920 | tf_op jit(solution)/shard_map/dot_general | solution.py:23
  227.1 8.7 %copy.5 = f32[1800,960]{1,0:T(8,128)} copy(f32[1800,960]{0,1:T(8,128)} %multiply_bitcast_fusion) | data formatting | bytes 13824000 | tf_op jit(solution)/shard_map/mul | solution.py:30
  (1 shorter events, 0.0 us)
Async XLA Ops:
  6.5 105.6 %copy-start = (f32[256,960]{0,1:T(8,128)S(1)}, f32[256,960]{0,1:T(8,128)}, u32[]{:S(2)}) copy-start(f32[256,960]{0,1:T(8,128)} %param.3) | copy-start | bytes 2949124
  6.5 189.6 %all-gather.2.cloned.1.call-start = ((), (), s32[]{:S(2)}) async-start(), calls=%async_computation.1 | async-start | bytes 16711680 | tf_op jit(solution)/shard_map/all_gather | solution.py:22
  32.1 33.4 %collective-permute-start = (f32[960,256]{1,0:T(8,128)}, f32[960,256]{1,0:T(8,128)}, u32[]{:S(2)}, u32[]{:S(2)}) collective-permute-start(f32[960,256]{1,0:T(8,128)} %bitcast.12), channel_id=1, source_target_pairs={{0,64},{16,80},{32,96},{48,112},{64,0},{80,16},{96,32},{112,48},{1... | collective-permute-start | bytes 2949128 | tf_op jit(solution)/shard_map/ppermute | solution.py:18
  33.2 74.1 %collective-permute-start.1 = (f32[960,256]{1,0:T(8,128)}, f32[960,256]{1,0:T(8,128)}, u32[]{:S(2)}, u32[]{:S(2)}) collective-permute-start(f32[960,256]{1,0:T(8,128)} %bitcast.13), channel_id=1, source_target_pairs={{0,80},{16,96},{32,112},{48,64},{64,16},{80,32},{96,48},{112,0},{1... | collective-permute-start | bytes 2949128 | tf_op jit(solution)/shard_map/ppermute | solution.py:18
  34.9 114.9 %collective-permute-start.2 = (f32[960,256]{1,0:T(8,128)}, f32[960,256]{1,0:T(8,128)}, u32[]{:S(2)}, u32[]{:S(2)}) collective-permute-start(f32[960,256]{1,0:T(8,128)} %bitcast.14), channel_id=1, source_target_pairs={{0,96},{16,112},{32,64},{48,80},{64,32},{80,48},{96,0},{112,16},{1... | collective-permute-start | bytes 2949128 | tf_op jit(solution)/shard_map/ppermute | solution.py:18
  37.9 152.5 %collective-permute-start.3 = (f32[960,256]{1,0:T(8,128)}, f32[960,256]{1,0:T(8,128)}, u32[]{:S(2)}, u32[]{:S(2)}) collective-permute-start(f32[960,256]{1,0:T(8,128)} %bitcast.15), channel_id=1, source_target_pairs={{0,112},{16,64},{32,80},{48,96},{64,48},{80,0},{96,16},{112,32},{1... | collective-permute-start | bytes 2949128 | tf_op jit(solution)/shard_map/ppermute | solution.py:18
  40.4 152.4 %collective-permute-start.4 = (f32[960,256]{1,0:T(8,128)}, f32[960,256]{1,0:T(8,128)S(1)}, u32[]{:S(2)}, u32[]{:S(2)}) collective-permute-start(f32[960,256]{1,0:T(8,128)} %bitcast.16), channel_id=1, source_target_pairs={{0,32},{16,48},{32,0},{48,16},{64,96},{80,112},{96,64},{112,80},{1... | collective-permute-start | bytes 2949128 | tf_op jit(solution)/shard_map/ppermute | solution.py:18
  65.5 128.5 %collective-permute-start.5 = (f32[960,256]{1,0:T(8,128)}, f32[960,256]{1,0:T(8,128)S(1)}, u32[]{:S(2)}, u32[]{:S(2)}) collective-permute-start(f32[960,256]{1,0:T(8,128)} %bitcast.17), channel_id=1, source_target_pairs={{0,16},{16,32},{32,48},{48,0},{64,80},{80,96},{96,112},{112,64},{1... | collective-permute-start | bytes 2949128 | tf_op jit(solution)/shard_map/ppermute | solution.py:18
  107.3 87.7 %collective-permute-start.6 = (f32[960,256]{1,0:T(8,128)}, f32[960,256]{1,0:T(8,128)S(1)}, u32[]{:S(2)}, u32[]{:S(2)}) collective-permute-start(f32[960,256]{1,0:T(8,128)} %bitcast.18), channel_id=1, source_target_pairs={{0,48},{16,0},{32,16},{48,32},{64,112},{80,64},{96,80},{112,96},{1... | collective-permute-start | bytes 2949128 | tf_op jit(solution)/shard_map/ppermute | solution.py:18
Sparse Core Ops, SparseCore 0:
  32.2 159.8 all-gather.1

commit v6 on v5

--- a/solution.py
+++ b/solution.py
@@ -4,21 +4,33 @@
 from jax.sharding import PartitionSpec as P
 
 
+def _offsets(ng):
+    nz = ng // 2
+    offsets = [(1, dz) for dz in range(nz)] + [(0, dz) for dz in range(nz // 2, 0, -1)]
+    return nz, offsets + [(0, dz) for dz in range(nz // 2 + 1, nz)]
+
+
 def per_device(ng, amplitudes, integrals):
     g = lax.axis_index("ga")
     bk, nb = integrals.shape
-    nz = ng // 2
+    nz, offsets = _offsets(ng)
     yh, z = g // nz, lax.rem(g, nz)
+    pieces = amplitudes.reshape(ng, -1, amplitudes.shape[1])
+    stack = lax.dynamic_update_slice(jnp.zeros_like(pieces), pieces[g][None], (g, 0, 0))
+    for dy, dz in offsets:
+        pairs = [(i, ((i // nz + dy) % 2) * nz + (i % nz + dz) % nz) for i in range(ng)]
+        dst = lax.rem(yh + dy, 2) * nz + lax.rem(z + dz, nz)
+        got = lax.ppermute(pieces[dst], "ga", pairs)
+        src = lax.rem(yh + dy, 2) * nz + lax.rem(z - dz + nz, nz)
+        stack = lax.dynamic_update_slice(stack, got[None], (src, 0, 0))
+    regrouped = stack.transpose(1, 0, 2).reshape(stack.shape[1], -1)
     bt = integrals.T
     full_bt = lax.dynamic_update_slice(jnp.zeros((nb, bk * ng), jnp.float32), bt, (0, g * bk))
-    offsets = [(1, dz) for dz in range(nz)] + [(0, dz) for dz in range(nz // 2, 0, -1)]
-    offsets += [(0, dz) for dz in range(nz // 2 + 1, nz)]
     for dy, dz in offsets:
         pairs = [(i, ((i // nz + dy) % 2) * nz + (i % nz + dz) % nz) for i in range(ng)]
         got = lax.ppermute(bt, "ga", pairs)
         src = lax.rem(yh + dy, 2) * nz + lax.rem(z - dz + nz, nz)
         full_bt = lax.dynamic_update_slice(full_bt, got, (0, src * bk))
-    regrouped = lax.all_to_all(amplitudes, "ga", split_axis=0, concat_axis=1, tiled=True)
     full_rows = lax.all_gather(regrouped, "ka", axis=1, tiled=True)
     ladder = lax.dot_general(
         full_rows,

time: 246 us -> 265 us (1.077); the launches traced: 243 us -> 264 us
  matrix products: 30.9 us -> 56.3 us
  blocking collectives: 23.5 us -> 0 us
  starting transfers between devices: 10.9 us -> 28.3 us
  waiting for transfers between devices: 135 us -> 144 us
  local copies, waits for them, and re-layouts: 28.7 us -> 22 us
    dot_general x1, matrix products: 30.9 us -> 56.3 us  [per_device(): lax.dot_general(full_rows, full_bt, (((1,), (1,)), ((), ())), precision=l...]
    all_to_all x1 -> x0, blocking collectives: 23.5 us -> none  [per_device(): lax.all_to_all(amplitudes, 'ga', split_axis=0, concat_axis=1, tiled=True)]
    ppermute x0 -> x7, starting transfers between devices: none -> 15.5 us  [per_device(): got = lax.ppermute(pieces[dst], 'ga', pairs)]
    mul x1 -> x0, local copies, waits for them, and re-layouts: 8.71 us -> none  [per_device(): return 0.5 * ladder]
    ppermute x0 -> x7, waiting for transfers between devices: none -> 6.55 us  [per_device(): got = lax.ppermute(pieces[dst], 'ga', pairs)]
  transfers between devices with their start and end apart: 8 -> 15, of which waited for: 4 -> 8; matrix products, arithmetic and copies ran while one was open for 7% -> 7% of each run, Pallas kernels for 0% -> 0%
where the time goes in v6:
time: 265 us; the launch traced here: 264 us
  waiting for transfers between devices  144 us (54%)
  matrix products  56.3 us (21%)
  starting transfers between devices  28.3 us (11%)
  local copies, waits for them, and re-layouts  22 us (8%)
  between operations  13.6 us (5%)
    ppermute x7, waiting for transfers between devices, per_device(): got = lax.ppermute(bt, 'ga', pairs)  138 us
    dot_general x1, matrix products, per_device(): lax.dot_general(full_rows, full_bt, (((1,), (1,)), ((), ())), precision=l...  56.3 us
    ppermute x7, starting transfers between devices, per_device(): got = lax.ppermute(pieces[dst], 'ga', pairs)  15.5 us
    ppermute x7, starting transfers between devices, per_device(): got = lax.ppermute(bt, 'ga', pairs)  12.8 us
    dynamic_update_slice x7, local copies, waits for them, and re-layouts, per_device(): full_bt = lax.dynamic_update_slice(full_bt, got, (0, src * bk))  11.5 us
    ppermute x7, waiting for transfers between devices, per_device(): got = lax.ppermute(pieces[dst], 'ga', pairs)  6.55 us
  transfers between devices with their start and end apart: 15, of which 8 were waited for; matrix products, arithmetic and copies ran while one was open for 7% of the time, Pallas kernels for 0%

profile of v6, /device:TPU:1, one launch (start us, length us, event | category | flops | bytes accessed | tf_op | source)
XLA Modules:
  0.0 264.5 jit_solution(13182497846894764827)
XLA Ops:
  6.5 1.9 reshape.6
  8.5 0.7 constant_dynamic-slice_fusion
  9.2 3.8 %collective-permute-start = (f32[1800,16]{0,1:T(8,128)S(1)}, f32[1800,16]{0,1:T(8,128)S(1)}, u32[]{:S(2)}, u32[]{:S(2)}) collective-permute-start(f32[1800,16]{0,1:T(8,128)S(1)} %bitcast.56), channel_id=1, source_target_pairs={{0,64},{16,80},{32,96},{48,112},{64,0},{80,16},{96,32},{112,48},{1... | collective-permute-start | bytes 345608 | tf_op jit(solution)/shard_map/ppermute | solution.py:23
  13.0 1.5 collective-permute-start.1
  14.5 6.0 %collective-permute-start.2 = (f32[1800,16]{0,1:T(8,128)S(1)}, f32[1800,16]{0,1:T(8,128)S(1)}, u32[]{:S(2)}, u32[]{:S(2)}) collective-permute-start(f32[1800,16]{0,1:T(8,128)S(1)} %bitcast.54), channel_id=1, source_target_pairs={{0,96},{16,112},{32,64},{48,80},{64,32},{80,48},{96,0},{112,16},{1... | collective-permute-start | bytes 345608 | tf_op jit(solution)/shard_map/ppermute | solution.py:23
  21.1 0.8 collective-permute-start.4
  22.9 2.6 collective-permute-start.6
  25.6 1.5 collective-permute-done.3
  27.0 1.4 collective-permute-done.4
  28.4 3.3 %collective-permute-done.5 = f32[1800,16]{0,1:T(8,128)S(1)} collective-permute-done((f32[1800,16]{0,1:T(8,128)}, f32[1800,16]{0,1:T(8,128)S(1)}, u32[]{:S(2)}, u32[]{:S(2)}) %collective-permute-start.5) | collective-permute-done | bytes 115232 | tf_op jit(solution)/shard_map/ppermute | solution.py:23
  32.2 0.9 copy-done
  33.1 3.0 %collective-permute-start.7 = (f32[960,256]{1,0:T(8,128)S(1)}, f32[960,256]{1,0:T(8,128)S(1)}, u32[]{:S(2)}, u32[]{:S(2)}) collective-permute-start(f32[960,256]{1,0:T(8,128)S(1)} %bitcast.45), channel_id=1, source_target_pairs={{0,64},{16,80},{32,96},{48,112},{64,0},{80,16},{96,32},{112,48},{1... | collective-permute-start | bytes 2949128 | tf_op jit(solution)/shard_map/ppermute | solution.py:31
  36.2 1.4 collective-permute-start.8
  37.6 4.5 %collective-permute-start.9 = (f32[960,256]{1,0:T(8,128)S(1)}, f32[960,256]{1,0:T(8,128)}, u32[]{:S(2)}, u32[]{:S(2)}) collective-permute-start(f32[960,256]{1,0:T(8,128)S(1)} %bitcast.47), channel_id=1, source_target_pairs={{0,96},{16,112},{32,64},{48,80},{64,32},{80,48},{96,0},{112,16},{1... | collective-permute-start | bytes 2949128 | tf_op jit(solution)/shard_map/ppermute | solution.py:31
  42.1 1.0 collective-permute-start.10
  43.4 26.7 %collective-permute-done.7 = f32[960,256]{1,0:T(8,128)S(1)} collective-permute-done((f32[960,256]{1,0:T(8,128)S(1)}, f32[960,256]{1,0:T(8,128)S(1)}, u32[]{:S(2)}, u32[]{:S(2)}) %collective-permute-start.7) | collective-permute-done | bytes 983072 | tf_op jit(solution)/shard_map/ppermute | solution.py:31
  70.1 1.0 copy-done.2
  71.1 1.5 collective-permute-start.12
  72.5 40.4 %collective-permute-done.8 = f32[960,256]{1,0:T(8,128)} collective-permute-done((f32[960,256]{1,0:T(8,128)S(1)}, f32[960,256]{1,0:T(8,128)}, u32[]{:S(2)}, u32[]{:S(2)}) %collective-permute-start.8) | collective-permute-done | bytes 983072 | tf_op jit(solution)/shard_map/ppermute | solution.py:31
  112.9 1.1 collective-permute-start.13
  114.0 4.1 %broadcast_in_dim.35 = f32[960,2048]{1,0:T(8,128)} broadcast(f32[]{:T(128)} %constant.51.clone.1), dimensions={} | broadcast | bytes 7864324 | tf_op jit(solution)/shard_map/broadcast_in_dim | solution.py:28
  118.2 1.1 constant_dynamic-update-slice_fusion.7
  119.2 1.1 constant_dynamic-update-slice_fusion.6
  120.3 2.3 constant_dynamic-update-slice_fusion.5
  122.7 31.9 %collective-permute-done.9 = f32[960,256]{1,0:T(8,128)} collective-permute-done((f32[960,256]{1,0:T(8,128)S(1)}, f32[960,256]{1,0:T(8,128)}, u32[]{:S(2)}, u32[]{:S(2)}) %collective-permute-start.9) | collective-permute-done | bytes 983072 | tf_op jit(solution)/shard_map/ppermute | solution.py:31
  154.6 2.4 constant_dynamic-update-slice_fusion.4
  157.0 38.7 %collective-permute-done.10 = f32[960,256]{1,0:T(8,128)} collective-permute-done((f32[960,256]{1,0:T(8,128)S(1)}, f32[960,256]{1,0:T(8,128)}, u32[]{:S(2)}, u32[]{:S(2)}) %collective-permute-start.10) | collective-permute-done | bytes 983072 | tf_op jit(solution)/shard_map/ppermute | solution.py:31
  195.7 2.3 constant_dynamic-update-slice_fusion.3
  198.0 1.1 constant_dynamic-update-slice_fusion.2
  199.1 1.2 constant_dynamic-update-slice_fusion.1
  200.2 1.1 constant_dynamic-update-slice_fusion
  201.3 56.3 %convolution_multiply_fusion = f32[1800,960]{1,0:T(8,128)} fusion(f32[1800,2048]{0,1:T(8,128)} %all-gather.2.cloned.1.call-done, f32[960,2048]{1,0:T(8,128)} %constant_dynamic-update-slice_fusion), kind=kOutput, calls=%fused_computation | convolution fusion | flops 21235392512 | bytes 29521920 | tf_op jit(solution)/shard_map/dot_general | solution.py:35
  (35 shorter events, 2.3 us)
Async XLA Ops:
  6.5 26.6 %copy-start.1 = (f32[256,960]{0,1:T(8,128)S(1)}, f32[256,960]{0,1:T(8,128)}, u32[]{:S(2)}) copy-start(f32[256,960]{0,1:T(8,128)} %param.3) | copy-start | bytes 2949124
  6.5 194.8 %all-gather.2.cloned.1.call-start = ((), (), s32[]{:S(2)}) async-start(), calls=%async_computation | async-start | bytes 16711680 | tf_op jit(solution)/shard_map/all_gather | solution.py:34
  9.2 13.5 %collective-permute-start = (f32[1800,16]{0,1:T(8,128)S(1)}, f32[1800,16]{0,1:T(8,128)S(1)}, u32[]{:S(2)}, u32[]{:S(2)}) collective-permute-start(f32[1800,16]{0,1:T(8,128)S(1)} %bitcast.56), channel_id=1, source_target_pairs={{0,64},{16,80},{32,96},{48,112},{64,0},{80,16},{96,32},{112,48},{1... | collective-permute-start | bytes 345608 | tf_op jit(solution)/shard_map/ppermute | solution.py:23
  13.0 9.9 %collective-permute-start.1 = (f32[1800,16]{0,1:T(8,128)S(1)}, f32[1800,16]{0,1:T(8,128)S(1)}, u32[]{:S(2)}, u32[]{:S(2)}) collective-permute-start(f32[1800,16]{0,1:T(8,128)S(1)} %bitcast.55), channel_id=1, source_target_pairs={{0,80},{16,96},{32,112},{48,64},{64,16},{80,32},{96,48},{112,0},{1... | collective-permute-start | bytes 345608 | tf_op jit(solution)/shard_map/ppermute | solution.py:23
  14.5 11.0 %collective-permute-start.2 = (f32[1800,16]{0,1:T(8,128)S(1)}, f32[1800,16]{0,1:T(8,128)S(1)}, u32[]{:S(2)}, u32[]{:S(2)}) collective-permute-start(f32[1800,16]{0,1:T(8,128)S(1)} %bitcast.54), channel_id=1, source_target_pairs={{0,96},{16,112},{32,64},{48,80},{64,32},{80,48},{96,0},{112,16},{1... | collective-permute-start | bytes 345608 | tf_op jit(solution)/shard_map/ppermute | solution.py:23
  20.5 6.5 %collective-permute-start.3 = (f32[1800,16]{0,1:T(8,128)S(1)}, f32[1800,16]{0,1:T(8,128)S(1)}, u32[]{:S(2)}, u32[]{:S(2)}) collective-permute-start(f32[1800,16]{0,1:T(8,128)S(1)} %bitcast.53), channel_id=1, source_target_pairs={{0,112},{16,64},{32,80},{48,96},{64,48},{80,0},{96,16},{112,32},{1... | collective-permute-start | bytes 345608 | tf_op jit(solution)/shard_map/ppermute | solution.py:23
  21.1 7.3 %collective-permute-start.4 = (f32[1800,16]{0,1:T(8,128)S(1)}, f32[1800,16]{0,1:T(8,128)S(1)}, u32[]{:S(2)}, u32[]{:S(2)}) collective-permute-start(f32[1800,16]{0,1:T(8,128)S(1)} %bitcast.52), channel_id=1, source_target_pairs={{0,32},{16,48},{32,0},{48,16},{64,96},{80,112},{96,64},{112,80},{1... | collective-permute-start | bytes 345608 | tf_op jit(solution)/shard_map/ppermute | solution.py:23
  22.7 9.1 %collective-permute-start.5 = (f32[1800,16]{0,1:T(8,128)}, f32[1800,16]{0,1:T(8,128)S(1)}, u32[]{:S(2)}, u32[]{:S(2)}) collective-permute-start(f32[1800,16]{0,1:T(8,128)} %bitcast.58), channel_id=1, source_target_pairs={{0,16},{16,32},{32,48},{48,0},{64,80},{80,96},{96,112},{112,64},{1... | collective-permute-start | bytes 345608 | tf_op jit(solution)/shard_map/ppermute | solution.py:23
  22.9 9.3 %collective-permute-start.6 = (f32[1800,16]{0,1:T(8,128)S(1)}, f32[1800,16]{0,1:T(8,128)S(1)}, u32[]{:S(2)}, u32[]{:S(2)}) collective-permute-start(f32[1800,16]{0,1:T(8,128)S(1)} %bitcast.57), channel_id=1, source_target_pairs={{0,48},{16,0},{32,16},{48,32},{64,112},{80,64},{96,80},{112,96},{1... | collective-permute-start | bytes 345608 | tf_op jit(solution)/shard_map/ppermute | solution.py:23
  32.2 0.9 copy-start
  33.1 36.9 %collective-permute-start.7 = (f32[960,256]{1,0:T(8,128)S(1)}, f32[960,256]{1,0:T(8,128)S(1)}, u32[]{:S(2)}, u32[]{:S(2)}) collective-permute-start(f32[960,256]{1,0:T(8,128)S(1)} %bitcast.45), channel_id=1, source_target_pairs={{0,64},{16,80},{32,96},{48,112},{64,0},{80,16},{96,32},{112,48},{1... | collective-permute-start | bytes 2949128 | tf_op jit(solution)/shard_map/ppermute | solution.py:31
  36.2 76.8 %collective-permute-start.8 = (f32[960,256]{1,0:T(8,128)S(1)}, f32[960,256]{1,0:T(8,128)}, u32[]{:S(2)}, u32[]{:S(2)}) collective-permute-start(f32[960,256]{1,0:T(8,128)S(1)} %bitcast.46), channel_id=1, source_target_pairs={{0,80},{16,96},{32,112},{48,64},{64,16},{80,32},{96,48},{112,0},{1... | collective-permute-start | bytes 2949128 | tf_op jit(solution)/shard_map/ppermute | solution.py:31
  37.6 117.0 %collective-permute-start.9 = (f32[960,256]{1,0:T(8,128)S(1)}, f32[960,256]{1,0:T(8,128)}, u32[]{:S(2)}, u32[]{:S(2)}) collective-permute-start(f32[960,256]{1,0:T(8,128)S(1)} %bitcast.47), channel_id=1, source_target_pairs={{0,96},{16,112},{32,64},{48,80},{64,32},{80,48},{96,0},{112,16},{1... | collective-permute-start | bytes 2949128 | tf_op jit(solution)/shard_map/ppermute | solution.py:31
  42.1 153.6 %collective-permute-start.10 = (f32[960,256]{1,0:T(8,128)S(1)}, f32[960,256]{1,0:T(8,128)}, u32[]{:S(2)}, u32[]{:S(2)}) collective-permute-start(f32[960,256]{1,0:T(8,128)S(1)} %bitcast.48), channel_id=1, source_target_pairs={{0,112},{16,64},{32,80},{48,96},{64,48},{80,0},{96,16},{112,32},{1... | collective-permute-start | bytes 2949128 | tf_op jit(solution)/shard_map/ppermute | solution.py:31
  43.1 154.8 %collective-permute-start.11 = (f32[960,256]{1,0:T(8,128)S(1)}, f32[960,256]{1,0:T(8,128)S(1)}, u32[]{:S(2)}, u32[]{:S(2)}) collective-permute-start(f32[960,256]{1,0:T(8,128)S(1)} %bitcast.49), channel_id=1, source_target_pairs={{0,32},{16,48},{32,0},{48,16},{64,96},{80,112},{96,64},{112,80},{1... | collective-permute-start | bytes 2949128 | tf_op jit(solution)/shard_map/ppermute | solution.py:31
  70.1 1.0 copy-start.2
  71.1 128.0 %collective-permute-start.12 = (f32[960,256]{1,0:T(8,128)S(1)}, f32[960,256]{1,0:T(8,128)S(1)}, u32[]{:S(2)}, u32[]{:S(2)}) collective-permute-start(f32[960,256]{1,0:T(8,128)S(1)} %bitcast.50), channel_id=1, source_target_pairs={{0,16},{16,32},{32,48},{48,0},{64,80},{80,96},{96,112},{112,64},{1... | collective-permute-start | bytes 2949128 | tf_op jit(solution)/shard_map/ppermute | solution.py:31
  72.5 46.7 %copy-start.3 = (f32[960,256]{1,0:T(8,128)S(1)}, f32[960,256]{1,0:T(8,128)}, u32[]{:S(2)}) copy-start(f32[960,256]{1,0:T(8,128)} %copy-done.2) | copy-start | bytes 2949124
  112.9 87.3 %collective-permute-start.13 = (f32[960,256]{1,0:T(8,128)S(1)}, f32[960,256]{1,0:T(8,128)S(1)}, u32[]{:S(2)}, u32[]{:S(2)}) collective-permute-start(f32[960,256]{1,0:T(8,128)S(1)} %bitcast.51), channel_id=1, source_target_pairs={{0,48},{16,0},{32,16},{48,32},{64,112},{80,64},{96,80},{112,96},{1... | collective-permute-start | bytes 2949128 | tf_op jit(solution)/shard_map/ppermute | solution.py:31
Sparse Core Ops, SparseCore 0:
  33.3 161.8 all-gather.1

commit v7 on v6

v7 whole, which is shorter than its diff:
```python
import jax
import jax.numpy as jnp
from jax import lax
from jax.sharding import Mesh
from jax.sharding import PartitionSpec as P


def _offsets(ng):
    nz = ng // 2
    offsets = [(1, dz) for dz in range(nz)] + [(0, dz) for dz in range(nz // 2, 0, -1)]
    return nz, offsets + [(0, dz) for dz in range(nz // 2 + 1, nz)]


def per_device(ng, nxc, amplitudes, integrals):
    g = lax.axis_index("ga")
    ylo = lax.axis_index("ylo")
    bk, nb = integrals.shape
    nz, offsets = _offsets(ng)
    yh, z = g // nz, lax.rem(g, nz)
    regrouped = lax.all_to_all(amplitudes, "ga", split_axis=0, concat_axis=1, tiled=True)
    kw = regrouped.shape[1]
    other = lax.ppermute(regrouped, "ylo", [(0, 1), (1, 0)])
    pair = jnp.zeros((regrouped.shape[0], 2 * kw), jnp.float32)
    pair = lax.dynamic_update_slice(pair, regrouped, (0, ylo * kw))
    pair = lax.dynamic_update_slice(pair, other, (0, (1 - ylo) * kw))
    full_rows = lax.all_gather(pair, "xc", axis=1, tiled=True)

    bt = integrals.T
    full_bt = jnp.zeros((nb, bk * ng), jnp.float32)
    per = bk // kw

    def place(full_bt, blk, src):
        for h in range(per):
            kb = src * per + h
            pos = lax.rem(kb, nxc) * 2 + kb // nxc
            full_bt = lax.dynamic_update_slice(full_bt, blk[:, h * kw:(h + 1) * kw], (0, pos * kw))
        return full_bt

    full_bt = place(full_bt, bt, g)
    for dy, dz in offsets:
        pairs = [(i, ((i // nz + dy) % 2) * nz + (i % nz + dz) % nz) for i in range(ng)]
        got = lax.ppermute(bt, "ga", pairs)
        src = lax.rem(yh + dy, 2) * nz + lax.rem(z - dz + nz, nz)
        full_bt = place(full_bt, got, src)
    ladder = lax.dot_general(
        full_rows,
        full_bt,
        (((1,), (1,)), ((), ())),
        precision=lax.Precision.HIGH,
        preferred_element_type=jnp.float32,
    )
    return 0.5 * ladder


def solution(mesh):
    ng = mesh.shape["ga"]
    nk = mesh.shape["ka"]
    fine = Mesh(mesh.devices.reshape(ng, 2, nk // 2), ("ga", "ylo", "xc"))
    placed = (P(None, ("ylo", "xc", "ga")), P("ga", ("ylo", "xc")))
    return jax.shard_map(
        lambda a, b: per_device(ng, nk // 2, a, b), mesh=fine, in_specs=placed,
        out_specs=P("ga", ("ylo", "xc")), check_vma=False
    )
```

time: 265 us -> 229 us (0.86)
  waiting for transfers between devices: 144 us -> 90.9 us
  blocking collectives: 0 us -> 23.4 us
  starting transfers between devices: 28.3 us -> 11.3 us
  local copies, waits for them, and re-layouts: 22 us -> 31.8 us
    ppermute x7, waiting for transfers between devices: 138 us -> 71.7 us  [per_device(): got = lax.ppermute(bt, 'ga', pairs)]
    all_to_all x0 -> x1, blocking collectives: none -> 23.4 us  [per_device(): lax.all_to_all(amplitudes, 'ga', split_axis=0, concat_axis=1, tiled=True)]
    ppermute x7 -> x1, starting transfers between devices: 15.5 us -> 0.43 us  [per_device(): other = lax.ppermute(regrouped, 'ylo', [(0, 1), (1, 0)])]
    ppermute x7 -> x1, waiting for transfers between devices: 6.55 us -> 19.2 us  [per_device(): other = lax.ppermute(regrouped, 'ylo', [(0, 1), (1, 0)])]
    dynamic_update_slice x16 -> x18, local copies, waits for them, and re-layouts: 12.7 us -> 20.4 us  [the longest x16 20.3 us: place(): lax.dynamic_update_slice(full_bt, blk[:, h * kw:(h + 1) * kw], (0, pos *...]
    all_to_all x0 -> x3, local copies, waits for them, and re-layouts: none -> 3.2 us  [per_device(): lax.all_to_all(amplitudes, 'ga', split_axis=0, concat_axis=1, tiled=True)]
  transfers between devices with their start and end apart: 15 -> 9, of which waited for: 8 -> 7; matrix products, arithmetic and copies ran while one was open for 7% -> 11% of each run, Pallas kernels for 0% -> 0%
where the time goes in v7:
time: 229 us; the launch traced here: 227 us
  waiting for transfers between devices  90.9 us (40%)
  matrix products  56.3 us (25%)
  local copies, waits for them, and re-layouts  31.8 us (14%)
  blocking collectives  23.4 us (10%)
  between operations  13.5 us (6%)
  starting transfers between devices  11.3 us (5%)
    ppermute x7, waiting for transfers between devices, per_device(): got = lax.ppermute(bt, 'ga', pairs)  71.7 us
    dot_general x1, matrix products, per_device(): lax.dot_general(full_rows, full_bt, (((1,), (1,)), ((), ())), precision=l...  56.3 us
    all_to_all x1, blocking collectives, per_device(): lax.all_to_all(amplitudes, 'ga', split_axis=0, concat_axis=1, tiled=True)  23.4 us
    dynamic_update_slice x16, local copies, waits for them, and re-layouts, place(): lax.dynamic_update_slice(full_bt, blk[:, h * kw:(h + 1) * kw], (0, pos *...  20.3 us
    ppermute x1, waiting for transfers between devices, per_device(): other = lax.ppermute(regrouped, 'ylo', [(0, 1), (1, 0)])  19.2 us
    ppermute x7, starting transfers between devices, per_device(): got = lax.ppermute(bt, 'ga', pairs)  10.8 us
    broadcast_in_dim x1, local copies, waits for them, and re-layouts, per_device(): full_bt = jnp.zeros((nb, bk * ng), jnp.float32)  5.28 us
  transfers between devices with their start and end apart: 9, of which 7 were waited for; matrix products, arithmetic and copies ran while one was open for 11% of the time, Pallas kernels for 0%

profile of v7, /device:TPU:1, one launch (start us, length us, event | category | flops | bytes accessed | tf_op | source)
XLA Modules:
  0.0 227.1 jit_solution(5873535339013233857)
XLA Ops:
  6.5 1.8 all_to_all.14
  8.5 23.4 %all_to_all.19 = f32[8,1800,16]{1,2,0:T(8,128)S(1)} all-to-all(f32[8,1800,16]{1,2,0:T(8,128)S(1)} %copy.4), channel_id=1, replica_groups=mesh['ga'=8,'ylo'=2,'xc'=8] {'ga'}, dimensions={0} | all-to-all | bytes 1843200 | tf_op jit(solution)/shard_map/all_to_all | solution.py:20
  31.9 1.2 copy.5
  33.8 19.2 %collective-permute-done = f32[1800,128]{1,0:T(8,128)} collective-permute-done((f32[1800,128]{1,0:T(8,128)}, f32[1800,128]{1,0:T(8,128)}, u32[]{:S(2)}, u32[]{:S(2)}) %collective-permute-start) | collective-permute-done | bytes 921632 | tf_op jit(solution)/shard_map/ppermute | solution.py:22
  53.0 1.5 copy.6
  54.6 1.2 copy-done
  55.9 1.8 collective-permute-start.1
  57.6 1.0 collective-permute-start.2
  58.7 3.7 %collective-permute-start.3 = (f32[960,256]{1,0:T(8,128)}, f32[960,256]{1,0:T(8,128)}, u32[]{:S(2)}, u32[]{:S(2)}) collective-permute-start(f32[960,256]{1,0:T(8,128)} %bitcast.12), channel_id=1, source_target_pairs={{0,96},{16,112},{32,64},{48,80},{64,32},{80,48},{96,0},{112,16},{1... | collective-permute-start | bytes 2949128 | tf_op jit(solution)/shard_map/ppermute | solution.py:42
  62.4 2.3 %collective-permute-start.4 = (f32[960,256]{1,0:T(8,128)}, f32[960,256]{1,0:T(8,128)S(1)}, u32[]{:S(2)}, u32[]{:S(2)}) collective-permute-start(f32[960,256]{1,0:T(8,128)} %bitcast.13), channel_id=1, source_target_pairs={{0,112},{16,64},{32,80},{48,96},{64,48},{80,0},{96,16},{112,32},{1... | collective-permute-start | bytes 2949128 | tf_op jit(solution)/shard_map/ppermute | solution.py:42
  64.7 1.3 collective-permute-start.5
  66.1 5.3 %broadcast_in_dim.7 = f32[960,2048]{1,0:T(8,128)} broadcast(f32[]{:T(128)} %constant.160.clone.1), dimensions={} | broadcast | bytes 7864324 | tf_op jit(solution)/shard_map/broadcast_in_dim | solution.py:29
  71.4 0.9 slice_dynamic-update-slice_fusion.15
  72.2 0.9 slice_dynamic-update-slice_fusion.14
  73.1 4.6 %collective-permute-done.1 = f32[960,256]{1,0:T(8,128)} collective-permute-done((f32[960,256]{1,0:T(8,128)}, f32[960,256]{1,0:T(8,128)}, u32[]{:S(2)}, u32[]{:S(2)}) %collective-permute-start.1) | collective-permute-done | bytes 983072 | tf_op jit(solution)/shard_map/ppermute | solution.py:42
  77.7 1.9 slice_dynamic-update-slice_fusion.13
  79.7 1.9 slice_dynamic-update-slice_fusion.12
  81.6 18.8 %collective-permute-done.2 = f32[960,256]{1,0:T(8,128)} collective-permute-done((f32[960,256]{1,0:T(8,128)}, f32[960,256]{1,0:T(8,128)}, u32[]{:S(2)}, u32[]{:S(2)}) %collective-permute-start.2) | collective-permute-done | bytes 983072 | tf_op jit(solution)/shard_map/ppermute | solution.py:42
  100.9 1.9 slice_dynamic-update-slice_fusion.11
  102.8 1.9 slice_dynamic-update-slice_fusion.10
  104.7 17.2 %collective-permute-done.3 = f32[960,256]{1,0:T(8,128)} collective-permute-done((f32[960,256]{1,0:T(8,128)}, f32[960,256]{1,0:T(8,128)}, u32[]{:S(2)}, u32[]{:S(2)}) %collective-permute-start.3) | collective-permute-done | bytes 983072 | tf_op jit(solution)/shard_map/ppermute | solution.py:42
  121.9 2.0 slice_dynamic-update-slice_fusion.9
  123.8 2.0 slice_dynamic-update-slice_fusion.8
  125.8 16.0 %collective-permute-done.4 = f32[960,256]{1,0:T(8,128)S(1)} collective-permute-done((f32[960,256]{1,0:T(8,128)}, f32[960,256]{1,0:T(8,128)S(1)}, u32[]{:S(2)}, u32[]{:S(2)}) %collective-permute-start.4) | collective-permute-done | bytes 983072 | tf_op jit(solution)/shard_map/ppermute | solution.py:42
  143.6 0.9 slice_dynamic-update-slice_fusion.5
  144.5 0.9 slice_dynamic-update-slice_fusion.4
  145.3 8.0 %collective-permute-done.6 = f32[960,256]{1,0:T(8,128)S(1)} collective-permute-done((f32[960,256]{1,0:T(8,128)S(1)}, f32[960,256]{1,0:T(8,128)S(1)}, u32[]{:S(2)}, u32[]{:S(2)}) %collective-permute-start.6) | collective-permute-done | bytes 983072 | tf_op jit(solution)/shard_map/ppermute | solution.py:42
  153.3 0.9 slice_dynamic-update-slice_fusion.3
  155.1 7.2 %collective-permute-done.7 = f32[960,256]{1,0:T(8,128)S(1)} collective-permute-done((f32[960,256]{1,0:T(8,128)S(1)}, f32[960,256]{1,0:T(8,128)S(1)}, u32[]{:S(2)}, u32[]{:S(2)}) %collective-permute-start.7) | collective-permute-done | bytes 983072 | tf_op jit(solution)/shard_map/ppermute | solution.py:42
  162.2 0.9 slice_dynamic-update-slice_fusion.1
  163.1 0.9 slice_dynamic-update-slice_fusion
  164.0 56.3 %convolution_multiply_fusion = f32[1800,960]{1,0:T(8,128)} fusion(f32[1800,2048]{0,1:T(8,128)} %all-gather.2.cloned.1.call-done, f32[960,2048]{1,0:T(8,128)} %slice_dynamic-update-slice_fusion), kind=kOutput, calls=%fused_computation | convolution fusion | flops 21235392512 | bytes 29521920 | tf_op jit(solution)/shard_map/dot_general | solution.py:45
  (17 shorter events, 4.1 us)
Async XLA Ops:
  6.5 157.5 %all-gather.2.cloned.1.call-start = ((), (), s32[]{:S(2)}) async-start(), calls=%async_computation.1 | async-start | bytes 17694720 | tf_op jit(solution)/shard_map/all_gather | solution.py:26
  33.1 19.9 %collective-permute-start = (f32[1800,128]{1,0:T(8,128)}, f32[1800,128]{1,0:T(8,128)}, u32[]{:S(2)}, u32[]{:S(2)}) collective-permute-start(f32[1800,128]{1,0:T(8,128)} %copy.5), channel_id=1, source_target_pairs={{0,8},{8,0},{1,9},{9,1},{2,10},{10,2},{3,11},{11,3},{4,12},{12,4},... | collective-permute-start | bytes 2764808 | tf_op jit(solution)/shard_map/ppermute | solution.py:22
  54.6 1.3 copy-start
  54.6 16.8 %copy-start.1 = (f32[256,960]{0,1:T(8,128)S(1)}, f32[256,960]{0,1:T(8,128)}, u32[]{:S(2)}) copy-start(f32[256,960]{0,1:T(8,128)} %param.3) | copy-start | bytes 2949124
  55.9 21.8 %collective-permute-start.1 = (f32[960,256]{1,0:T(8,128)}, f32[960,256]{1,0:T(8,128)}, u32[]{:S(2)}, u32[]{:S(2)}) collective-permute-start(f32[960,256]{1,0:T(8,128)} %bitcast.10), channel_id=1, source_target_pairs={{0,64},{16,80},{32,96},{48,112},{64,0},{80,16},{96,32},{112,48},{1... | collective-permute-start | bytes 2949128 | tf_op jit(solution)/shard_map/ppermute | solution.py:42
  57.6 42.7 %collective-permute-start.2 = (f32[960,256]{1,0:T(8,128)}, f32[960,256]{1,0:T(8,128)}, u32[]{:S(2)}, u32[]{:S(2)}) collective-permute-start(f32[960,256]{1,0:T(8,128)} %bitcast.11), channel_id=1, source_target_pairs={{0,80},{16,96},{32,112},{48,64},{64,16},{80,32},{96,48},{112,0},{1... | collective-permute-start | bytes 2949128 | tf_op jit(solution)/shard_map/ppermute | solution.py:42
  58.7 63.2 %collective-permute-start.3 = (f32[960,256]{1,0:T(8,128)}, f32[960,256]{1,0:T(8,128)}, u32[]{:S(2)}, u32[]{:S(2)}) collective-permute-start(f32[960,256]{1,0:T(8,128)} %bitcast.12), channel_id=1, source_target_pairs={{0,96},{16,112},{32,64},{48,80},{64,32},{80,48},{96,0},{112,16},{1... | collective-permute-start | bytes 2949128 | tf_op jit(solution)/shard_map/ppermute | solution.py:42
  62.4 79.4 %collective-permute-start.4 = (f32[960,256]{1,0:T(8,128)}, f32[960,256]{1,0:T(8,128)S(1)}, u32[]{:S(2)}, u32[]{:S(2)}) collective-permute-start(f32[960,256]{1,0:T(8,128)} %bitcast.13), channel_id=1, source_target_pairs={{0,112},{16,64},{32,80},{48,96},{64,48},{80,0},{96,16},{112,32},{1... | collective-permute-start | bytes 2949128 | tf_op jit(solution)/shard_map/ppermute | solution.py:42
  64.7 78.8 %collective-permute-start.5 = (f32[960,256]{1,0:T(8,128)}, f32[960,256]{1,0:T(8,128)S(1)}, u32[]{:S(2)}, u32[]{:S(2)}) collective-permute-start(f32[960,256]{1,0:T(8,128)} %bitcast.14), channel_id=1, source_target_pairs={{0,32},{16,48},{32,0},{48,16},{64,96},{80,112},{96,64},{112,80},{1... | collective-permute-start | bytes 2949128 | tf_op jit(solution)/shard_map/ppermute | solution.py:42
  77.7 75.6 %collective-permute-start.6 = (f32[960,256]{1,0:T(8,128)S(1)}, f32[960,256]{1,0:T(8,128)S(1)}, u32[]{:S(2)}, u32[]{:S(2)}) collective-permute-start(f32[960,256]{1,0:T(8,128)S(1)} %bitcast.17), channel_id=1, source_target_pairs={{0,16},{16,32},{32,48},{48,0},{64,80},{80,96},{96,112},{112,64},{1... | collective-permute-start | bytes 2949128 | tf_op jit(solution)/shard_map/ppermute | solution.py:42
  100.3 61.9 %collective-permute-start.7 = (f32[960,256]{1,0:T(8,128)S(1)}, f32[960,256]{1,0:T(8,128)S(1)}, u32[]{:S(2)}, u32[]{:S(2)}) collective-permute-start(f32[960,256]{1,0:T(8,128)S(1)} %bitcast.18), channel_id=1, source_target_pairs={{0,48},{16,0},{32,16},{48,32},{64,112},{80,64},{96,80},{112,96},{1... | collective-permute-start | bytes 2949128 | tf_op jit(solution)/shard_map/ppermute | solution.py:42
Sparse Core Ops, SparseCore 0:
  56.0 81.4 all-gather.1

commit v8 on v7

--- a/solution.py
+++ b/solution.py
@@ -1,6 +1,7 @@
 import jax
 import jax.numpy as jnp
 from jax import lax
+from jax.experimental.layout import Layout, with_layout_constraint
 from jax.sharding import Mesh
 from jax.sharding import PartitionSpec as P
 
@@ -42,14 +43,15 @@
         got = lax.ppermute(bt, "ga", pairs)
         src = lax.rem(yh + dy, 2) * nz + lax.rem(z - dz + nz, nz)
         full_bt = place(full_bt, got, src)
-    ladder = lax.dot_general(
+    ladder_t = lax.dot_general(
+        full_bt,
         full_rows,
-        full_bt,
         (((1,), (1,)), ((), ())),
         precision=lax.Precision.HIGH,
         preferred_element_type=jnp.float32,
     )
-    return 0.5 * ladder
+    ladder_t = with_layout_constraint(ladder_t, Layout(major_to_minor=(0, 1)))
+    return (0.5 * ladder_t).T
 
 
 def solution(mesh):

time: 229 us -> 212 us (0.926)
  matrix products: 56.3 us -> 30.9 us
  local copies, waits for them, and re-layouts: 31.8 us -> 40.5 us
    dot_general x1, matrix products: 56.3 us -> 30.9 us  [per_device(): lax.dot_general(full_bt, full_rows, (((1,), (1,)), ((), ())), precision=l...]
    transpose x0 -> x1, local copies, waits for them, and re-layouts: none -> 8.71 us  [per_device(): return (0.5 * ladder_t).T]
  transfers between devices with their start and end apart: 9 -> 9, of which waited for: 7 -> 7; matrix products, arithmetic and copies ran while one was open for 11% -> 12% of each run, Pallas kernels for 0% -> 0%
where the time goes in v8:
time: 212 us; the launch traced here: 210 us
  waiting for transfers between devices  90.9 us (43%)
  local copies, waits for them, and re-layouts  40.5 us (19%)
  matrix products  30.9 us (15%)
  blocking collectives  23.4 us (11%)
  between operations  13.5 us (6%)
  starting transfers between devices  11.3 us (5%)
    ppermute x7, waiting for transfers between devices, per_device(): got = lax.ppermute(bt, 'ga', pairs)  71.7 us
    dot_general x1, matrix products, per_device(): lax.dot_general(full_bt, full_rows, (((1,), (1,)), ((), ())), precision=l...  30.9 us
    all_to_all x1, blocking collectives, per_device(): lax.all_to_all(amplitudes, 'ga', split_axis=0, concat_axis=1, tiled=True)  23.4 us
    dynamic_update_slice x16, local copies, waits for them, and re-layouts, place(): lax.dynamic_update_slice(full_bt, blk[:, h * kw:(h + 1) * kw], (0, pos *...  20.3 us
    ppermute x1, waiting for transfers between devices, per_device(): other = lax.ppermute(regrouped, 'ylo', [(0, 1), (1, 0)])  19.2 us
    ppermute x7, starting transfers between devices, per_device(): got = lax.ppermute(bt, 'ga', pairs)  10.8 us
    transpose x1, local copies, waits for them, and re-layouts, per_device(): return (0.5 * ladder_t).T  8.71 us
    broadcast_in_dim x1, local copies, waits for them, and re-layouts, per_device(): full_bt = jnp.zeros((nb, bk * ng), jnp.float32)  5.28 us
  transfers between devices with their start and end apart: 9, of which 7 were waited for; matrix products, arithmetic and copies ran while one was open for 12% of the time, Pallas kernels for 0%

profile of v8, /device:TPU:1, one launch (start us, length us, event | category | flops | bytes accessed | tf_op | source)
XLA Modules:
  0.0 210.5 jit_solution(5896079934689971068)
XLA Ops:
  6.5 1.8 all_to_all.14
  8.5 23.4 %all_to_all.19 = f32[8,1800,16]{1,2,0:T(8,128)S(1)} all-to-all(f32[8,1800,16]{1,2,0:T(8,128)S(1)} %copy.6), channel_id=1, replica_groups=mesh['ga'=8,'ylo'=2,'xc'=8] {'ga'}, dimensions={0} | all-to-all | bytes 1843200 | tf_op jit(solution)/shard_map/all_to_all | solution.py:21
  31.9 1.2 copy.7
  33.8 19.2 %collective-permute-done.7 = f32[1800,128]{1,0:T(8,128)} collective-permute-done((f32[1800,128]{1,0:T(8,128)}, f32[1800,128]{1,0:T(8,128)}, u32[]{:S(2)}, u32[]{:S(2)}) %collective-permute-start.7) | collective-permute-done | bytes 921632 | tf_op jit(solution)/shard_map/ppermute | solution.py:23
  53.0 1.5 copy.8
  54.6 1.2 copy-done
  55.9 1.8 collective-permute-start
  57.6 1.0 collective-permute-start.1
  58.7 3.7 %collective-permute-start.2 = (f32[960,256]{1,0:T(8,128)}, f32[960,256]{1,0:T(8,128)}, u32[]{:S(2)}, u32[]{:S(2)}) collective-permute-start(f32[960,256]{1,0:T(8,128)} %bitcast.14), channel_id=1, source_target_pairs={{0,96},{16,112},{32,64},{48,80},{64,32},{80,48},{96,0},{112,16},{1... | collective-permute-start | bytes 2949128 | tf_op jit(solution)/shard_map/ppermute | solution.py:43
  62.4 2.3 %collective-permute-start.3 = (f32[960,256]{1,0:T(8,128)}, f32[960,256]{1,0:T(8,128)S(1)}, u32[]{:S(2)}, u32[]{:S(2)}) collective-permute-start(f32[960,256]{1,0:T(8,128)} %bitcast.15), channel_id=1, source_target_pairs={{0,112},{16,64},{32,80},{48,96},{64,48},{80,0},{96,16},{112,32},{1... | collective-permute-start | bytes 2949128 | tf_op jit(solution)/shard_map/ppermute | solution.py:43
  64.7 1.3 collective-permute-start.4
  66.1 5.3 %broadcast_in_dim.6 = f32[960,2048]{1,0:T(8,128)} broadcast(f32[]{:T(128)} %constant.160.clone.1), dimensions={} | broadcast | bytes 7864324 | tf_op jit(solution)/shard_map/broadcast_in_dim | solution.py:30
  71.4 0.9 slice_dynamic-update-slice_fusion.15
  72.2 0.9 slice_dynamic-update-slice_fusion.14
  73.1 4.6 %collective-permute-done = f32[960,256]{1,0:T(8,128)} collective-permute-done((f32[960,256]{1,0:T(8,128)}, f32[960,256]{1,0:T(8,128)}, u32[]{:S(2)}, u32[]{:S(2)}) %collective-permute-start) | collective-permute-done | bytes 983072 | tf_op jit(solution)/shard_map/ppermute | solution.py:43
  77.7 1.9 slice_dynamic-update-slice_fusion.13
  79.7 1.9 slice_dynamic-update-slice_fusion.12
  81.6 18.8 %collective-permute-done.1 = f32[960,256]{1,0:T(8,128)} collective-permute-done((f32[960,256]{1,0:T(8,128)}, f32[960,256]{1,0:T(8,128)}, u32[]{:S(2)}, u32[]{:S(2)}) %collective-permute-start.1) | collective-permute-done | bytes 983072 | tf_op jit(solution)/shard_map/ppermute | solution.py:43
  100.9 1.9 slice_dynamic-update-slice_fusion.11
  102.8 1.9 slice_dynamic-update-slice_fusion.10
  104.7 17.2 %collective-permute-done.2 = f32[960,256]{1,0:T(8,128)} collective-permute-done((f32[960,256]{1,0:T(8,128)}, f32[960,256]{1,0:T(8,128)}, u32[]{:S(2)}, u32[]{:S(2)}) %collective-permute-start.2) | collective-permute-done | bytes 983072 | tf_op jit(solution)/shard_map/ppermute | solution.py:43
  121.9 2.0 slice_dynamic-update-slice_fusion.9
  123.8 2.0 slice_dynamic-update-slice_fusion.8
  125.8 16.0 %collective-permute-done.3 = f32[960,256]{1,0:T(8,128)S(1)} collective-permute-done((f32[960,256]{1,0:T(8,128)}, f32[960,256]{1,0:T(8,128)S(1)}, u32[]{:S(2)}, u32[]{:S(2)}) %collective-permute-start.3) | collective-permute-done | bytes 983072 | tf_op jit(solution)/shard_map/ppermute | solution.py:43
  143.6 0.9 slice_dynamic-update-slice_fusion.5
  144.5 0.9 slice_dynamic-update-slice_fusion.4
  145.3 8.0 %collective-permute-done.5 = f32[960,256]{1,0:T(8,128)S(1)} collective-permute-done((f32[960,256]{1,0:T(8,128)S(1)}, f32[960,256]{1,0:T(8,128)S(1)}, u32[]{:S(2)}, u32[]{:S(2)}) %collective-permute-start.5) | collective-permute-done | bytes 983072 | tf_op jit(solution)/shard_map/ppermute | solution.py:43
  153.3 0.9 slice_dynamic-update-slice_fusion.3
  155.1 7.2 %collective-permute-done.6 = f32[960,256]{1,0:T(8,128)S(1)} collective-permute-done((f32[960,256]{1,0:T(8,128)S(1)}, f32[960,256]{1,0:T(8,128)S(1)}, u32[]{:S(2)}, u32[]{:S(2)}) %collective-permute-start.6) | collective-permute-done | bytes 983072 | tf_op jit(solution)/shard_map/ppermute | solution.py:43
  163.1 0.9 slice_dynamic-update-slice_fusion
  164.0 30.9 %multiply_bitcast_fusion = f32[1800,960]{0,1:T(8,128)} fusion(f32[960,2048]{1,0:T(8,128)} %slice_dynamic-update-slice_fusion, f32[1800,2048]{0,1:T(8,128)} %all-gather.2.cloned.1.call-done), kind=kOutput, calls=%fused_computation | convolution fusion | flops 21235392512 | bytes 29521920 | tf_op jit(solution)/shard_map/dot_general | solution.py:46
  194.9 8.7 %copy.9 = f32[1800,960]{1,0:T(8,128)} copy(f32[1800,960]{0,1:T(8,128)} %multiply_bitcast_fusion) | data formatting | bytes 13824000 | tf_op jit(solution)/shard_map/transpose | solution.py:54
  (18 shorter events, 5.0 us)
Async XLA Ops:
  6.5 157.5 %all-gather.2.cloned.1.call-start = ((), (), s32[]{:S(2)}) async-start(), calls=%async_computation.1 | async-start | bytes 17694720 | tf_op jit(solution)/shard_map/all_gather | solution.py:27
  33.1 19.9 %collective-permute-start.7 = (f32[1800,128]{1,0:T(8,128)}, f32[1800,128]{1,0:T(8,128)}, u32[]{:S(2)}, u32[]{:S(2)}) collective-permute-start(f32[1800,128]{1,0:T(8,128)} %copy.7), channel_id=1, source_target_pairs={{0,8},{8,0},{1,9},{9,1},{2,10},{10,2},{3,11},{11,3},{4,12},{12,4},... | collective-permute-start | bytes 2764808 | tf_op jit(solution)/shard_map/ppermute | solution.py:23
  54.6 1.3 copy-start
  54.6 16.8 %copy-start.1 = (f32[256,960]{0,1:T(8,128)S(1)}, f32[256,960]{0,1:T(8,128)}, u32[]{:S(2)}) copy-start(f32[256,960]{0,1:T(8,128)} %param.3) | copy-start | bytes 2949124
  55.9 21.8 %collective-permute-start = (f32[960,256]{1,0:T(8,128)}, f32[960,256]{1,0:T(8,128)}, u32[]{:S(2)}, u32[]{:S(2)}) collective-permute-start(f32[960,256]{1,0:T(8,128)} %bitcast.12), channel_id=1, source_target_pairs={{0,64},{16,80},{32,96},{48,112},{64,0},{80,16},{96,32},{112,48},{1... | collective-permute-start | bytes 2949128 | tf_op jit(solution)/shard_map/ppermute | solution.py:43
  57.6 42.7 %collective-permute-start.1 = (f32[960,256]{1,0:T(8,128)}, f32[960,256]{1,0:T(8,128)}, u32[]{:S(2)}, u32[]{:S(2)}) collective-permute-start(f32[960,256]{1,0:T(8,128)} %bitcast.13), channel_id=1, source_target_pairs={{0,80},{16,96},{32,112},{48,64},{64,16},{80,32},{96,48},{112,0},{1... | collective-permute-start | bytes 2949128 | tf_op jit(solution)/shard_map/ppermute | solution.py:43
  58.7 63.2 %collective-permute-start.2 = (f32[960,256]{1,0:T(8,128)}, f32[960,256]{1,0:T(8,128)}, u32[]{:S(2)}, u32[]{:S(2)}) collective-permute-start(f32[960,256]{1,0:T(8,128)} %bitcast.14), channel_id=1, source_target_pairs={{0,96},{16,112},{32,64},{48,80},{64,32},{80,48},{96,0},{112,16},{1... | collective-permute-start | bytes 2949128 | tf_op jit(solution)/shard_map/ppermute | solution.py:43
  62.4 79.4 %collective-permute-start.3 = (f32[960,256]{1,0:T(8,128)}, f32[960,256]{1,0:T(8,128)S(1)}, u32[]{:S(2)}, u32[]{:S(2)}) collective-permute-start(f32[960,256]{1,0:T(8,128)} %bitcast.15), channel_id=1, source_target_pairs={{0,112},{16,64},{32,80},{48,96},{64,48},{80,0},{96,16},{112,32},{1... | collective-permute-start | bytes 2949128 | tf_op jit(solution)/shard_map/ppermute | solution.py:43
  64.7 78.8 %collective-permute-start.4 = (f32[960,256]{1,0:T(8,128)}, f32[960,256]{1,0:T(8,128)S(1)}, u32[]{:S(2)}, u32[]{:S(2)}) collective-permute-start(f32[960,256]{1,0:T(8,128)} %bitcast.16), channel_id=1, source_target_pairs={{0,32},{16,48},{32,0},{48,16},{64,96},{80,112},{96,64},{112,80},{1... | collective-permute-start | bytes 2949128 | tf_op jit(solution)/shard_map/ppermute | solution.py:43
  77.7 75.6 %collective-permute-start.5 = (f32[960,256]{1,0:T(8,128)S(1)}, f32[960,256]{1,0:T(8,128)S(1)}, u32[]{:S(2)}, u32[]{:S(2)}) collective-permute-start(f32[960,256]{1,0:T(8,128)S(1)} %bitcast.19), channel_id=1, source_target_pairs={{0,16},{16,32},{32,48},{48,0},{64,80},{80,96},{96,112},{112,64},{1... | collective-permute-start | bytes 2949128 | tf_op jit(solution)/shard_map/ppermute | solution.py:43
  100.3 61.9 %collective-permute-start.6 = (f32[960,256]{1,0:T(8,128)S(1)}, f32[960,256]{1,0:T(8,128)S(1)}, u32[]{:S(2)}, u32[]{:S(2)}) collective-permute-start(f32[960,256]{1,0:T(8,128)S(1)} %bitcast.20), channel_id=1, source_target_pairs={{0,48},{16,0},{32,16},{48,32},{64,112},{80,64},{96,80},{112,96},{1... | collective-permute-start | bytes 2949128 | tf_op jit(solution)/shard_map/ppermute | solution.py:43
Sparse Core Ops, SparseCore 0:
  56.0 81.4 all-gather.1

commit v9 on v8

--- a/solution.py
+++ b/solution.py
@@ -6,17 +6,11 @@
 from jax.sharding import PartitionSpec as P
 
 
-def _offsets(ng):
-    nz = ng // 2
-    offsets = [(1, dz) for dz in range(nz)] + [(0, dz) for dz in range(nz // 2, 0, -1)]
-    return nz, offsets + [(0, dz) for dz in range(nz // 2 + 1, nz)]
-
-
 def per_device(ng, nxc, amplitudes, integrals):
     g = lax.axis_index("ga")
     ylo = lax.axis_index("ylo")
     bk, nb = integrals.shape
-    nz, offsets = _offsets(ng)
+    nz = ng // 2
     yh, z = g // nz, lax.rem(g, nz)
     regrouped = lax.all_to_all(amplitudes, "ga", split_axis=0, concat_axis=1, tiled=True)
     kw = regrouped.shape[1]
@@ -38,11 +32,16 @@
         return full_bt
 
     full_bt = place(full_bt, bt, g)
-    for dy, dz in offsets:
-        pairs = [(i, ((i // nz + dy) % 2) * nz + (i % nz + dz) % nz) for i in range(ng)]
-        got = lax.ppermute(bt, "ga", pairs)
-        src = lax.rem(yh + dy, 2) * nz + lax.rem(z - dz + nz, nz)
-        full_bt = place(full_bt, got, src)
+    across = [(i, ((i // nz + 1) % 2) * nz + i % nz) for i in range(ng)]
+    got = lax.ppermute(bt, "ga", across)
+    full_bt = place(full_bt, got, (1 - yh) * nz + z)
+    pair_b = jnp.concatenate([bt, got], axis=1)
+    for dz in [nz // 2] + [d for d in range(1, nz) if d != nz // 2]:
+        pairs = [(i, (i // nz) * nz + (i % nz + dz) % nz) for i in range(ng)]
+        got2 = lax.ppermute(pair_b, "ga", pairs)
+        zs = lax.rem(z - dz + nz, nz)
+        full_bt = place(full_bt, got2[:, :bk], yh * nz + zs)
+        full_bt = place(full_bt, got2[:, bk:], (1 - yh) * nz + zs)
     ladder_t = lax.dot_general(
         full_bt,
         full_rows,

time: 212 us -> 226 us (1.066)
  waiting for transfers between devices: 90.9 us -> 108 us
  starting transfers between devices: 11.3 us -> 6.99 us
  other arithmetic: 0 us -> 2.85 us
    ppermute x7 -> x4, waiting for transfers between devices: 71.7 us -> 88.6 us  [the longest x3 68.6 us: per_device(): got2 = lax.ppermute(pair_b, 'ga', pairs)]
    ppermute x7 -> x4, starting transfers between devices: 10.8 us -> 6.56 us  [the longest x3 4.78 us: per_device(): got2 = lax.ppermute(pair_b, 'ga', pairs)]
    concatenate x0 -> x1, other arithmetic: none -> 2.85 us  [per_device(): pair_b = jnp.concatenate([bt, got], axis=1)]
  transfers between devices with their start and end apart: 9 -> 6, of which waited for: 7 -> 4; matrix products, arithmetic and copies ran while one was open for 12% -> 11% of each run, Pallas kernels for 0% -> 0%
where the time goes in v9:
time: 226 us; the launch traced here: 225 us
  waiting for transfers between devices  108 us (48%)
  local copies, waits for them, and re-layouts  39.8 us (18%)
  matrix products  30.9 us (14%)
  blocking collectives  23.4 us (10%)
  between operations  13.4 us (6%)
  starting transfers between devices  6.99 us (3%)
  other arithmetic  2.85 us (1%)
    ppermute x3, waiting for transfers between devices, per_device(): got2 = lax.ppermute(pair_b, 'ga', pairs)  68.6 us
    dot_general x1, matrix products, per_device(): lax.dot_general(full_bt, full_rows, (((1,), (1,)), ((), ())), precision=l...  30.9 us
    all_to_all x1, blocking collectives, per_device(): lax.all_to_all(amplitudes, 'ga', split_axis=0, concat_axis=1, tiled=True)  23.4 us
    ppermute x1, waiting for transfers between devices, per_device(): got = lax.ppermute(bt, 'ga', across)  20 us
    ppermute x1, waiting for transfers between devices, per_device(): other = lax.ppermute(regrouped, 'ylo', [(0, 1), (1, 0)])  19.2 us
    dynamic_update_slice x16, local copies, waits for them, and re-layouts, place(): lax.dynamic_update_slice(full_bt, blk[:, h * kw:(h + 1) * kw], (0, pos *...  18.5 us
    transpose x1, local copies, waits for them, and re-layouts, per_device(): return (0.5 * ladder_t).T  8.71 us
    ppermute x3, starting transfers between devices, per_device(): got2 = lax.ppermute(pair_b, 'ga', pairs)  4.78 us
  transfers between devices with their start and end apart: 6, of which 4 were waited for; matrix products, arithmetic and copies ran while one was open for 11% of the time, Pallas kernels for 0%

profile of v9, /device:TPU:1, one launch (start us, length us, event | category | flops | bytes accessed | tf_op | source)
XLA Modules:
  0.0 225.2 jit_solution(18405289758150415673)
XLA Ops:
  6.5 1.8 all_to_all.14
  8.5 23.4 %all_to_all.19 = f32[8,1800,16]{1,2,0:T(8,128)S(1)} all-to-all(f32[8,1800,16]{1,2,0:T(8,128)S(1)} %copy.6), channel_id=1, replica_groups=mesh['ga'=8,'ylo'=2,'xc'=8] {'ga'}, dimensions={0} | all-to-all | bytes 1843200 | tf_op jit(solution)/shard_map/all_to_all | solution.py:15
  31.9 1.2 copy.7
  33.8 19.2 %collective-permute-done.4 = f32[1800,128]{1,0:T(8,128)} collective-permute-done((f32[1800,128]{1,0:T(8,128)}, f32[1800,128]{1,0:T(8,128)}, u32[]{:S(2)}, u32[]{:S(2)}) %collective-permute-start.4) | collective-permute-done | bytes 921632 | tf_op jit(solution)/shard_map/ppermute | solution.py:17
  53.0 2.5 %copy.8 = f32[1800,128]{0,1:T(8,128)} copy(f32[1800,128]{1,0:T(8,128)} %collective-permute-done.4) | data formatting | bytes 1843200 | tf_op jit(solution)/shard_map/ppermute | solution.py:17
  55.4 1.4 constant_dynamic-update-slice_fusion
  56.8 1.4 copy-done
  58.2 1.8 collective-permute-start
  59.9 20.0 %collective-permute-done = f32[960,256]{1,0:T(8,128)S(1)} collective-permute-done((f32[960,256]{1,0:T(8,128)}, f32[960,256]{1,0:T(8,128)S(1)}, u32[]{:S(2)}, u32[]{:S(2)}) %collective-permute-start) | collective-permute-done | bytes 983072 | tf_op jit(solution)/shard_map/ppermute | solution.py:36
  79.9 2.8 %pad_maximum_fusion = f32[960,512]{1,0:T(8,128)} fusion(f32[960,256]{1,0:T(8,128)S(1)} %collective-permute-done, f32[960,256]{1,0:T(8,128)} %bitcast.13), kind=kLoop, calls=%fused_computation.1 | loop fusion | flops 491520 | bytes 3932160 | tf_op jit(solution)/shard_map/concatenate | solution.py:38
  82.7 2.1 collective-permute-start.1
  84.8 4.1 %broadcast_in_dim.6 = f32[960,2048]{1,0:T(8,128)} broadcast(f32[]{:T(128)} %constant.154.clone.1), dimensions={} | broadcast | bytes 7864324 | tf_op jit(solution)/shard_map/broadcast_in_dim | solution.py:24
  88.9 0.9 slice_dynamic-update-slice_fusion.15
  89.8 0.9 slice_dynamic-update-slice_fusion.14
  90.7 2.7 %collective-permute-start.3 = (f32[960,512]{1,0:T(8,128)}, f32[960,512]{1,0:T(8,128)S(1)}, u32[]{:S(2)}, u32[]{:S(2)}) collective-permute-start(f32[960,512]{1,0:T(8,128)} %pad_maximum_fusion), channel_id=1, source_target_pairs={{0,48},{16,0},{32,16},{48,32},{64,112},{80,64},{96,80},{112,96},{1... | collective-permute-start | bytes 5898248 | tf_op jit(solution)/shard_map/ppermute | solution.py:41
  94.2 0.9 slice_dynamic-update-slice_fusion.12
  95.1 29.7 %collective-permute-done.1 = f32[960,512]{1,0:T(8,128)} collective-permute-done((f32[960,512]{1,0:T(8,128)}, f32[960,512]{1,0:T(8,128)}, u32[]{:S(2)}, u32[]{:S(2)}) %collective-permute-start.1) | collective-permute-done | bytes 1966112 | tf_op jit(solution)/shard_map/ppermute | solution.py:41
  124.8 1.9 slice_dynamic-update-slice_fusion.11
  126.7 1.9 slice_dynamic-update-slice_fusion.10
  128.6 1.9 slice_dynamic-update-slice_fusion.9
  130.5 1.9 slice_dynamic-update-slice_fusion.8
  132.4 38.9 %collective-permute-done.2 = f32[960,512]{1,0:T(8,128)S(1)} collective-permute-done((f32[960,512]{1,0:T(8,128)}, f32[960,512]{1,0:T(8,128)S(1)}, u32[]{:S(2)}, u32[]{:S(2)}) %collective-permute-start.2) | collective-permute-done | bytes 1966112 | tf_op jit(solution)/shard_map/ppermute | solution.py:41
  171.3 0.9 slice_dynamic-update-slice_fusion.7
  172.3 0.9 slice_dynamic-update-slice_fusion.6
  173.2 0.9 slice_dynamic-update-slice_fusion.5
  174.1 0.9 slice_dynamic-update-slice_fusion.4
  175.0 0.9 slice_dynamic-update-slice_fusion.3
  175.9 0.9 slice_dynamic-update-slice_fusion.2
  176.8 1.0 slice_dynamic-update-slice_fusion.1
  177.8 1.0 slice_dynamic-update-slice_fusion
  178.8 30.9 %multiply_bitcast_fusion = f32[1800,960]{0,1:T(8,128)} fusion(f32[960,2048]{1,0:T(8,128)} %slice_dynamic-update-slice_fusion, f32[1800,2048]{0,1:T(8,128)} %all-gather.2.cloned.1.call-done), kind=kOutput, calls=%fused_computation | convolution fusion | flops 21235392512 | bytes 29521920 | tf_op jit(solution)/shard_map/dot_general | solution.py:45
  209.7 8.7 %copy.9 = f32[1800,960]{1,0:T(8,128)} copy(f32[1800,960]{0,1:T(8,128)} %multiply_bitcast_fusion) | data formatting | bytes 13824000 | tf_op jit(solution)/shard_map/transpose | solution.py:53
  (13 shorter events, 1.7 us)
Async XLA Ops:
  6.5 172.2 %all-gather.2.cloned.1.call-start = ((), (), s32[]{:S(2)}) async-start(), calls=%async_computation.1 | async-start | bytes 17694720 | tf_op jit(solution)/shard_map/all_gather | solution.py:21
  33.1 19.9 %collective-permute-start.4 = (f32[1800,128]{1,0:T(8,128)}, f32[1800,128]{1,0:T(8,128)}, u32[]{:S(2)}, u32[]{:S(2)}) collective-permute-start(f32[1800,128]{1,0:T(8,128)} %copy.7), channel_id=1, source_target_pairs={{0,8},{8,0},{1,9},{9,1},{2,10},{10,2},{3,11},{11,3},{4,12},{12,4},... | collective-permute-start | bytes 2764808 | tf_op jit(solution)/shard_map/ppermute | solution.py:17
  55.4 33.5 %copy-start.1 = (f32[256,960]{0,1:T(8,128)S(1)}, f32[256,960]{0,1:T(8,128)}, u32[]{:S(2)}) copy-start(f32[256,960]{0,1:T(8,128)} %param.3) | copy-start | bytes 2949124
  56.8 1.4 copy-start
  58.2 21.7 %collective-permute-start = (f32[960,256]{1,0:T(8,128)}, f32[960,256]{1,0:T(8,128)S(1)}, u32[]{:S(2)}, u32[]{:S(2)}) collective-permute-start(f32[960,256]{1,0:T(8,128)} %bitcast.12), channel_id=1, source_target_pairs={{0,64},{16,80},{32,96},{48,112},{64,0},{80,16},{96,32},{112,48},{1... | collective-permute-start | bytes 2949128 | tf_op jit(solution)/shard_map/ppermute | solution.py:36
  82.7 42.1 %collective-permute-start.1 = (f32[960,512]{1,0:T(8,128)}, f32[960,512]{1,0:T(8,128)}, u32[]{:S(2)}, u32[]{:S(2)}) collective-permute-start(f32[960,512]{1,0:T(8,128)} %pad_maximum_fusion), channel_id=1, source_target_pairs={{0,32},{16,48},{32,0},{48,16},{64,96},{80,112},{96,64},{112,80},{1... | collective-permute-start | bytes 5898248 | tf_op jit(solution)/shard_map/ppermute | solution.py:41
  84.8 86.5 %collective-permute-start.2 = (f32[960,512]{1,0:T(8,128)}, f32[960,512]{1,0:T(8,128)S(1)}, u32[]{:S(2)}, u32[]{:S(2)}) collective-permute-start(f32[960,512]{1,0:T(8,128)} %pad_maximum_fusion), channel_id=1, source_target_pairs={{0,16},{16,32},{32,48},{48,0},{64,80},{80,96},{96,112},{112,64},{1... | collective-permute-start | bytes 5898248 | tf_op jit(solution)/shard_map/ppermute | solution.py:41
  90.7 84.3 %collective-permute-start.3 = (f32[960,512]{1,0:T(8,128)}, f32[960,512]{1,0:T(8,128)S(1)}, u32[]{:S(2)}, u32[]{:S(2)}) collective-permute-start(f32[960,512]{1,0:T(8,128)} %pad_maximum_fusion), channel_id=1, source_target_pairs={{0,48},{16,0},{32,16},{48,32},{64,112},{80,64},{96,80},{112,96},{1... | collective-permute-start | bytes 5898248 | tf_op jit(solution)/shard_map/ppermute | solution.py:41
Sparse Core Ops, SparseCore 0:
  58.3 81.4 all-gather.1

commit v10 on v8

--- a/solution.py
+++ b/solution.py
@@ -13,12 +13,16 @@
 
 
 def per_device(ng, nxc, amplitudes, integrals):
-    g = lax.axis_index("ga")
+    nz = ng // 2
+    g = lax.axis_index("yh") * nz + lax.axis_index("zz")
     ylo = lax.axis_index("ylo")
     bk, nb = integrals.shape
     nz, offsets = _offsets(ng)
     yh, z = g // nz, lax.rem(g, nz)
-    regrouped = lax.all_to_all(amplitudes, "ga", split_axis=0, concat_axis=1, tiled=True)
+    half = lax.all_to_all(amplitudes, "yh", split_axis=0, concat_axis=1, tiled=True)
+    quarter = lax.all_to_all(half, "zz", split_axis=0, concat_axis=1, tiled=True)
+    cw = amplitudes.shape[1]
+    regrouped = quarter.reshape(-1, nz, 2, cw).transpose(0, 2, 1, 3).reshape(quarter.shape[0], -1)
     kw = regrouped.shape[1]
     other = lax.ppermute(regrouped, "ylo", [(0, 1), (1, 0)])
     pair = jnp.zeros((regrouped.shape[0], 2 * kw), jnp.float32)
@@ -40,7 +44,7 @@
     full_bt = place(full_bt, bt, g)
     for dy, dz in offsets:
         pairs = [(i, ((i // nz + dy) % 2) * nz + (i % nz + dz) % nz) for i in range(ng)]
-        got = lax.ppermute(bt, "ga", pairs)
+        got = lax.ppermute(bt, ("yh", "zz"), pairs)
         src = lax.rem(yh + dy, 2) * nz + lax.rem(z - dz + nz, nz)
         full_bt = place(full_bt, got, src)
     ladder_t = lax.dot_general(
@@ -57,9 +61,9 @@
 def solution(mesh):
     ng = mesh.shape["ga"]
     nk = mesh.shape["ka"]
-    fine = Mesh(mesh.devices.reshape(ng, 2, nk // 2), ("ga", "ylo", "xc"))
-    placed = (P(None, ("ylo", "xc", "ga")), P("ga", ("ylo", "xc")))
+    fine = Mesh(mesh.devices.reshape(2, ng // 2, 2, nk // 2), ("yh", "zz", "ylo", "xc"))
+    placed = (P(None, ("ylo", "xc", "yh", "zz")), P(("yh", "zz"), ("ylo", "xc")))
     return jax.shard_map(
         lambda a, b: per_device(ng, nk // 2, a, b), mesh=fine, in_specs=placed,
-        out_specs=P("ga", ("ylo", "xc")), check_vma=False
+        out_specs=P(("yh", "zz"), ("ylo", "xc")), check_vma=False
     )

time: 212 us -> 223 us (1.052)
  blocking collectives: 23.4 us -> 34.9 us
  waiting for transfers between devices: 90.9 us -> 88.2 us
    all_to_all x1 -> x2, blocking collectives: 23.4 us -> 34.9 us  [the longest x1 17.8 us: per_device(): lax.all_to_all(amplitudes, 'yh', split_axis=0, concat_axis=1, tiled=True)]
where the time goes in v10:
time: 223 us; the launch traced here: 220 us
  waiting for transfers between devices  88.2 us (40%)
  local copies, waits for them, and re-layouts  41.5 us (19%)
  blocking collectives  34.9 us (16%)
  matrix products  30.9 us (14%)
  between operations  13.5 us (6%)
  starting transfers between devices  10.9 us (5%)
    ppermute x7, waiting for transfers between devices, per_device(): got = lax.ppermute(bt, ('yh', 'zz'), pairs)  69.6 us
    dot_general x1, matrix products, per_device(): lax.dot_general(full_bt, full_rows, (((1,), (1,)), ((), ())), precision=l...  30.9 us
    dynamic_update_slice x16, local copies, waits for them, and re-layouts, place(): lax.dynamic_update_slice(full_bt, blk[:, h * kw:(h + 1) * kw], (0, pos *...  20.5 us
    ppermute x1, waiting for transfers between devices, per_device(): other = lax.ppermute(regrouped, 'ylo', [(0, 1), (1, 0)])  18.6 us
    all_to_all x1, blocking collectives, per_device(): lax.all_to_all(amplitudes, 'yh', split_axis=0, concat_axis=1, tiled=True)  17.8 us
    all_to_all x1, blocking collectives, per_device(): lax.all_to_all(half, 'zz', split_axis=0, concat_axis=1, tiled=True)  17.1 us
    ppermute x7, starting transfers between devices, per_device(): got = lax.ppermute(bt, ('yh', 'zz'), pairs)  10.5 us
    transpose x1, local copies, waits for them, and re-layouts, per_device(): return (0.5 * ladder_t).T  8.71 us
  transfers between devices with their start and end apart: 9, of which 7 were waited for; matrix products, arithmetic and copies ran while one was open for 12% of the time, Pallas kernels for 0%

profile of v10, /device:TPU:1, one launch (start us, length us, event | category | flops | bytes accessed | tf_op | source)
XLA Modules:
  0.0 219.9 jit_solution(2907001103060731901)
XLA Ops:
  6.5 1.9 all_to_all.24
  8.5 17.8 %all_to_all.32 = f32[2,7200,16]{1,2,0:T(8,128)S(1)} all-to-all(f32[2,7200,16]{1,2,0:T(8,128)S(1)} %copy.8), channel_id=1, replica_groups=mesh['yh'=2,'zz'=4,'ylo'=2,'xc'=8] {'yh'}, dimensions={0} | all-to-all | bytes 1843200 | tf_op jit(solution)/shard_map/all_to_all | solution.py:22
  27.0 17.1 %all_to_all.33 = f32[4,1800,32]{1,2,0:T(8,128)S(1)} all-to-all(f32[4,1800,32]{1,2,0:T(8,128)S(1)} %copy.9), channel_id=1, replica_groups=mesh['yh'=2,'zz'=4,'ylo'=2,'xc'=8] {'zz'}, dimensions={0} | all-to-all | bytes 1843200 | tf_op jit(solution)/shard_map/all_to_all | solution.py:23
  44.2 1.2 copy.11
  46.0 18.6 %collective-permute-done.7 = f32[1800,128]{1,0:T(8,128)} collective-permute-done((f32[1800,128]{1,0:T(8,128)}, f32[1800,128]{1,0:T(8,128)}, u32[]{:S(2)}, u32[]{:S(2)}) %collective-permute-start.7) | collective-permute-done | bytes 921632 | tf_op jit(solution)/shard_map/ppermute | solution.py:27
  64.6 1.5 copy.12
  66.2 1.2 copy-done
  68.1 2.4 %collective-permute-start.1 = (f32[960,256]{1,0:T(8,128)}, f32[960,256]{1,0:T(8,128)}, u32[]{:S(2)}, u32[]{:S(2)}) collective-permute-start(f32[960,256]{1,0:T(8,128)} %bitcast.21), channel_id=1, source_target_pairs={{0,80},{16,96},{32,112},{48,64},{64,16},{80,32},{96,48},{112,0},{1... | collective-permute-start | bytes 2949128 | tf_op jit(solution)/shard_map/ppermute | solution.py:47
  70.5 2.0 collective-permute-start.2
  72.6 2.5 %collective-permute-start.3 = (f32[960,256]{1,0:T(8,128)}, f32[960,256]{1,0:T(8,128)S(1)}, u32[]{:S(2)}, u32[]{:S(2)}) collective-permute-start(f32[960,256]{1,0:T(8,128)} %bitcast.23), channel_id=1, source_target_pairs={{0,112},{16,64},{32,80},{48,96},{64,48},{80,0},{96,16},{112,32},{1... | collective-permute-start | bytes 2949128 | tf_op jit(solution)/shard_map/ppermute | solution.py:47
  75.1 2.6 %collective-permute-start.4 = (f32[960,256]{1,0:T(8,128)}, f32[960,256]{1,0:T(8,128)S(1)}, u32[]{:S(2)}, u32[]{:S(2)}) collective-permute-start(f32[960,256]{1,0:T(8,128)} %bitcast.24), channel_id=1, source_target_pairs={{0,32},{16,48},{32,0},{48,16},{64,96},{80,112},{96,64},{112,80},{1... | collective-permute-start | bytes 2949128 | tf_op jit(solution)/shard_map/ppermute | solution.py:47
  77.7 5.3 %broadcast_in_dim.6 = f32[960,2048]{1,0:T(8,128)} broadcast(f32[]{:T(128)} %constant.164.clone.1), dimensions={} | broadcast | bytes 7864324 | tf_op jit(solution)/shard_map/broadcast_in_dim | solution.py:34
  83.0 0.9 slice_dynamic-update-slice_fusion.15
  83.8 0.9 slice_dynamic-update-slice_fusion.14
  84.7 3.9 %collective-permute-done = f32[960,256]{1,0:T(8,128)} collective-permute-done((f32[960,256]{1,0:T(8,128)}, f32[960,256]{1,0:T(8,128)}, u32[]{:S(2)}, u32[]{:S(2)}) %collective-permute-start) | collective-permute-done | bytes 983072 | tf_op jit(solution)/shard_map/ppermute | solution.py:47
  88.9 2.0 slice_dynamic-update-slice_fusion.13
  91.0 1.9 slice_dynamic-update-slice_fusion.12
  92.9 17.5 %collective-permute-done.1 = f32[960,256]{1,0:T(8,128)} collective-permute-done((f32[960,256]{1,0:T(8,128)}, f32[960,256]{1,0:T(8,128)}, u32[]{:S(2)}, u32[]{:S(2)}) %collective-permute-start.1) | collective-permute-done | bytes 983072 | tf_op jit(solution)/shard_map/ppermute | solution.py:47
  110.4 1.9 slice_dynamic-update-slice_fusion.11
  112.3 1.9 slice_dynamic-update-slice_fusion.10
  114.2 16.9 %collective-permute-done.2 = f32[960,256]{1,0:T(8,128)} collective-permute-done((f32[960,256]{1,0:T(8,128)}, f32[960,256]{1,0:T(8,128)}, u32[]{:S(2)}, u32[]{:S(2)}) %collective-permute-start.2) | collective-permute-done | bytes 983072 | tf_op jit(solution)/shard_map/ppermute | solution.py:47
  131.1 2.0 slice_dynamic-update-slice_fusion.9
  133.1 2.0 slice_dynamic-update-slice_fusion.8
  135.1 17.7 %collective-permute-done.3 = f32[960,256]{1,0:T(8,128)S(1)} collective-permute-done((f32[960,256]{1,0:T(8,128)}, f32[960,256]{1,0:T(8,128)S(1)}, u32[]{:S(2)}, u32[]{:S(2)}) %collective-permute-start.3) | collective-permute-done | bytes 983072 | tf_op jit(solution)/shard_map/ppermute | solution.py:47
  154.5 0.9 slice_dynamic-update-slice_fusion.5
  155.4 0.9 slice_dynamic-update-slice_fusion.4
  156.3 7.7 %collective-permute-done.5 = f32[960,256]{1,0:T(8,128)S(1)} collective-permute-done((f32[960,256]{1,0:T(8,128)S(1)}, f32[960,256]{1,0:T(8,128)S(1)}, u32[]{:S(2)}, u32[]{:S(2)}) %collective-permute-start.5) | collective-permute-done | bytes 983072 | tf_op jit(solution)/shard_map/ppermute | solution.py:47
  164.0 0.9 slice_dynamic-update-slice_fusion.3
  165.7 5.9 %collective-permute-done.6 = f32[960,256]{1,0:T(8,128)S(1)} collective-permute-done((f32[960,256]{1,0:T(8,128)S(1)}, f32[960,256]{1,0:T(8,128)S(1)}, u32[]{:S(2)}, u32[]{:S(2)}) %collective-permute-start.6) | collective-permute-done | bytes 983072 | tf_op jit(solution)/shard_map/ppermute | solution.py:47
  172.5 0.9 slice_dynamic-update-slice_fusion
  173.4 30.9 %multiply_bitcast_fusion = f32[1800,960]{0,1:T(8,128)} fusion(f32[960,2048]{1,0:T(8,128)} %slice_dynamic-update-slice_fusion, f32[1800,2048]{0,1:T(8,128)} %all-gather.2.cloned.1.call-done), kind=kOutput, calls=%fused_computation | convolution fusion | flops 21235392512 | bytes 29521920 | tf_op jit(solution)/shard_map/dot_general | solution.py:50
  204.3 8.7 %copy.13 = f32[1800,960]{1,0:T(8,128)} copy(f32[1800,960]{0,1:T(8,128)} %multiply_bitcast_fusion) | data formatting | bytes 13824000 | tf_op jit(solution)/shard_map/transpose | solution.py:58
  (22 shorter events, 5.9 us)
Async XLA Ops:
  6.5 166.8 %all-gather.2.cloned.1.call-start = ((), (), s32[]{:S(2)}) async-start(), calls=%async_computation.2 | async-start | bytes 17694720 | tf_op jit(solution)/shard_map/all_gather | solution.py:31
  45.4 19.2 %collective-permute-start.7 = (f32[1800,128]{1,0:T(8,128)}, f32[1800,128]{1,0:T(8,128)}, u32[]{:S(2)}, u32[]{:S(2)}) collective-permute-start(f32[1800,128]{1,0:T(8,128)} %copy.11), channel_id=1, source_target_pairs={{0,8},{8,0},{1,9},{9,1},{2,10},{10,2},{3,11},{11,3},{4,12},{12,4},... | collective-permute-start | bytes 2764808 | tf_op jit(solution)/shard_map/ppermute | solution.py:27
  66.2 1.3 copy-start
  66.2 16.8 %copy-start.1 = (f32[256,960]{0,1:T(8,128)S(1)}, f32[256,960]{0,1:T(8,128)}, u32[]{:S(2)}) copy-start(f32[256,960]{0,1:T(8,128)} %param.3) | copy-start | bytes 2949124
  67.5 21.2 %collective-permute-start = (f32[960,256]{1,0:T(8,128)}, f32[960,256]{1,0:T(8,128)}, u32[]{:S(2)}, u32[]{:S(2)}) collective-permute-start(f32[960,256]{1,0:T(8,128)} %bitcast.20), channel_id=1, source_target_pairs={{0,64},{16,80},{32,96},{48,112},{64,0},{80,16},{96,32},{112,48},{1... | collective-permute-start | bytes 2949128 | tf_op jit(solution)/shard_map/ppermute | solution.py:47
  68.1 42.3 %collective-permute-start.1 = (f32[960,256]{1,0:T(8,128)}, f32[960,256]{1,0:T(8,128)}, u32[]{:S(2)}, u32[]{:S(2)}) collective-permute-start(f32[960,256]{1,0:T(8,128)} %bitcast.21), channel_id=1, source_target_pairs={{0,80},{16,96},{32,112},{48,64},{64,16},{80,32},{96,48},{112,0},{1... | collective-permute-start | bytes 2949128 | tf_op jit(solution)/shard_map/ppermute | solution.py:47
  70.5 60.6 %collective-permute-start.2 = (f32[960,256]{1,0:T(8,128)}, f32[960,256]{1,0:T(8,128)}, u32[]{:S(2)}, u32[]{:S(2)}) collective-permute-start(f32[960,256]{1,0:T(8,128)} %bitcast.22), channel_id=1, source_target_pairs={{0,96},{16,112},{32,64},{48,80},{64,32},{80,48},{96,0},{112,16},{1... | collective-permute-start | bytes 2949128 | tf_op jit(solution)/shard_map/ppermute | solution.py:47
  72.6 80.2 %collective-permute-start.3 = (f32[960,256]{1,0:T(8,128)}, f32[960,256]{1,0:T(8,128)S(1)}, u32[]{:S(2)}, u32[]{:S(2)}) collective-permute-start(f32[960,256]{1,0:T(8,128)} %bitcast.23), channel_id=1, source_target_pairs={{0,112},{16,64},{32,80},{48,96},{64,48},{80,0},{96,16},{112,32},{1... | collective-permute-start | bytes 2949128 | tf_op jit(solution)/shard_map/ppermute | solution.py:47
  75.1 79.5 %collective-permute-start.4 = (f32[960,256]{1,0:T(8,128)}, f32[960,256]{1,0:T(8,128)S(1)}, u32[]{:S(2)}, u32[]{:S(2)}) collective-permute-start(f32[960,256]{1,0:T(8,128)} %bitcast.24), channel_id=1, source_target_pairs={{0,32},{16,48},{32,0},{48,16},{64,96},{80,112},{96,64},{112,80},{1... | collective-permute-start | bytes 2949128 | tf_op jit(solution)/shard_map/ppermute | solution.py:47
  88.6 75.4 %collective-permute-start.5 = (f32[960,256]{1,0:T(8,128)S(1)}, f32[960,256]{1,0:T(8,128)S(1)}, u32[]{:S(2)}, u32[]{:S(2)}) collective-permute-start(f32[960,256]{1,0:T(8,128)S(1)} %bitcast.27), channel_id=1, source_target_pairs={{0,16},{16,32},{32,48},{48,0},{64,80},{80,96},{96,112},{112,64},{1... | collective-permute-start | bytes 2949128 | tf_op jit(solution)/shard_map/ppermute | solution.py:47
  110.4 61.2 %collective-permute-start.6 = (f32[960,256]{1,0:T(8,128)S(1)}, f32[960,256]{1,0:T(8,128)S(1)}, u32[]{:S(2)}, u32[]{:S(2)}) collective-permute-start(f32[960,256]{1,0:T(8,128)S(1)} %bitcast.28), channel_id=1, source_target_pairs={{0,48},{16,0},{32,16},{48,32},{64,112},{80,64},{96,80},{112,96},{1... | collective-permute-start | bytes 2949128 | tf_op jit(solution)/shard_map/ppermute | solution.py:47
Sparse Core Ops, SparseCore 0:
  67.6 81.2 all-gather.1

commit v11 on v8

--- a/solution.py
+++ b/solution.py
@@ -14,16 +14,15 @@
 
 def per_device(ng, nxc, amplitudes, integrals):
     g = lax.axis_index("ga")
-    ylo = lax.axis_index("ylo")
     bk, nb = integrals.shape
     nz, offsets = _offsets(ng)
     yh, z = g // nz, lax.rem(g, nz)
-    regrouped = lax.all_to_all(amplitudes, "ga", split_axis=0, concat_axis=1, tiled=True)
-    kw = regrouped.shape[1]
-    other = lax.ppermute(regrouped, "ylo", [(0, 1), (1, 0)])
-    pair = jnp.zeros((regrouped.shape[0], 2 * kw), jnp.float32)
-    pair = lax.dynamic_update_slice(pair, regrouped, (0, ylo * kw))
-    pair = lax.dynamic_update_slice(pair, other, (0, (1 - ylo) * kw))
+    cw = amplitudes.shape[1]
+    kw = ng * cw
+    twice = jnp.repeat(amplitudes.reshape(ng, -1, cw), 2, axis=0).reshape(-1, cw)
+    both = lax.all_to_all(twice, ("ga", "ylo"), split_axis=0, concat_axis=1, tiled=True)
+    rows = both.shape[0]
+    pair = both.reshape(rows, ng, 2, cw).transpose(0, 2, 1, 3).reshape(rows, 2 * kw)
     full_rows = lax.all_gather(pair, "xc", axis=1, tiled=True)
 
     bt = integrals.T

time: 212 us -> 203 us (0.958)
  waiting for transfers between devices: 90.9 us -> 76.2 us
  blocking collectives: 23.4 us -> 34.3 us
  local copies, waits for them, and re-layouts: 40.5 us -> 37.5 us
    ppermute x1 -> x0, waiting for transfers between devices: 19.2 us -> none  [per_device(): other = lax.ppermute(regrouped, 'ylo', [(0, 1), (1, 0)])]
    all_to_all x1, blocking collectives: 23.4 us -> 34.3 us  [per_device(): lax.all_to_all(twice, ('ga', 'ylo'), split_axis=0, concat_axis=1, tiled=T...]
    ppermute x7, waiting for transfers between devices: 71.7 us -> 76.2 us  [per_device(): got = lax.ppermute(bt, 'ga', pairs)]
    all_to_all x3 -> x0, local copies, waits for them, and re-layouts: 3.2 us -> none  [per_device(): lax.all_to_all(amplitudes, 'ga', split_axis=0, concat_axis=1, tiled=True)]
  transfers between devices with their start and end apart: 9 -> 8, of which waited for: 7 -> 6; matrix products, arithmetic and copies ran while one was open for 12% -> 12% of each run, Pallas kernels for 0% -> 0%
where the time goes in v11:
time: 203 us
  waiting for transfers between devices  76.2 us (38%)
  local copies, waits for them, and re-layouts  37.5 us (18%)
  blocking collectives  34.3 us (17%)
  matrix products  30.9 us (15%)
  between operations  13.4 us (7%)
  starting transfers between devices  10.2 us (5%)
    ppermute x7, waiting for transfers between devices, per_device(): got = lax.ppermute(bt, 'ga', pairs)  76.2 us
    all_to_all x1, blocking collectives, per_device(): lax.all_to_all(twice, ('ga', 'ylo'), split_axis=0, concat_axis=1, tiled=T...  34.3 us
    dot_general x1, matrix products, per_device(): lax.dot_general(full_bt, full_rows, (((1,), (1,)), ((), ())), precision=l...  30.9 us
    dynamic_update_slice x16, local copies, waits for them, and re-layouts, place(): lax.dynamic_update_slice(full_bt, blk[:, h * kw:(h + 1) * kw], (0, pos *...  20.3 us
    ppermute x7, starting transfers between devices, per_device(): got = lax.ppermute(bt, 'ga', pairs)  10.2 us
    transpose x1, local copies, waits for them, and re-layouts, per_device(): return (0.5 * ladder_t).T  8.71 us
    broadcast_in_dim x1, local copies, waits for them, and re-layouts, per_device(): full_bt = jnp.zeros((nb, bk * ng), jnp.float32)  4.85 us
  transfers between devices with their start and end apart: 8, of which 6 were waited for; matrix products, arithmetic and copies ran while one was open for 12% of the time, Pallas kernels for 0%

profile of v11, /device:TPU:1, one launch (start us, length us, event | category | flops | bytes accessed | tf_op | source)
XLA Modules:
  0.0 202.6 jit_solution(16244274782648275406)
XLA Ops:
  6.5 1.9 reshape.14
  8.8 34.3 %all_to_all.16 = f32[16,1800,16]{1,2,0:T(8,128)S(1)} all-to-all(f32[16,1800,16]{1,2,0:T(8,128)S(1)} %bitcast.15), channel_id=1, replica_groups=mesh['ga'=8,'ylo'=2,'xc'=8] {'ga','ylo'}, dimensions={0} | all-to-all | bytes 3686400 | tf_op jit(solution)/shard_map/all_to_all | solution.py:23
  43.1 1.4 copy.8
  45.1 0.9 collective-permute-start.1
  46.0 5.1 %collective-permute-start.2 = (f32[960,256]{1,0:T(8,128)S(1)}, f32[960,256]{1,0:T(8,128)}, u32[]{:S(2)}, u32[]{:S(2)}) collective-permute-start(f32[960,256]{1,0:T(8,128)S(1)} %bitcast.19), channel_id=1, source_target_pairs={{0,96},{16,112},{32,64},{48,80},{64,32},{80,48},{96,0},{112,16},{1... | collective-permute-start | bytes 2949128 | tf_op jit(solution)/shard_map/ppermute | solution.py:42
  51.2 1.0 collective-permute-start.3
  52.1 2.6 %collective-permute-start.4 = (f32[960,256]{1,0:T(8,128)S(1)}, f32[960,256]{1,0:T(8,128)S(1)}, u32[]{:S(2)}, u32[]{:S(2)}) collective-permute-start(f32[960,256]{1,0:T(8,128)S(1)} %bitcast.21), channel_id=1, source_target_pairs={{0,32},{16,48},{32,0},{48,16},{64,96},{80,112},{96,64},{112,80},{1... | collective-permute-start | bytes 2949128 | tf_op jit(solution)/shard_map/ppermute | solution.py:42
  54.7 4.8 %broadcast_in_dim.6 = f32[960,2048]{1,0:T(8,128)} broadcast(f32[]{:T(128)} %constant.155.clone.1), dimensions={} | broadcast | bytes 7864324 | tf_op jit(solution)/shard_map/broadcast_in_dim | solution.py:29
  59.6 0.9 slice_dynamic-update-slice_fusion.15
  60.5 0.9 slice_dynamic-update-slice_fusion.14
  61.4 6.1 %collective-permute-done = f32[960,256]{1,0:T(8,128)} collective-permute-done((f32[960,256]{1,0:T(8,128)S(1)}, f32[960,256]{1,0:T(8,128)}, u32[]{:S(2)}, u32[]{:S(2)}) %collective-permute-start) | collective-permute-done | bytes 983072 | tf_op jit(solution)/shard_map/ppermute | solution.py:42
  67.5 2.0 slice_dynamic-update-slice_fusion.13
  69.4 2.0 slice_dynamic-update-slice_fusion.12
  71.4 20.4 %collective-permute-done.1 = f32[960,256]{1,0:T(8,128)} collective-permute-done((f32[960,256]{1,0:T(8,128)S(1)}, f32[960,256]{1,0:T(8,128)}, u32[]{:S(2)}, u32[]{:S(2)}) %collective-permute-start.1) | collective-permute-done | bytes 983072 | tf_op jit(solution)/shard_map/ppermute | solution.py:42
  91.8 1.9 slice_dynamic-update-slice_fusion.11
  93.7 1.9 slice_dynamic-update-slice_fusion.10
  95.6 15.4 %collective-permute-done.2 = f32[960,256]{1,0:T(8,128)} collective-permute-done((f32[960,256]{1,0:T(8,128)S(1)}, f32[960,256]{1,0:T(8,128)}, u32[]{:S(2)}, u32[]{:S(2)}) %collective-permute-start.2) | collective-permute-done | bytes 983072 | tf_op jit(solution)/shard_map/ppermute | solution.py:42
  111.0 1.9 slice_dynamic-update-slice_fusion.9
  112.9 1.9 slice_dynamic-update-slice_fusion.8
  114.8 15.4 %collective-permute-done.3 = f32[960,256]{1,0:T(8,128)S(1)} collective-permute-done((f32[960,256]{1,0:T(8,128)S(1)}, f32[960,256]{1,0:T(8,128)S(1)}, u32[]{:S(2)}, u32[]{:S(2)}) %collective-permute-start.3) | collective-permute-done | bytes 983072 | tf_op jit(solution)/shard_map/ppermute | solution.py:42
  130.2 0.8 slice_dynamic-update-slice_fusion.7
  131.0 0.9 slice_dynamic-update-slice_fusion.6
  131.9 0.9 slice_dynamic-update-slice_fusion.5
  132.8 0.9 slice_dynamic-update-slice_fusion.4
  133.7 7.9 %collective-permute-done.5 = f32[960,256]{1,0:T(8,128)S(1)} collective-permute-done((f32[960,256]{1,0:T(8,128)S(1)}, f32[960,256]{1,0:T(8,128)S(1)}, u32[]{:S(2)}, u32[]{:S(2)}) %collective-permute-start.5) | collective-permute-done | bytes 983072 | tf_op jit(solution)/shard_map/ppermute | solution.py:42
  141.5 0.9 slice_dynamic-update-slice_fusion.3
  142.4 0.9 slice_dynamic-update-slice_fusion.2
  143.3 11.1 %collective-permute-done.6 = f32[960,256]{1,0:T(8,128)S(1)} collective-permute-done((f32[960,256]{1,0:T(8,128)S(1)}, f32[960,256]{1,0:T(8,128)S(1)}, u32[]{:S(2)}, u32[]{:S(2)}) %collective-permute-start.6) | collective-permute-done | bytes 983072 | tf_op jit(solution)/shard_map/ppermute | solution.py:42
  154.3 0.9 slice_dynamic-update-slice_fusion.1
  155.2 0.8 slice_dynamic-update-slice_fusion
  156.1 30.9 %multiply_bitcast_fusion = f32[1800,960]{0,1:T(8,128)} fusion(f32[960,2048]{1,0:T(8,128)} %slice_dynamic-update-slice_fusion, f32[1800,2048]{0,1:T(8,128)} %all-gather.2.cloned.1.call-done), kind=kOutput, calls=%fused_computation | convolution fusion | flops 21235392512 | bytes 29521920 | tf_op jit(solution)/shard_map/dot_general | solution.py:45
  187.0 8.7 %copy.9 = f32[1800,960]{1,0:T(8,128)} copy(f32[1800,960]{0,1:T(8,128)} %multiply_bitcast_fusion) | data formatting | bytes 13824000 | tf_op jit(solution)/shard_map/transpose | solution.py:53
  (11 shorter events, 0.9 us)
Async XLA Ops:
  6.5 38.0 %copy-start = (f32[256,960]{0,1:T(8,128)S(1)}, f32[256,960]{0,1:T(8,128)}, u32[]{:S(2)}) copy-start(f32[256,960]{0,1:T(8,128)} %param.3) | copy-start | bytes 2949124
  6.5 149.6 %all-gather.2.cloned.1.call-start = ((), (), s32[]{:S(2)}) async-start(), calls=%async_computation.1 | async-start | bytes 17694720 | tf_op jit(solution)/shard_map/all_gather | solution.py:26
  44.5 22.9 %collective-permute-start = (f32[960,256]{1,0:T(8,128)S(1)}, f32[960,256]{1,0:T(8,128)}, u32[]{:S(2)}, u32[]{:S(2)}) collective-permute-start(f32[960,256]{1,0:T(8,128)S(1)} %bitcast.17), channel_id=1, source_target_pairs={{0,64},{16,80},{32,96},{48,112},{64,0},{80,16},{96,32},{112,48},{1... | collective-permute-start | bytes 2949128 | tf_op jit(solution)/shard_map/ppermute | solution.py:42
  45.1 46.7 %collective-permute-start.1 = (f32[960,256]{1,0:T(8,128)S(1)}, f32[960,256]{1,0:T(8,128)}, u32[]{:S(2)}, u32[]{:S(2)}) collective-permute-start(f32[960,256]{1,0:T(8,128)S(1)} %bitcast.18), channel_id=1, source_target_pairs={{0,80},{16,96},{32,112},{48,64},{64,16},{80,32},{96,48},{112,0},{1... | collective-permute-start | bytes 2949128 | tf_op jit(solution)/shard_map/ppermute | solution.py:42
  46.0 65.0 %collective-permute-start.2 = (f32[960,256]{1,0:T(8,128)S(1)}, f32[960,256]{1,0:T(8,128)}, u32[]{:S(2)}, u32[]{:S(2)}) collective-permute-start(f32[960,256]{1,0:T(8,128)S(1)} %bitcast.19), channel_id=1, source_target_pairs={{0,96},{16,112},{32,64},{48,80},{64,32},{80,48},{96,0},{112,16},{1... | collective-permute-start | bytes 2949128 | tf_op jit(solution)/shard_map/ppermute | solution.py:42
  51.2 79.0 %collective-permute-start.3 = (f32[960,256]{1,0:T(8,128)S(1)}, f32[960,256]{1,0:T(8,128)S(1)}, u32[]{:S(2)}, u32[]{:S(2)}) collective-permute-start(f32[960,256]{1,0:T(8,128)S(1)} %bitcast.20), channel_id=1, source_target_pairs={{0,112},{16,64},{32,80},{48,96},{64,48},{80,0},{96,16},{112,32},{1... | collective-permute-start | bytes 2949128 | tf_op jit(solution)/shard_map/ppermute | solution.py:42
  52.1 79.8 %collective-permute-start.4 = (f32[960,256]{1,0:T(8,128)S(1)}, f32[960,256]{1,0:T(8,128)S(1)}, u32[]{:S(2)}, u32[]{:S(2)}) collective-permute-start(f32[960,256]{1,0:T(8,128)S(1)} %bitcast.21), channel_id=1, source_target_pairs={{0,32},{16,48},{32,0},{48,16},{64,96},{80,112},{96,64},{112,80},{1... | collective-permute-start | bytes 2949128 | tf_op jit(solution)/shard_map/ppermute | solution.py:42
  67.5 74.1 %collective-permute-start.5 = (f32[960,256]{1,0:T(8,128)S(1)}, f32[960,256]{1,0:T(8,128)S(1)}, u32[]{:S(2)}, u32[]{:S(2)}) collective-permute-start(f32[960,256]{1,0:T(8,128)S(1)} %bitcast.24), channel_id=1, source_target_pairs={{0,16},{16,32},{32,48},{48,0},{64,80},{80,96},{96,112},{112,64},{1... | collective-permute-start | bytes 2949128 | tf_op jit(solution)/shard_map/ppermute | solution.py:42
  91.8 62.6 %collective-permute-start.6 = (f32[960,256]{1,0:T(8,128)S(1)}, f32[960,256]{1,0:T(8,128)S(1)}, u32[]{:S(2)}, u32[]{:S(2)}) collective-permute-start(f32[960,256]{1,0:T(8,128)S(1)} %bitcast.25), channel_id=1, source_target_pairs={{0,48},{16,0},{32,16},{48,32},{64,112},{80,64},{96,80},{112,96},{1... | collective-permute-start | bytes 2949128 | tf_op jit(solution)/shard_map/ppermute | solution.py:42
Sparse Core Ops, SparseCore 0:
  44.6 79.8 all-gather.1

commit v12 on v11

--- a/solution.py
+++ b/solution.py
@@ -1,6 +1,7 @@
 import jax
 import jax.numpy as jnp
 from jax import lax
+from jax.experimental import pallas as pl
 from jax.experimental.layout import Layout, with_layout_constraint
 from jax.sharding import Mesh
 from jax.sharding import PartitionSpec as P
@@ -50,7 +51,24 @@
         preferred_element_type=jnp.float32,
     )
     ladder_t = with_layout_constraint(ladder_t, Layout(major_to_minor=(0, 1)))
-    return (0.5 * ladder_t).T
+    return _scaled_transpose(ladder_t)
+
+
+def _transpose_kernel(x_ref, o_ref):
+    o_ref[...] = (0.5 * x_ref[...]).T
+
+
+def _scaled_transpose(x):
+    n, m = x.shape
+    tb = 256
+    return pl.pallas_call(
+        _transpose_kernel,
+        out_shape=jax.ShapeDtypeStruct((m, n), x.dtype),
+        grid=(pl.cdiv(m, tb),),
+        in_specs=[pl.BlockSpec((n, tb), lambda i: (0, i))],
+        out_specs=pl.BlockSpec((tb, n), lambda i: (i, 0)),
+        cost_estimate=pl.CostEstimate(flops=n * m, bytes_accessed=8 * n * m, transcendentals=0),
+    )(x)
 
 
 def solution(mesh):

time: 203 us -> 204 us (level)
  Pallas kernels: 0 us -> 9.37 us
  local copies, waits for them, and re-layouts: 37.5 us -> 28.7 us
    pallas_call x0 -> x1, Pallas kernels: none -> 9.37 us  [_scaled_transpose(): pl.pallas_call(_transpose_kernel, out_shape=jax.ShapeDtypeStruct((m, n),...]
    transpose x1 -> x0, local copies, waits for them, and re-layouts: 8.71 us -> none  [per_device(): return (0.5 * ladder_t).T]
where the time goes in v12:
time: 204 us; the launch traced here: 203 us
  waiting for transfers between devices  76.2 us (37%)
  blocking collectives  34.3 us (17%)
  matrix products  30.9 us (15%)
  local copies, waits for them, and re-layouts  28.7 us (14%)
  between operations  13.4 us (7%)
  starting transfers between devices  10.2 us (5%)
  Pallas kernels  9.37 us (5%)
    ppermute x7, waiting for transfers between devices, per_device(): got = lax.ppermute(bt, 'ga', pairs)  76.2 us
    all_to_all x1, blocking collectives, per_device(): lax.all_to_all(twice, ('ga', 'ylo'), split_axis=0, concat_axis=1, tiled=T...  34.3 us
    dot_general x1, matrix products, per_device(): lax.dot_general(full_bt, full_rows, (((1,), (1,)), ((), ())), precision=l...  30.9 us
    dynamic_update_slice x16, local copies, waits for them, and re-layouts, place(): lax.dynamic_update_slice(full_bt, blk[:, h * kw:(h + 1) * kw], (0, pos *...  20.3 us
    ppermute x7, starting transfers between devices, per_device(): got = lax.ppermute(bt, 'ga', pairs)  10.2 us
    pallas_call x1, Pallas kernels, _scaled_transpose(): pl.pallas_call(_transpose_kernel, out_shape=jax.ShapeDtypeStruct((m, n),...  9.37 us
    broadcast_in_dim x1, local copies, waits for them, and re-layouts, per_device(): full_bt = jnp.zeros((nb, bk * ng), jnp.float32)  4.85 us
  transfers between devices with their start and end apart: 8, of which 6 were waited for; matrix products, arithmetic and copies ran while one was open for 12% of the time, Pallas kernels for 0%

profile of v12, /device:TPU:1, one launch (start us, length us, event | category | flops | bytes accessed | tf_op | source)
XLA Modules:
  0.0 203.2 jit_solution(17201543896747124417)
XLA Ops:
  6.5 1.9 reshape.14
  8.8 34.3 %all_to_all.16 = f32[16,1800,16]{1,2,0:T(8,128)S(1)} all-to-all(f32[16,1800,16]{1,2,0:T(8,128)S(1)} %bitcast.13), channel_id=1, replica_groups=mesh['ga'=8,'ylo'=2,'xc'=8] {'ga','ylo'}, dimensions={0} | all-to-all | bytes 3686400 | tf_op jit(solution)/shard_map/all_to_all | solution.py:24
  43.1 1.4 copy.6
  45.1 0.9 collective-permute-start.1
  46.0 5.1 %collective-permute-start.2 = (f32[960,256]{1,0:T(8,128)S(1)}, f32[960,256]{1,0:T(8,128)}, u32[]{:S(2)}, u32[]{:S(2)}) collective-permute-start(f32[960,256]{1,0:T(8,128)S(1)} %bitcast.17), channel_id=1, source_target_pairs={{0,96},{16,112},{32,64},{48,80},{64,32},{80,48},{96,0},{112,16},{1... | collective-permute-start | bytes 2949128 | tf_op jit(solution)/shard_map/ppermute | solution.py:43
  51.2 1.0 collective-permute-start.3
  52.1 2.6 %collective-permute-start.4 = (f32[960,256]{1,0:T(8,128)S(1)}, f32[960,256]{1,0:T(8,128)S(1)}, u32[]{:S(2)}, u32[]{:S(2)}) collective-permute-start(f32[960,256]{1,0:T(8,128)S(1)} %bitcast.19), channel_id=1, source_target_pairs={{0,32},{16,48},{32,0},{48,16},{64,96},{80,112},{96,64},{112,80},{1... | collective-permute-start | bytes 2949128 | tf_op jit(solution)/shard_map/ppermute | solution.py:43
  54.7 4.8 %broadcast_in_dim.6 = f32[960,2048]{1,0:T(8,128)} broadcast(f32[]{:T(128)} %constant.154.clone.1), dimensions={} | broadcast | bytes 7864324 | tf_op jit(solution)/shard_map/broadcast_in_dim | solution.py:30
  59.6 0.9 slice_dynamic-update-slice_fusion.15
  60.5 0.9 slice_dynamic-update-slice_fusion.14
  61.4 6.1 %collective-permute-done = f32[960,256]{1,0:T(8,128)} collective-permute-done((f32[960,256]{1,0:T(8,128)S(1)}, f32[960,256]{1,0:T(8,128)}, u32[]{:S(2)}, u32[]{:S(2)}) %collective-permute-start) | collective-permute-done | bytes 983072 | tf_op jit(solution)/shard_map/ppermute | solution.py:43
  67.5 2.0 slice_dynamic-update-slice_fusion.13
  69.4 2.0 slice_dynamic-update-slice_fusion.12
  71.4 20.4 %collective-permute-done.1 = f32[960,256]{1,0:T(8,128)} collective-permute-done((f32[960,256]{1,0:T(8,128)S(1)}, f32[960,256]{1,0:T(8,128)}, u32[]{:S(2)}, u32[]{:S(2)}) %collective-permute-start.1) | collective-permute-done | bytes 983072 | tf_op jit(solution)/shard_map/ppermute | solution.py:43
  91.8 1.9 slice_dynamic-update-slice_fusion.11
  93.7 1.9 slice_dynamic-update-slice_fusion.10
  95.6 15.4 %collective-permute-done.2 = f32[960,256]{1,0:T(8,128)} collective-permute-done((f32[960,256]{1,0:T(8,128)S(1)}, f32[960,256]{1,0:T(8,128)}, u32[]{:S(2)}, u32[]{:S(2)}) %collective-permute-start.2) | collective-permute-done | bytes 983072 | tf_op jit(solution)/shard_map/ppermute | solution.py:43
  111.0 1.9 slice_dynamic-update-slice_fusion.9
  112.9 1.9 slice_dynamic-update-slice_fusion.8
  114.8 15.4 %collective-permute-done.3 = f32[960,256]{1,0:T(8,128)S(1)} collective-permute-done((f32[960,256]{1,0:T(8,128)S(1)}, f32[960,256]{1,0:T(8,128)S(1)}, u32[]{:S(2)}, u32[]{:S(2)}) %collective-permute-start.3) | collective-permute-done | bytes 983072 | tf_op jit(solution)/shard_map/ppermute | solution.py:43
  130.2 0.8 slice_dynamic-update-slice_fusion.7
  131.0 0.9 slice_dynamic-update-slice_fusion.6
  131.9 0.9 slice_dynamic-update-slice_fusion.5
  132.8 0.9 slice_dynamic-update-slice_fusion.4
  133.7 7.9 %collective-permute-done.5 = f32[960,256]{1,0:T(8,128)S(1)} collective-permute-done((f32[960,256]{1,0:T(8,128)S(1)}, f32[960,256]{1,0:T(8,128)S(1)}, u32[]{:S(2)}, u32[]{:S(2)}) %collective-permute-start.5) | collective-permute-done | bytes 983072 | tf_op jit(solution)/shard_map/ppermute | solution.py:43
  141.5 0.9 slice_dynamic-update-slice_fusion.3
  142.4 0.9 slice_dynamic-update-slice_fusion.2
  143.3 11.1 %collective-permute-done.6 = f32[960,256]{1,0:T(8,128)S(1)} collective-permute-done((f32[960,256]{1,0:T(8,128)S(1)}, f32[960,256]{1,0:T(8,128)S(1)}, u32[]{:S(2)}, u32[]{:S(2)}) %collective-permute-start.6) | collective-permute-done | bytes 983072 | tf_op jit(solution)/shard_map/ppermute | solution.py:43
  154.3 0.9 slice_dynamic-update-slice_fusion.1
  155.2 0.8 slice_dynamic-update-slice_fusion
  156.1 30.9 %fusion.x_ref = f32[960,1800]{1,0:T(8,128)} fusion(f32[960,2048]{1,0:T(8,128)} %slice_dynamic-update-slice_fusion, f32[1800,2048]{0,1:T(8,128)} %all-gather.2.cloned.1.call-done), kind=kOutput, calls=%fused_computation.16 | convolution fusion | flops 21233664000 | bytes 29521920 | tf_op jit(solution)/shard_map/dot_general | solution.py:46
  187.0 9.4 %shard_map.28 = f32[1800,960]{1,0:T(8,128)} custom-call(f32[960,1800]{1,0:T(8,128)} %fusion.x_ref), custom_call_target="tpu_custom_call" | custom-call | flops 1728000 | bytes 13824000 | tf_op jit(solution)/shard_map/pallas_call | solution.py:64
  (11 shorter events, 0.9 us)
Async XLA Ops:
  6.5 38.0 %copy-start = (f32[256,960]{0,1:T(8,128)S(1)}, f32[256,960]{0,1:T(8,128)}, u32[]{:S(2)}) copy-start(f32[256,960]{0,1:T(8,128)} %param.3) | copy-start | bytes 2949124
  6.5 149.6 %all-gather.2.cloned.1.call-start = ((), (), s32[]{:S(2)}) async-start(), calls=%async_computation.1 | async-start | bytes 17694720 | tf_op jit(solution)/shard_map/all_gather | solution.py:27
  44.5 22.9 %collective-permute-start = (f32[960,256]{1,0:T(8,128)S(1)}, f32[960,256]{1,0:T(8,128)}, u32[]{:S(2)}, u32[]{:S(2)}) collective-permute-start(f32[960,256]{1,0:T(8,128)S(1)} %bitcast.15), channel_id=1, source_target_pairs={{0,64},{16,80},{32,96},{48,112},{64,0},{80,16},{96,32},{112,48},{1... | collective-permute-start | bytes 2949128 | tf_op jit(solution)/shard_map/ppermute | solution.py:43
  45.1 46.7 %collective-permute-start.1 = (f32[960,256]{1,0:T(8,128)S(1)}, f32[960,256]{1,0:T(8,128)}, u32[]{:S(2)}, u32[]{:S(2)}) collective-permute-start(f32[960,256]{1,0:T(8,128)S(1)} %bitcast.16), channel_id=1, source_target_pairs={{0,80},{16,96},{32,112},{48,64},{64,16},{80,32},{96,48},{112,0},{1... | collective-permute-start | bytes 2949128 | tf_op jit(solution)/shard_map/ppermute | solution.py:43
  46.0 65.0 %collective-permute-start.2 = (f32[960,256]{1,0:T(8,128)S(1)}, f32[960,256]{1,0:T(8,128)}, u32[]{:S(2)}, u32[]{:S(2)}) collective-permute-start(f32[960,256]{1,0:T(8,128)S(1)} %bitcast.17), channel_id=1, source_target_pairs={{0,96},{16,112},{32,64},{48,80},{64,32},{80,48},{96,0},{112,16},{1... | collective-permute-start | bytes 2949128 | tf_op jit(solution)/shard_map/ppermute | solution.py:43
  51.2 79.0 %collective-permute-start.3 = (f32[960,256]{1,0:T(8,128)S(1)}, f32[960,256]{1,0:T(8,128)S(1)}, u32[]{:S(2)}, u32[]{:S(2)}) collective-permute-start(f32[960,256]{1,0:T(8,128)S(1)} %bitcast.18), channel_id=1, source_target_pairs={{0,112},{16,64},{32,80},{48,96},{64,48},{80,0},{96,16},{112,32},{1... | collective-permute-start | bytes 2949128 | tf_op jit(solution)/shard_map/ppermute | solution.py:43
  52.1 79.8 %collective-permute-start.4 = (f32[960,256]{1,0:T(8,128)S(1)}, f32[960,256]{1,0:T(8,128)S(1)}, u32[]{:S(2)}, u32[]{:S(2)}) collective-permute-start(f32[960,256]{1,0:T(8,128)S(1)} %bitcast.19), channel_id=1, source_target_pairs={{0,32},{16,48},{32,0},{48,16},{64,96},{80,112},{96,64},{112,80},{1... | collective-permute-start | bytes 2949128 | tf_op jit(solution)/shard_map/ppermute | solution.py:43
  67.5 74.1 %collective-permute-start.5 = (f32[960,256]{1,0:T(8,128)S(1)}, f32[960,256]{1,0:T(8,128)S(1)}, u32[]{:S(2)}, u32[]{:S(2)}) collective-permute-start(f32[960,256]{1,0:T(8,128)S(1)} %bitcast.22), channel_id=1, source_target_pairs={{0,16},{16,32},{32,48},{48,0},{64,80},{80,96},{96,112},{112,64},{1... | collective-permute-start | bytes 2949128 | tf_op jit(solution)/shard_map/ppermute | solution.py:43
  91.8 62.6 %collective-permute-start.6 = (f32[960,256]{1,0:T(8,128)S(1)}, f32[960,256]{1,0:T(8,128)S(1)}, u32[]{:S(2)}, u32[]{:S(2)}) collective-permute-start(f32[960,256]{1,0:T(8,128)S(1)} %bitcast.23), channel_id=1, source_target_pairs={{0,48},{16,0},{32,16},{48,32},{64,112},{80,64},{96,80},{112,96},{1... | collective-permute-start | bytes 2949128 | tf_op jit(solution)/shard_map/ppermute | solution.py:43
Sparse Core Ops, SparseCore 0:
  44.6 79.8 all-gather.1

commit v13 on v11

--- a/solution.py
+++ b/solution.py
@@ -36,16 +36,13 @@
             full_bt = lax.dynamic_update_slice(full_bt, blk[:, h * kw:(h + 1) * kw], (0, pos * kw))
         return full_bt
 
-    full_bt = place(full_bt, bt, g)
-    for dy, dz in offsets:
-        pairs = [(i, ((i // nz + dy) % 2) * nz + (i % nz + dz) % nz) for i in range(ng)]
-        got = lax.ppermute(bt, "ga", pairs)
-        src = lax.rem(yh + dy, 2) * nz + lax.rem(z - dz + nz, nz)
-        full_bt = place(full_bt, got, src)
+    got = lax.all_to_all(jnp.broadcast_to(bt, (ng,) + bt.shape), "ga", 0, 0, tiled=True)
+    rows = full_rows.shape[0]
+    a_k = full_rows.reshape(rows, nxc, 2, kw).transpose(0, 2, 1, 3).reshape(rows, ng, bk)
     ladder_t = lax.dot_general(
-        full_bt,
-        full_rows,
-        (((1,), (1,)), ((), ())),
+        got,
+        a_k,
+        (((0, 2), (1, 2)), ((), ())),
         precision=lax.Precision.HIGH,
         preferred_element_type=jnp.float32,
     )

time: 203 us -> 207 us (1.020)
  local copies, waits for them, and re-layouts: 37.5 us -> 48.8 us
  starting transfers between devices: 10.2 us -> 4.91 us
  waiting for transfers between devices: 76.2 us -> 71.4 us
  matrix products: 30.9 us -> 33.5 us
    ppermute x7 -> x0, waiting for transfers between devices: 76.2 us -> none  [per_device(): got = lax.ppermute(bt, 'ga', pairs)]
    all_gather x1, waiting for transfers between devices: 0.01 us -> 71.4 us  [per_device(): full_rows = lax.all_gather(pair, 'xc', axis=1, tiled=True)]
    reshape x0 -> x2, local copies, waits for them, and re-layouts: none -> 32.8 us  [per_device(): full_rows.reshape(rows, nxc, 2, kw).transpose(0, 2, 1, 3)]
    dynamic_update_slice x16 -> x0, local copies, waits for them, and re-layouts: 20.3 us -> none  [place(): lax.dynamic_update_slice(full_bt, blk[:, h * kw:(h + 1) * kw], (0, pos *...]
    ppermute x7 -> x0, starting transfers between devices: 10.2 us -> none  [per_device(): got = lax.ppermute(bt, 'ga', pairs)]
    all_to_all x0 -> x1, starting transfers between devices: none -> 4.9 us  [per_device(): lax.all_to_all(jnp.broadcast_to(bt, (ng,) + bt.shape), 'ga', 0, 0, tiled=...]
    dot_general x1, matrix products: 30.9 us -> 33.5 us  [per_device(): lax.dot_general(got, a_k, (((0, 2), (1, 2)), ((), ())), precision=lax.Pre...]
  transfers between devices with their start and end apart: 8 -> 2, of which waited for: 6 -> 1; matrix products, arithmetic and copies ran while one was open for 12% -> 18% of each run, Pallas kernels for 0% -> 0%
where the time goes in v13:
time: 207 us; the launch traced here: 206 us
  waiting for transfers between devices  71.4 us (34%)
  local copies, waits for them, and re-layouts  48.8 us (24%)
  blocking collectives  34.3 us (17%)
  matrix products  33.5 us (16%)
  between operations  13.4 us (6%)
  starting transfers between devices  4.91 us (2%)
    all_gather x1, waiting for transfers between devices, per_device(): full_rows = lax.all_gather(pair, 'xc', axis=1, tiled=True)  71.4 us
    all_to_all x1, blocking collectives, per_device(): lax.all_to_all(twice, ('ga', 'ylo'), split_axis=0, concat_axis=1, tiled=T...  34.3 us
    dot_general x1, matrix products, per_device(): lax.dot_general(got, a_k, (((0, 2), (1, 2)), ((), ())), precision=lax.Pre...  33.5 us
    reshape x2, local copies, waits for them, and re-layouts, per_device(): full_rows.reshape(rows, nxc, 2, kw).transpose(0, 2, 1, 3)  32.8 us
    transpose x1, local copies, waits for them, and re-layouts, per_device(): return (0.5 * ladder_t).T  8.71 us
    all_to_all x1, starting transfers between devices, per_device(): lax.all_to_all(jnp.broadcast_to(bt, (ng,) + bt.shape), 'ga', 0, 0, tiled=...  4.9 us
  transfers between devices with their start and end apart: 2, of which 1 were waited for; matrix products, arithmetic and copies ran while one was open for 18% of the time, Pallas kernels for 0%

profile of v13, /device:TPU:1, one launch (start us, length us, event | category | flops | bytes accessed | tf_op | source)
XLA Modules:
  0.0 206.4 jit_solution(4007898617263082059)
XLA Ops:
  6.5 0.0 copy-start
  6.5 0.0 all-gather.2.cloned.1.call-start
  6.5 1.9 reshape.20
  8.4 0.2 copy.9
  8.6 0.1 broadcast_in_dim.7
  8.8 34.3 %all_to_all.21 = f32[16,1800,16]{1,2,0:T(8,128)S(1)} all-to-all(f32[16,1800,16]{1,2,0:T(8,128)S(1)} %bitcast.24), channel_id=1, replica_groups=mesh['ga'=8,'ylo'=2,'xc'=8] {'ga','ylo'}, dimensions={0} | all-to-all | bytes 3686400 | tf_op jit(solution)/shard_map/all_to_all | solution.py:23
  43.1 1.4 copy.10
  44.5 0.0 all-gather.2.cloned.1.call-update
  44.5 0.0 copy-done
  44.5 3.7 %broadcast_in_dim.6 = f32[8,960,256]{2,1,0:T(8,128)} broadcast(f32[960,256]{1,0:T(8,128)S(1)} %bitcast.26), dimensions={1,2} | broadcast | bytes 8847360 | tf_op jit(solution)/shard_map/broadcast_in_dim | solution.py:39
  48.2 4.9 %all-to-all-start = ((f32[8,960,256]{2,1,0:T(8,128)}), f32[8,960,256]{2,1,0:T(8,128)}, u32[]{:S(2)}, u32[]{:S(2)}) async-start(f32[8,960,256]{2,1,0:T(8,128)} %broadcast_in_dim.6), calls=%async_computation | async-start | bytes 15728640 | tf_op jit(solution)/shard_map/all_to_all | solution.py:39
  53.2 71.4 %all-gather.2.cloned.1.call-done = f32[1800,2048]{0,1:T(8,128)} async-done(((f32[1800,256]{0,1:T(8,128)}), f32[1800,2048]{0,1:T(8,128)}) %all-gather.2.cloned.1.call-update) | async-done | bytes 14745616 | tf_op jit(solution)/shard_map/all_gather | solution.py:26
  124.5 15.6 %copy.11 = f32[1800,8,2,128]{3,1,2,0:T(8,128)} copy(f32[1800,8,2,128]{0,3,2,1:T(8,128)} %bitcast.22) | data formatting | bytes 29491200 | tf_op jit(solution)/shard_map/reshape | solution.py:41
  140.2 17.1 %reshape.24 = f32[1800,8,256]{2,1,0:T(8,128)} reshape(f32[1800,2,8,128]{3,2,1,0:T(8,128)} %bitcast.21) | data formatting | bytes 29491200 | tf_op jit(solution)/shard_map/reshape | solution.py:41
  157.3 0.0 all-to-all-done
  157.3 33.5 %fusion.2 = f32[1800,960]{0,1:T(8,128)} fusion(f32[8,960,256]{2,1,0:T(8,128)} %all-to-all-done, f32[1800,8,256]{2,1,0:T(8,128)} %reshape.24), kind=kOutput, calls=%fused_computation.3 | convolution fusion | flops 21235392512 | bytes 29521920 | tf_op jit(solution)/shard_map/dot_general | solution.py:42
  190.8 8.7 %copy.13 = f32[1800,960]{1,0:T(8,128)} copy(f32[1800,960]{0,1:T(8,128)} %fusion.2) | data formatting | bytes 13824000 | tf_op jit(solution)/shard_map/transpose | solution.py:50
Async XLA Ops:
  6.5 38.0 %copy-start = (f32[256,960]{0,1:T(8,128)S(1)}, f32[256,960]{0,1:T(8,128)}, u32[]{:S(2)}) copy-start(f32[256,960]{0,1:T(8,128)} %param.3) | copy-start | bytes 2949124
  6.5 118.0 %all-gather.2.cloned.1.call-start = ((), (), s32[]{:S(2)}) async-start(), calls=%async_computation.2 | async-start | bytes 17694720 | tf_op jit(solution)/shard_map/all_gather | solution.py:26
  48.2 109.0 %all-to-all-start = ((f32[8,960,256]{2,1,0:T(8,128)}), f32[8,960,256]{2,1,0:T(8,128)}, u32[]{:S(2)}, u32[]{:S(2)}) async-start(f32[8,960,256]{2,1,0:T(8,128)} %broadcast_in_dim.6), calls=%async_computation | async-start | bytes 15728640 | tf_op jit(solution)/shard_map/all_to_all | solution.py:39
Sparse Core Ops, SparseCore 0:
  44.6 79.8 all-gather.1

commit v14 on v13

--- a/solution.py
+++ b/solution.py
@@ -37,12 +37,13 @@
         return full_bt
 
     got = lax.all_to_all(jnp.broadcast_to(bt, (ng,) + bt.shape), "ga", 0, 0, tiled=True)
-    rows = full_rows.shape[0]
-    a_k = full_rows.reshape(rows, nxc, 2, kw).transpose(0, 2, 1, 3).reshape(rows, ng, bk)
+    hx = nxc // 2
+    full_bt = got.reshape(2, hx, nb, per, kw).transpose(2, 1, 3, 0, 4).reshape(nb, ng * bk)
+    a_k = full_rows
     ladder_t = lax.dot_general(
-        got,
+        full_bt,
         a_k,
-        (((0, 2), (1, 2)), ((), ())),
+        (((1,), (1,)), ((), ())),
         precision=lax.Precision.HIGH,
         preferred_element_type=jnp.float32,
     )

time: 207 us -> 220 us (1.063); the launches traced: 206 us -> 217 us
  blocking collectives: 34.3 us -> 126 us
  waiting for transfers between devices: 71.4 us -> 0.02 us
  starting transfers between devices: 4.91 us -> 0.01 us
  matrix products: 33.5 us -> 31 us
    all_to_all x0 -> x1, blocking collectives: none -> 91.5 us  [per_device(): lax.all_to_all(jnp.broadcast_to(bt, (ng,) + bt.shape), 'ga', 0, 0, tiled=...]
    all_gather x1, waiting for transfers between devices: 71.4 us -> 0.01 us  [per_device(): full_rows = lax.all_gather(pair, 'xc', axis=1, tiled=True)]
    transpose x0 -> x1, local copies, waits for them, and re-layouts: none -> 12.5 us  [per_device(): got.reshape(2, hx, nb, per, kw).transpose(2, 1, 3, 0, 4)]
    reshape x2, local copies, waits for them, and re-layouts: 32.8 us -> 21.2 us  [per_device(): got.reshape(2, hx, nb, per, kw).transpose(2, 1, 3, 0, 4)]
    all_to_all x1 -> x0, starting transfers between devices: 4.9 us -> none  [per_device(): lax.all_to_all(jnp.broadcast_to(bt, (ng,) + bt.shape), 'ga', 0, 0, tiled=...]
    broadcast_in_dim x1, local copies, waits for them, and re-layouts: 3.71 us -> 0.67 us  [per_device(): jnp.broadcast_to(bt, (ng,) + bt.shape)]
    dot_general x1, matrix products: 33.5 us -> 31 us  [per_device(): lax.dot_general(full_bt, a_k, (((1,), (1,)), ((), ())), precision=lax.Pre...]
  transfers between devices with their start and end apart: 2 -> 1, of which waited for: 1 -> 0; matrix products, arithmetic and copies ran while one was open for 18% -> 16% of each run, Pallas kernels for 0% -> 0%
where the time goes in v14:
time: 220 us; the launch traced here: 217 us
  blocking collectives  126 us (57%)
  local copies, waits for them, and re-layouts  46.7 us (21%)
  matrix products  31 us (14%)
  between operations  13.4 us (6%)
    all_to_all x1, blocking collectives, per_device(): lax.all_to_all(jnp.broadcast_to(bt, (ng,) + bt.shape), 'ga', 0, 0, tiled=...  91.5 us
    all_to_all x1, blocking collectives, per_device(): lax.all_to_all(twice, ('ga', 'ylo'), split_axis=0, concat_axis=1, tiled=T...  34.3 us
    dot_general x1, matrix products, per_device(): lax.dot_general(full_bt, a_k, (((1,), (1,)), ((), ())), precision=lax.Pre...  31 us
    reshape x2, local copies, waits for them, and re-layouts, per_device(): got.reshape(2, hx, nb, per, kw).transpose(2, 1, 3, 0, 4)  21.2 us
    transpose x1, local copies, waits for them, and re-layouts, per_device(): got.reshape(2, hx, nb, per, kw).transpose(2, 1, 3, 0, 4)  12.5 us
    transpose x1, local copies, waits for them, and re-layouts, per_device(): return (0.5 * ladder_t).T  8.71 us
  transfers between devices with their start and end apart: 1, of which 0 were waited for; matrix products, arithmetic and copies ran while one was open for 16% of the time, Pallas kernels for 0%

profile of v14, /device:TPU:1, one launch (start us, length us, event | category | flops | bytes accessed | tf_op | source)
XLA Modules:
  0.0 217.0 jit_solution(7055886722259368166)
XLA Ops:
  6.5 0.0 copy-start
  6.5 0.0 all-gather.2.cloned.1.call-start
  6.5 1.9 reshape.22
  8.4 0.2 copy.8
  8.6 0.1 broadcast_in_dim.7
  8.8 34.3 %all_to_all.21 = f32[16,1800,16]{1,2,0:T(8,128)S(1)} all-to-all(f32[16,1800,16]{1,2,0:T(8,128)S(1)} %bitcast.17), channel_id=1, replica_groups=mesh['ga'=8,'ylo'=2,'xc'=8] {'ga','ylo'}, dimensions={0} | all-to-all | bytes 3686400 | tf_op jit(solution)/shard_map/all_to_all | solution.py:23
  43.1 1.4 copy.9
  44.5 0.0 all-gather.2.cloned.1.call-update
  44.5 0.0 copy-done
  44.5 0.7 broadcast_in_dim.6
  45.2 91.5 %all_to_all.22 = f32[8,960,256]{2,1,0:T(8,128)} all-to-all(f32[8,960,256]{2,1,0:T(8,128)S(1)} %broadcast_in_dim.6), channel_id=1, replica_groups=mesh['ga'=8,'ylo'=2,'xc'=8] {'ga'}, dimensions={0} | all-to-all | bytes 15728640 | tf_op jit(solution)/shard_map/all_to_all | solution.py:39
  136.7 10.4 %reshape.20 = f32[2,4,960,2,128]{4,3,2,1,0:T(2,128)} reshape(f32[8,960,256]{2,1,0:T(8,128)} %all_to_all.22) | data formatting | bytes 15728640 | tf_op jit(solution)/shard_map/reshape | solution.py:41
  147.2 12.5 %copy.7 = f32[960,4,2,2,128]{4,3,2,1,0:T(2,128)} copy(f32[960,4,2,2,128]{4,2,0,1,3:T(2,128)} %bitcast.15) | data formatting | bytes 15728640 | tf_op jit(solution)/shard_map/transpose | solution.py:41
  159.6 10.8 %reshape.21 = f32[960,2048]{1,0:T(8,128)} reshape(f32[960,4,2,2,128]{4,3,2,1,0:T(2,128)} %copy.7) | data formatting | bytes 15728640 | tf_op jit(solution)/shard_map/reshape | solution.py:41
  170.4 0.0 all-gather.2.cloned.1.call-done
  170.4 31.0 %multiply_bitcast_fusion = f32[1800,960]{0,1:T(8,128)} fusion(f32[960,2048]{1,0:T(8,128)} %reshape.21, f32[1800,2048]{0,1:T(8,128)} %all-gather.2.cloned.1.call-done), kind=kOutput, calls=%fused_computation | convolution fusion | flops 21235392512 | bytes 29521920 | tf_op jit(solution)/shard_map/dot_general | solution.py:43
  201.4 8.7 %copy.10 = f32[1800,960]{1,0:T(8,128)} copy(f32[1800,960]{0,1:T(8,128)} %multiply_bitcast_fusion) | data formatting | bytes 13824000 | tf_op jit(solution)/shard_map/transpose | solution.py:51
Async XLA Ops:
  6.5 38.0 %copy-start = (f32[256,960]{0,1:T(8,128)S(1)}, f32[256,960]{0,1:T(8,128)}, u32[]{:S(2)}) copy-start(f32[256,960]{0,1:T(8,128)} %param.3) | copy-start | bytes 2949124
  6.5 163.9 %all-gather.2.cloned.1.call-start = ((), (), s32[]{:S(2)}) async-start(), calls=%async_computation.2 | async-start | bytes 17694720 | tf_op jit(solution)/shard_map/all_gather | solution.py:26
Sparse Core Ops, SparseCore 0:
  44.6 79.8 all-gather.1

commit v15 on v14

--- a/solution.py
+++ b/solution.py
@@ -1,6 +1,7 @@
 import jax
 import jax.numpy as jnp
 from jax import lax
+from jax.experimental import pallas as pl
 from jax.experimental.layout import Layout, with_layout_constraint
 from jax.sharding import Mesh
 from jax.sharding import PartitionSpec as P
@@ -10,6 +11,10 @@
     nz = ng // 2
     offsets = [(1, dz) for dz in range(nz)] + [(0, dz) for dz in range(nz // 2, 0, -1)]
     return nz, offsets + [(0, dz) for dz in range(nz // 2 + 1, nz)]
+
+
+def _copy_kernel(x_ref, o_ref):
+    o_ref[...] = x_ref[...]
 
 
 def per_device(ng, nxc, amplitudes, integrals):
@@ -37,8 +42,15 @@
         return full_bt
 
     got = lax.all_to_all(jnp.broadcast_to(bt, (ng,) + bt.shape), "ga", 0, 0, tiled=True)
-    hx = nxc // 2
-    full_bt = got.reshape(2, hx, nb, per, kw).transpose(2, 1, 3, 0, 4).reshape(nb, ng * bk)
+    nblk = ng * per
+    full_bt = pl.pallas_call(
+        _copy_kernel,
+        out_shape=jax.ShapeDtypeStruct((nb, ng * bk), jnp.float32),
+        grid=(nblk,),
+        in_specs=[pl.BlockSpec((None, nb, kw), lambda i: (i // per, 0, i % per))],
+        out_specs=pl.BlockSpec((nb, kw), lambda i: (0, (i % nxc) * 2 + i // nxc)),
+        cost_estimate=pl.CostEstimate(flops=0, bytes_accessed=8 * nb * ng * bk, transcendentals=0),
+    )(got)
     a_k = full_rows
     ladder_t = lax.dot_general(
         full_bt,

time: 220 us -> 198 us (0.900)
  local copies, waits for them, and re-layouts: 46.7 us -> 13 us
  Pallas kernels: 0 us -> 11.9 us
    reshape x2 -> x0, local copies, waits for them, and re-layouts: 21.2 us -> none  [per_device(): got.reshape(2, hx, nb, per, kw).transpose(2, 1, 3, 0, 4)]
    transpose x1 -> x0, local copies, waits for them, and re-layouts: 12.5 us -> none  [per_device(): got.reshape(2, hx, nb, per, kw).transpose(2, 1, 3, 0, 4)]
    pallas_call x0 -> x1, Pallas kernels: none -> 11.9 us  [per_device(): pl.pallas_call(_copy_kernel, out_shape=jax.ShapeDtypeStruct((nb, ng * bk)...]
  transfers between devices with their start and end apart: 1 -> 1, of which waited for: 0 -> 0; matrix products, arithmetic and copies ran while one was open for 16% -> 0% of each run, Pallas kernels for 0% -> 6%
where the time goes in v15:
time: 198 us; the launch traced here: 195 us
  blocking collectives  126 us (64%)
  matrix products  31 us (16%)
  between operations  13.4 us (7%)
  local copies, waits for them, and re-layouts  13 us (7%)
  Pallas kernels  11.9 us (6%)
    all_to_all x1, blocking collectives, per_device(): lax.all_to_all(jnp.broadcast_to(bt, (ng,) + bt.shape), 'ga', 0, 0, tiled=...  91.5 us
    all_to_all x1, blocking collectives, per_device(): lax.all_to_all(twice, ('ga', 'ylo'), split_axis=0, concat_axis=1, tiled=T...  34.3 us
    dot_general x1, matrix products, per_device(): lax.dot_general(full_bt, a_k, (((1,), (1,)), ((), ())), precision=lax.Pre...  31 us
    pallas_call x1, Pallas kernels, per_device(): pl.pallas_call(_copy_kernel, out_shape=jax.ShapeDtypeStruct((nb, ng * bk)...  11.9 us
    transpose x1, local copies, waits for them, and re-layouts, per_device(): return (0.5 * ladder_t).T  8.71 us
  transfers between devices with their start and end apart: 1, of which 0 were waited for; matrix products, arithmetic and copies ran while one was open for 0% of the time, Pallas kernels for 6%

profile of v15, /device:TPU:1, one launch (start us, length us, event | category | flops | bytes accessed | tf_op | source)
XLA Modules:
  0.0 195.1 jit_solution(6073658891903295519)
XLA Ops:
  6.5 0.0 copy-start
  6.5 0.0 all-gather.2.cloned.1.call-start
  6.5 1.9 reshape.14
  8.4 0.2 copy.7
  8.6 0.1 broadcast_in_dim.7
  8.8 34.3 %all_to_all.21 = f32[16,1800,16]{1,2,0:T(8,128)S(1)} all-to-all(f32[16,1800,16]{1,2,0:T(8,128)S(1)} %bitcast.15), channel_id=1, replica_groups=mesh['ga'=8,'ylo'=2,'xc'=8] {'ga','ylo'}, dimensions={0} | all-to-all | bytes 3686400 | tf_op jit(solution)/shard_map/all_to_all | solution.py:28
  43.1 1.4 copy.8
  44.5 0.0 all-gather.2.cloned.1.call-update
  44.5 0.0 copy-done
  44.5 0.7 broadcast_in_dim.6
  45.2 91.5 %all_to_all.22.x_ref = f32[8,960,256]{2,1,0:T(8,128)} all-to-all(f32[8,960,256]{2,1,0:T(8,128)S(1)} %broadcast_in_dim.6), channel_id=1, replica_groups=mesh['ga'=8,'ylo'=2,'xc'=8] {'ga'}, dimensions={0} | all-to-all | bytes 15728640 | tf_op jit(solution)/shard_map/all_to_all | solution.py:44
  136.7 11.9 %shard_map.28 = f32[960,2048]{1,0:T(8,128)} custom-call(f32[8,960,256]{2,1,0:T(8,128)} %all_to_all.22.x_ref), custom_call_target="tpu_custom_call" | custom-call | bytes 15728640 | tf_op jit(solution)/shard_map/pallas_call | solution.py:46
  148.6 0.0 all-gather.2.cloned.1.call-done
  148.6 31.0 %multiply_bitcast_fusion = f32[1800,960]{0,1:T(8,128)} fusion(f32[960,2048]{1,0:T(8,128)} %shard_map.28, f32[1800,2048]{0,1:T(8,128)} %all-gather.2.cloned.1.call-done), kind=kOutput, calls=%fused_computation | convolution fusion | flops 21235392512 | bytes 29521920 | tf_op jit(solution)/shard_map/dot_general | solution.py:55
  179.6 8.7 %copy.9 = f32[1800,960]{1,0:T(8,128)} copy(f32[1800,960]{0,1:T(8,128)} %multiply_bitcast_fusion) | data formatting | bytes 13824000 | tf_op jit(solution)/shard_map/transpose | solution.py:63
Async XLA Ops:
  6.5 38.0 %copy-start = (f32[256,960]{0,1:T(8,128)S(1)}, f32[256,960]{0,1:T(8,128)}, u32[]{:S(2)}) copy-start(f32[256,960]{0,1:T(8,128)} %param.3) | copy-start | bytes 2949124
  6.5 142.1 %all-gather.2.cloned.1.call-start = ((), (), s32[]{:S(2)}) async-start(), calls=%async_computation.2 | async-start | bytes 17694720 | tf_op jit(solution)/shard_map/all_gather | solution.py:31
Sparse Core Ops, SparseCore 0:
  44.6 79.8 all-gather.1

commit v16 on v15

--- a/solution.py
+++ b/solution.py
@@ -1,7 +1,10 @@
+import functools
+
 import jax
 import jax.numpy as jnp
 from jax import lax
 from jax.experimental import pallas as pl
+from jax.experimental.pallas import tpu as pltpu
 from jax.experimental.layout import Layout, with_layout_constraint
 from jax.sharding import Mesh
 from jax.sharding import PartitionSpec as P
@@ -13,8 +16,10 @@
     return nz, offsets + [(0, dz) for dz in range(nz // 2 + 1, nz)]
 
 
-def _copy_kernel(x_ref, o_ref):
-    o_ref[...] = x_ref[...]
+def _order_kernel(nxc, per, kw, x_ref, o_ref):
+    for kb in range(x_ref.shape[0] * per):
+        p = (kb % nxc) * 2 + kb // nxc
+        o_ref[:, p * kw:(p + 1) * kw] = x_ref[kb // per, :, (kb % per) * kw:(kb % per + 1) * kw]
 
 
 def per_device(ng, nxc, amplitudes, integrals):
@@ -42,13 +47,11 @@
         return full_bt
 
     got = lax.all_to_all(jnp.broadcast_to(bt, (ng,) + bt.shape), "ga", 0, 0, tiled=True)
-    nblk = ng * per
     full_bt = pl.pallas_call(
-        _copy_kernel,
+        functools.partial(_order_kernel, nxc, per, kw),
         out_shape=jax.ShapeDtypeStruct((nb, ng * bk), jnp.float32),
-        grid=(nblk,),
-        in_specs=[pl.BlockSpec((None, nb, kw), lambda i: (i // per, 0, i % per))],
-        out_specs=pl.BlockSpec((nb, kw), lambda i: (0, (i % nxc) * 2 + i // nxc)),
+        in_specs=[pl.BlockSpec(memory_space=pltpu.VMEM)],
+        out_specs=pl.BlockSpec(memory_space=pltpu.VMEM),
         cost_estimate=pl.CostEstimate(flops=0, bytes_accessed=8 * nb * ng * bk, transcendentals=0),
     )(got)
     a_k = full_rows

time: 198 us -> 193 us (0.975)
  Pallas kernels: 11.9 us -> 7.42 us
    pallas_call x1, Pallas kernels: 11.9 us -> 7.42 us  [per_device(): pl.pallas_call(functools.partial(_order_kernel, nxc, per, kw), out_shape=...]
  transfers between devices with their start and end apart: 1 -> 1, of which waited for: 0 -> 0; matrix products, arithmetic and copies ran while one was open for 0% -> 0% of each run, Pallas kernels for 6% -> 4%
where the time goes in v16:
time: 193 us; the launch traced here: 191 us
  blocking collectives  126 us (65%)
  matrix products  31 us (16%)
  between operations  13.4 us (7%)
  local copies, waits for them, and re-layouts  13 us (7%)
  Pallas kernels  7.42 us (4%)
    all_to_all x1, blocking collectives, per_device(): lax.all_to_all(jnp.broadcast_to(bt, (ng,) + bt.shape), 'ga', 0, 0, tiled=...  91.5 us
    all_to_all x1, blocking collectives, per_device(): lax.all_to_all(twice, ('ga', 'ylo'), split_axis=0, concat_axis=1, tiled=T...  34.3 us
    dot_general x1, matrix products, per_device(): lax.dot_general(full_bt, a_k, (((1,), (1,)), ((), ())), precision=lax.Pre...  31 us
    transpose x1, local copies, waits for them, and re-layouts, per_device(): return (0.5 * ladder_t).T  8.71 us
    pallas_call x1, Pallas kernels, per_device(): pl.pallas_call(functools.partial(_order_kernel, nxc, per, kw), out_shape=...  7.42 us
  transfers between devices with their start and end apart: 1, of which 0 were waited for; matrix products, arithmetic and copies ran while one was open for 0% of the time, Pallas kernels for 4%

profile of v16, /device:TPU:1, one launch (start us, length us, event | category | flops | bytes accessed | tf_op | source)
XLA Modules:
  0.0 190.7 jit_solution(5447654099545374401)
XLA Ops:
  6.5 0.0 copy-start
  6.5 0.0 all-gather.2.cloned.1.call-start
  6.5 1.9 reshape.14
  8.4 0.2 copy.7
  8.6 0.1 broadcast_in_dim.7
  8.8 34.3 %all_to_all.21 = f32[16,1800,16]{1,2,0:T(8,128)S(1)} all-to-all(f32[16,1800,16]{1,2,0:T(8,128)S(1)} %bitcast.15), channel_id=1, replica_groups=mesh['ga'=8,'ylo'=2,'xc'=8] {'ga','ylo'}, dimensions={0} | all-to-all | bytes 3686400 | tf_op jit(solution)/shard_map/all_to_all | solution.py:33
  43.1 1.4 copy.8
  44.5 0.0 all-gather.2.cloned.1.call-update
  44.5 0.0 copy-done
  44.5 0.7 broadcast_in_dim.6
  45.2 91.5 %all_to_all.22.x_ref = f32[8,960,256]{2,1,0:T(8,128)} all-to-all(f32[8,960,256]{2,1,0:T(8,128)S(1)} %broadcast_in_dim.6), channel_id=1, replica_groups=mesh['ga'=8,'ylo'=2,'xc'=8] {'ga'}, dimensions={0} | all-to-all | bytes 15728640 | tf_op jit(solution)/shard_map/all_to_all | solution.py:49
  136.7 7.4 %shard_map.28 = f32[960,2048]{1,0:T(8,128)} custom-call(f32[8,960,256]{2,1,0:T(8,128)} %all_to_all.22.x_ref), custom_call_target="tpu_custom_call" | custom-call | bytes 15728640 | tf_op jit(solution)/shard_map/pallas_call | solution.py:50
  144.2 0.0 all-gather.2.cloned.1.call-done
  144.2 31.0 %multiply_bitcast_fusion = f32[1800,960]{0,1:T(8,128)} fusion(f32[960,2048]{1,0:T(8,128)} %shard_map.28, f32[1800,2048]{0,1:T(8,128)} %all-gather.2.cloned.1.call-done), kind=kOutput, calls=%fused_computation | convolution fusion | flops 21235392512 | bytes 29521920 | tf_op jit(solution)/shard_map/dot_general | solution.py:58
  175.2 8.7 %copy.9 = f32[1800,960]{1,0:T(8,128)} copy(f32[1800,960]{0,1:T(8,128)} %multiply_bitcast_fusion) | data formatting | bytes 13824000 | tf_op jit(solution)/shard_map/transpose | solution.py:66
Async XLA Ops:
  6.5 38.0 %copy-start = (f32[256,960]{0,1:T(8,128)S(1)}, f32[256,960]{0,1:T(8,128)}, u32[]{:S(2)}) copy-start(f32[256,960]{0,1:T(8,128)} %param.3) | copy-start | bytes 2949124
  6.5 137.6 %all-gather.2.cloned.1.call-start = ((), (), s32[]{:S(2)}) async-start(), calls=%async_computation.2 | async-start | bytes 17694720 | tf_op jit(solution)/shard_map/all_gather | solution.py:36
Sparse Core Ops, SparseCore 0:
  44.6 79.8 all-gather.1

commit v17 on v13

--- a/solution.py
+++ b/solution.py
@@ -1,6 +1,10 @@
+import functools
+
 import jax
 import jax.numpy as jnp
 from jax import lax
+from jax.experimental import pallas as pl
+from jax.experimental.pallas import tpu as pltpu
 from jax.experimental.layout import Layout, with_layout_constraint
 from jax.sharding import Mesh
 from jax.sharding import PartitionSpec as P
@@ -10,6 +14,12 @@
     nz = ng // 2
     offsets = [(1, dz) for dz in range(nz)] + [(0, dz) for dz in range(nz // 2, 0, -1)]
     return nz, offsets + [(0, dz) for dz in range(nz // 2 + 1, nz)]
+
+
+def _order_kernel(nxc, per, kw, x_ref, o_ref):
+    for kb in range(x_ref.shape[0] * per):
+        p = (kb % nxc) * 2 + kb // nxc
+        o_ref[:, p * kw:(p + 1) * kw] = x_ref[kb // per, :, (kb % per) * kw:(kb % per + 1) * kw]
 
 
 def per_device(ng, nxc, amplitudes, integrals):
@@ -23,7 +33,8 @@
     both = lax.all_to_all(twice, ("ga", "ylo"), split_axis=0, concat_axis=1, tiled=True)
     rows = both.shape[0]
     pair = both.reshape(rows, ng, 2, cw).transpose(0, 2, 1, 3).reshape(rows, 2 * kw)
-    full_rows = lax.all_gather(pair, "xc", axis=1, tiled=True)
+    full_rows = lax.all_gather(pair.reshape(rows, 2, kw), "xc", axis=2, tiled=True)
+    full_rows = full_rows.reshape(rows, -1)
 
     bt = integrals.T
     full_bt = jnp.zeros((nb, bk * ng), jnp.float32)
@@ -37,11 +48,9 @@
         return full_bt
 
     got = lax.all_to_all(jnp.broadcast_to(bt, (ng,) + bt.shape), "ga", 0, 0, tiled=True)
-    rows = full_rows.shape[0]
-    a_k = full_rows.reshape(rows, nxc, 2, kw).transpose(0, 2, 1, 3).reshape(rows, ng, bk)
     ladder_t = lax.dot_general(
         got,
-        a_k,
+        full_rows.reshape(rows, ng, bk),
         (((0, 2), (1, 2)), ((), ())),
         precision=lax.Precision.HIGH,
         preferred_element_type=jnp.float32,

time: 207 us -> 190 us (0.918); the launches traced: 206 us -> 187 us
  blocking collectives: 34.3 us -> 126 us
  waiting for transfers between devices: 71.4 us -> 0.02 us
  local copies, waits for them, and re-layouts: 48.8 us -> 13 us
  starting transfers between devices: 4.91 us -> 0.01 us
    all_to_all x0 -> x1, blocking collectives: none -> 91.5 us  [per_device(): lax.all_to_all(jnp.broadcast_to(bt, (ng,) + bt.shape), 'ga', 0, 0, tiled=...]
    all_gather x1, waiting for transfers between devices: 71.4 us -> 0.01 us  [per_device(): lax.all_gather(pair.reshape(rows, 2, kw), 'xc', axis=2, tiled=True)]
    reshape x2 -> x0, local copies, waits for them, and re-layouts: 32.8 us -> none  [per_device(): full_rows.reshape(rows, nxc, 2, kw).transpose(0, 2, 1, 3)]
    all_to_all x1 -> x0, starting transfers between devices: 4.9 us -> none  [per_device(): lax.all_to_all(jnp.broadcast_to(bt, (ng,) + bt.shape), 'ga', 0, 0, tiled=...]
    broadcast_in_dim x1, local copies, waits for them, and re-layouts: 3.71 us -> 0.67 us  [per_device(): jnp.broadcast_to(bt, (ng,) + bt.shape)]
  transfers between devices with their start and end apart: 2 -> 1, of which waited for: 1 -> 0; matrix products, arithmetic and copies ran while one was open for 18% -> 0% of each run, Pallas kernels for 0% -> 0%
where the time goes in v17:
time: 190 us; the launch traced here: 187 us
  blocking collectives  126 us (66%)
  matrix products  35 us (18%)
  between operations  13.4 us (7%)
  local copies, waits for them, and re-layouts  13 us (7%)
    all_to_all x1, blocking collectives, per_device(): lax.all_to_all(jnp.broadcast_to(bt, (ng,) + bt.shape), 'ga', 0, 0, tiled=...  91.5 us
    dot_general x1, matrix products, per_device(): lax.dot_general(got, full_rows.reshape(rows, ng, bk), (((0, 2), (1, 2)),...  35 us
    all_to_all x1, blocking collectives, per_device(): lax.all_to_all(twice, ('ga', 'ylo'), split_axis=0, concat_axis=1, tiled=T...  34.3 us
    transpose x1, local copies, waits for them, and re-layouts, per_device(): return (0.5 * ladder_t).T  8.71 us
  transfers between devices with their start and end apart: 1, of which 0 were waited for; matrix products, arithmetic and copies ran while one was open for 0% of the time, Pallas kernels for 0%

profile of v17, /device:TPU:1, one launch (start us, length us, event | category | flops | bytes accessed | tf_op | source)
XLA Modules:
  0.0 187.3 jit_solution(7797893212612513046)
XLA Ops:
  6.5 0.0 copy-start
  6.5 0.0 all-gather.2.cloned.1.call-start
  6.5 1.9 reshape.11
  8.4 0.2 copy.9
  8.6 0.1 broadcast_in_dim.7
  8.8 34.3 %all_to_all.21 = f32[16,1800,16]{1,2,0:T(8,128)S(1)} all-to-all(f32[16,1800,16]{1,2,0:T(8,128)S(1)} %bitcast.20), channel_id=1, replica_groups=mesh['ga'=8,'ylo'=2,'xc'=8] {'ga','ylo'}, dimensions={0} | all-to-all | bytes 3686400 | tf_op jit(solution)/shard_map/all_to_all | solution.py:33
  43.1 1.4 copy.10
  44.5 0.0 all-gather.2.cloned.1.call-update
  44.5 0.0 copy-done
  44.5 0.7 broadcast_in_dim.6
  45.2 91.5 %all_to_all.22 = f32[8,960,256]{2,1,0:T(8,128)} all-to-all(f32[8,960,256]{2,1,0:T(8,128)S(1)} %broadcast_in_dim.6), channel_id=1, replica_groups=mesh['ga'=8,'ylo'=2,'xc'=8] {'ga'}, dimensions={0} | all-to-all | bytes 15728640 | tf_op jit(solution)/shard_map/all_to_all | solution.py:50
  136.7 0.0 all-gather.2.cloned.1.call-done
  136.7 35.0 %fusion = f32[1800,960]{0,1:T(8,128)} fusion(f32[8,960,256]{2,1,0:T(8,128)} %all_to_all.22, f32[1800,8,256]{0,2,1:T(8,128)} %bitcast.23), kind=kOutput, calls=%fused_computation.1 | convolution fusion | flops 21235392512 | bytes 29521920 | tf_op jit(solution)/shard_map/dot_general | solution.py:51
  171.7 8.7 %copy.13 = f32[1800,960]{1,0:T(8,128)} copy(f32[1800,960]{0,1:T(8,128)} %fusion) | data formatting | bytes 13824000 | tf_op jit(solution)/shard_map/transpose | solution.py:59
Async XLA Ops:
  6.5 38.0 %copy-start = (f32[256,960]{0,1:T(8,128)S(1)}, f32[256,960]{0,1:T(8,128)}, u32[]{:S(2)}) copy-start(f32[256,960]{0,1:T(8,128)} %param.3) | copy-start | bytes 2949124
  6.5 130.2 %all-gather.2.cloned.1.call-start = ((), (), s32[]{:S(2)}) async-start(), calls=%async_computation.2 | async-start | bytes 17694720 | tf_op jit(solution)/shard_map/all_gather | solution.py:36
Sparse Core Ops, SparseCore 0:
  44.6 79.8 all-gather.1

commit v18 on v17

--- a/solution.py
+++ b/solution.py
@@ -48,15 +48,14 @@
         return full_bt
 
     got = lax.all_to_all(jnp.broadcast_to(bt, (ng,) + bt.shape), "ga", 0, 0, tiled=True)
-    ladder_t = lax.dot_general(
+    ladder = lax.dot_general(
+        full_rows.reshape(rows, ng, bk),
         got,
-        full_rows.reshape(rows, ng, bk),
-        (((0, 2), (1, 2)), ((), ())),
+        (((1, 2), (0, 2)), ((), ())),
         precision=lax.Precision.HIGH,
         preferred_element_type=jnp.float32,
     )
-    ladder_t = with_layout_constraint(ladder_t, Layout(major_to_minor=(0, 1)))
-    return (0.5 * ladder_t).T
+    return 0.5 * ladder
 
 
 def solution(mesh):

time: 190 us -> 202 us (1.063)
  matrix products: 35 us -> 56.3 us
  local copies, waits for them, and re-layouts: 13 us -> 4.28 us
    dot_general x1, matrix products: 35 us -> 56.3 us  [per_device(): lax.dot_general(full_rows.reshape(rows, ng, bk), got, (((1, 2), (0, 2)),...]
    transpose x1 -> x0, local copies, waits for them, and re-layouts: 8.71 us -> none  [per_device(): return (0.5 * ladder_t).T]
where the time goes in v18:
time: 202 us; the launch traced here: 200 us
  blocking collectives  126 us (62%)
  matrix products  56.3 us (28%)
  between operations  13.4 us (7%)
  local copies, waits for them, and re-layouts  4.28 us (2%)
    all_to_all x1, blocking collectives, per_device(): lax.all_to_all(jnp.broadcast_to(bt, (ng,) + bt.shape), 'ga', 0, 0, tiled=...  91.5 us
    dot_general x1, matrix products, per_device(): lax.dot_general(full_rows.reshape(rows, ng, bk), got, (((1, 2), (0, 2)),...  56.3 us
    all_to_all x1, blocking collectives, per_device(): lax.all_to_all(twice, ('ga', 'ylo'), split_axis=0, concat_axis=1, tiled=T...  34.3 us
  transfers between devices with their start and end apart: 1, of which 0 were waited for; matrix products, arithmetic and copies ran while one was open for 0% of the time, Pallas kernels for 0%

profile of v18, /device:TPU:1, one launch (start us, length us, event | category | flops | bytes accessed | tf_op | source)
XLA Modules:
  0.0 199.9 jit_solution(4633473263861239777)
XLA Ops:
  6.5 0.0 copy-start
  6.5 0.0 all-gather.2.cloned.1.call-start
  6.5 1.9 reshape.11
  8.4 0.2 copy.7
  8.6 0.1 broadcast_in_dim.6
  8.8 34.3 %all_to_all.21 = f32[16,1800,16]{1,2,0:T(8,128)S(1)} all-to-all(f32[16,1800,16]{1,2,0:T(8,128)S(1)} %bitcast.16), channel_id=1, replica_groups=mesh['ga'=8,'ylo'=2,'xc'=8] {'ga','ylo'}, dimensions={0} | all-to-all | bytes 3686400 | tf_op jit(solution)/shard_map/all_to_all | solution.py:33
  43.1 1.4 copy.8
  44.5 0.0 all-gather.2.cloned.1.call-update
  44.5 0.0 copy-done
  44.5 0.7 broadcast_in_dim.7
  45.2 91.5 %all_to_all.22 = f32[8,960,256]{2,1,0:T(8,128)} all-to-all(f32[8,960,256]{2,1,0:T(8,128)S(1)} %broadcast_in_dim.7), channel_id=1, replica_groups=mesh['ga'=8,'ylo'=2,'xc'=8] {'ga'}, dimensions={0} | all-to-all | bytes 15728640 | tf_op jit(solution)/shard_map/all_to_all | solution.py:50
  136.7 0.0 all-gather.2.cloned.1.call-done
  136.7 56.3 %bitcast_multiply_fusion = f32[1800,960]{1,0:T(8,128)} fusion(f32[1800,8,256]{0,2,1:T(8,128)} %bitcast.19, f32[8,960,256]{2,1,0:T(8,128)} %all_to_all.22), kind=kOutput, calls=%fused_computation | convolution fusion | flops 21235392512 | bytes 29521920 | tf_op jit(solution)/shard_map/dot_general | solution.py:51
Async XLA Ops:
  6.5 38.0 %copy-start = (f32[256,960]{0,1:T(8,128)S(1)}, f32[256,960]{0,1:T(8,128)}, u32[]{:S(2)}) copy-start(f32[256,960]{0,1:T(8,128)} %param.3) | copy-start | bytes 2949124
  6.5 130.2 %all-gather.2.cloned.1.call-start = ((), (), s32[]{:S(2)}) async-start(), calls=%async_computation.2 | async-start | bytes 17694720 | tf_op jit(solution)/shard_map/all_gather | solution.py:36
Sparse Core Ops, SparseCore 0:
  44.6 79.8 all-gather.1

commit v19 on v17

--- a/solution.py
+++ b/solution.py
@@ -47,11 +47,11 @@
             full_bt = lax.dynamic_update_slice(full_bt, blk[:, h * kw:(h + 1) * kw], (0, pos * kw))
         return full_bt
 
-    got = lax.all_to_all(jnp.broadcast_to(bt, (ng,) + bt.shape), "ga", 0, 0, tiled=True)
+    got = lax.all_to_all(jnp.broadcast_to(integrals, (ng,) + integrals.shape), "ga", 0, 0, tiled=True)
     ladder_t = lax.dot_general(
         got,
         full_rows.reshape(rows, ng, bk),
-        (((0, 2), (1, 2)), ((), ())),
+        (((0, 1), (1, 2)), ((), ())),
         precision=lax.Precision.HIGH,
         preferred_element_type=jnp.float32,
     )

time: 190 us -> 190 us (level)
  no operation moved by 1% of the time
where the time goes in v19:
time: 190 us; the launch traced here: 187 us
  blocking collectives  126 us (66%)
  matrix products  35 us (18%)
  between operations  13.4 us (7%)
  local copies, waits for them, and re-layouts  13 us (7%)
    all_to_all x1, blocking collectives, per_device(): lax.all_to_all(jnp.broadcast_to(integrals, (ng,) + integrals.shape), 'ga'...  91.5 us
    dot_general x1, matrix products, per_device(): lax.dot_general(got, full_rows.reshape(rows, ng, bk), (((0, 1), (1, 2)),...  35 us
    all_to_all x1, blocking collectives, per_device(): lax.all_to_all(twice, ('ga', 'ylo'), split_axis=0, concat_axis=1, tiled=T...  34.3 us
    transpose x1, local copies, waits for them, and re-layouts, per_device(): return (0.5 * ladder_t).T  8.71 us
  transfers between devices with their start and end apart: 1, of which 0 were waited for; matrix products, arithmetic and copies ran while one was open for 0% of the time, Pallas kernels for 0%

profile of v19, /device:TPU:1, one launch (start us, length us, event | category | flops | bytes accessed | tf_op | source)
XLA Modules:
  0.0 187.3 jit_solution(7797893212612513046)
XLA Ops:
  6.5 0.0 copy-start
  6.5 0.0 all-gather.2.cloned.1.call-start
  6.5 1.9 reshape.11
  8.4 0.2 copy.9
  8.6 0.1 broadcast_in_dim.7
  8.8 34.3 %all_to_all.21 = f32[16,1800,16]{1,2,0:T(8,128)S(1)} all-to-all(f32[16,1800,16]{1,2,0:T(8,128)S(1)} %bitcast.19), channel_id=1, replica_groups=mesh['ga'=8,'ylo'=2,'xc'=8] {'ga','ylo'}, dimensions={0} | all-to-all | bytes 3686400 | tf_op jit(solution)/shard_map/all_to_all | solution.py:33
  43.1 1.4 copy.10
  44.5 0.0 all-gather.2.cloned.1.call-update
  44.5 0.0 copy-done
  44.5 0.7 broadcast_in_dim.6
  45.2 91.5 %all_to_all.22 = f32[8,256,960]{1,2,0:T(8,128)} all-to-all(f32[8,256,960]{1,2,0:T(8,128)S(1)} %broadcast_in_dim.6), channel_id=1, replica_groups=mesh['ga'=8,'ylo'=2,'xc'=8] {'ga'}, dimensions={0} | all-to-all | bytes 15728640 | tf_op jit(solution)/shard_map/all_to_all | solution.py:50
  136.7 0.0 all-gather.2.cloned.1.call-done
  136.7 35.0 %fusion = f32[1800,960]{0,1:T(8,128)} fusion(f32[8,256,960]{1,2,0:T(8,128)} %all_to_all.22, f32[1800,8,256]{0,2,1:T(8,128)} %bitcast.21), kind=kOutput, calls=%fused_computation.1 | convolution fusion | flops 21235392512 | bytes 29521920 | tf_op jit(solution)/shard_map/dot_general | solution.py:51
  171.7 8.7 %copy.13 = f32[1800,960]{1,0:T(8,128)} copy(f32[1800,960]{0,1:T(8,128)} %fusion) | data formatting | bytes 13824000 | tf_op jit(solution)/shard_map/transpose | solution.py:59
Async XLA Ops:
  6.5 38.0 %copy-start = (f32[256,960]{0,1:T(8,128)S(1)}, f32[256,960]{0,1:T(8,128)}, u32[]{:S(2)}) copy-start(f32[256,960]{0,1:T(8,128)} %param.3) | copy-start | bytes 2949124
  6.5 130.2 %all-gather.2.cloned.1.call-start = ((), (), s32[]{:S(2)}) async-start(), calls=%async_computation.2 | async-start | bytes 17694720 | tf_op jit(solution)/shard_map/all_gather | solution.py:36
Sparse Core Ops, SparseCore 0:
  44.6 79.8 all-gather.1
